TPU v7x, 32 devices: a whole 2x2x4 slice. The times are simulated.
32 devices in a mesh: comp: 2 (over y), gx: 4 (over x, core), gy: 4 (over z).
Axes of the slice: x: 2, y: 2, z: 4, core: 2. Of those that a mesh axis runs over, the one named last changes fastest.
Arguments:
- state: float32 [2, 30, 128, 1024], P('comp', None, 'gx', 'gy'), may hold values from -6 to 6
- conduct: float32 [2, 30, 128, 1024], P('comp', None, 'gx', 'gy'), may hold values from 0.3 to 3
- storage: float32 [2], P('comp'), may hold values from 0.05 to 0.5
- surface_source: float32 [2, 128, 1024], P('comp', 'gx', 'gy'), may hold values from -6 to 6
- plant_type: int32 [2, 128, 1024], P('comp', 'gx', 'gy'), may hold values from 0 to 15
- plant_table: float32 [16, 2], replicated, may hold values from 0.3 to 3
- layer_weights: float32 [2, 16, 6], replicated, may hold values from 0.05 to 1
- remap_rows: int32 [2, 128], P('comp', 'gx'), may hold values from 0 to 31
- remap_weights: float32 [2, 1024, 128], P('comp', 'gy'), may hold values from 0 to 1
Outputs:
- new_state: float32 [2, 30, 128, 1024], P('comp', None, 'gx', 'gy')
- exchange_flux: float32 [2, 128, 1024], P('comp', 'gx', 'gy')
All inputs are finite; a program needn't handle non-finite values.
Results may differ from a plain program's by a relative error of at most 0.0003.
Values sent between devices are 32-bit elements; how exact they have to be, the bound alone decides.
No kernel may reach another device: no remote copies, remote signals or barrier semaphores. Data moves between devices by JAX's collectives and lax.ppermute only.
A program may use at most 64 MiB of HBM per device.

v0:
```python
import jax
import jax.numpy as jnp
from jax import lax
from jax.sharding import PartitionSpec as P

NS = 6
PATCH = 128
PLANTS = 16
ITERS = 3


def from_partner(value, axis, distance):
    mask = 2**distance
    pairs = [(source, source ^ mask) for source in range(lax.axis_size(axis))]
    return lax.ppermute(value, axis, pairs)


def extended(block, sides, width):
    for axis, dim in sides:
        count = lax.axis_size(axis)
        forward = [(i, i + 1) for i in range(count - 1)]
        backward = [(target, source) for source, target in forward]
        low = lax.ppermute(
            lax.slice_in_dim(block, block.shape[dim] - width, None, axis=dim), axis, forward
        )
        high = lax.ppermute(lax.slice_in_dim(block, 0, width, axis=dim), axis, backward)
        block = jnp.concatenate([low, block, high], axis=dim)
    return block


def apply_padded(vp, kp):
    v = vp[1:-1, 1:-1, 1:-1]
    kc = kp[1:-1, 1:-1, 1:-1]
    total = jnp.zeros_like(v)
    moves = [(2, 1, 1), (0, 1, 1), (1, 2, 1), (1, 0, 1), (1, 1, 2), (1, 1, 0)]
    for a, b, e in moves:
        vn = vp[a : a + v.shape[0], b : b + v.shape[1], e : e + v.shape[2]]
        kn = kp[a : a + v.shape[0], b : b + v.shape[1], e : e + v.shape[2]]
        total = total + 0.5 * (kc + kn) * (v - vn)
    return total


def pad_levels(field):
    return jnp.pad(field, ((1, 1), (0, 0), (0, 0)))


def least_squares(hmat, beta):
    gram = jnp.sum(hmat[:, :, None] * hmat[:, None, :], axis=0)
    target_vector = beta * hmat[0, :]
    factor = jnp.linalg.cholesky(gram)
    return jax.scipy.linalg.cho_solve((factor, True), target_vector)


def one_hot_types(kinds):
    return (kinds[None, :, :] == jnp.arange(PLANTS)[:, None, None]).astype(jnp.float32)


def forcing_for(layers, rows, weights, kinds, profile):
    hp = lax.Precision.HIGHEST
    picked = jnp.take(layers, rows, axis=1)
    width = layers.shape[2]
    blocks = picked.reshape(layers.shape[0], layers.shape[1], width // PATCH, PATCH)
    wblk = weights.reshape(width // PATCH, PATCH, PATCH)
    remapped = jnp.einsum("lxbk,bjk->lxbj", blocks, wblk, precision=hp).reshape(layers.shape)
    prof = jnp.einsum("pl,pxy->lxy", profile, one_hot_types(kinds), precision=hp)
    return jnp.sum(prof * remapped, axis=0)


def body(
    state,
    conduct,
    storage,
    surface_source,
    plant_type,
    plant_table,
    layer_weights,
    remap_rows,
    remap_weights,
):
    hp = lax.Precision.HIGHEST
    comp_index = lax.axis_index("comp")
    field = state[0]
    levels = field.shape[0]
    keff = conduct[0] * (1.0 + 0.5 * jnp.tanh(field))
    kinds = plant_type[0]
    own_table = jnp.where(comp_index == 0, layer_weights[0], layer_weights[1])
    other_table = jnp.where(comp_index == 0, layer_weights[1], layer_weights[0])
    layers = field[:NS]
    partner_layers = from_partner(layers, "comp", 0)
    other_force = forcing_for(partner_layers, remap_rows[0], remap_weights[0], kinds, other_table)
    selector = one_hot_types(kinds)
    own_prof = jnp.einsum("pl,pxy->lxy", own_table, selector, precision=hp)
    own_force = jnp.sum(own_prof * layers, axis=0)
    atmospheric_forcing = jnp.where(comp_index == 0, own_force, other_force)
    soil_force = jnp.where(comp_index == 0, other_force, own_force)
    params = jnp.einsum("pq,pxy->qxy", plant_table, selector, precision=hp)
    flux = params[0] * (params[1] * soil_force - atmospheric_forcing)
    sign = 1.0 - 2.0 * comp_index.astype(jnp.float32)
    top = sign * flux[None] * own_prof
    source = jnp.concatenate([top, jnp.zeros((levels - NS,) + flux.shape, jnp.float32)], axis=0)
    source = source.at[0].add(surface_source[0])
    diagonal_shift = storage[0]
    depth = 1
    stacked = jnp.stack([field, keff])
    padded = extended(stacked, (("gx", 2), ("gy", 3)), depth)
    kext = padded[1]

    def apply_extended_operator(vector):
        return apply_padded(pad_levels(vector), pad_levels(kext))

    rhs_rim = 0
    rhs = source - apply_extended_operator(padded[0])
    beta = jnp.sqrt(lax.psum(jnp.sum(rhs * rhs), ("gx", "gy")))
    basis = [rhs / beta]
    rims = [rhs_rim]
    hmat = jnp.zeros((ITERS + 1, ITERS), jnp.float32)
    for j in range(ITERS):
        operate_vector = basis[j]
        padded_vector = extended(operate_vector, (("gx", 1), ("gy", 2)), 1)
        krylov_vector = diagonal_shift * operate_vector + apply_extended_operator(padded_vector)
        near = [basis[i] for i in range(j + 1)]
        interior_vector = krylov_vector
        partials = jnp.stack([jnp.sum(interior_vector * near[i]) for i in range(j + 1)])
        heights, squared = lax.psum(
            (partials, jnp.sum(interior_vector * interior_vector)), ("gx", "gy")
        )
        for i in range(j + 1):
            krylov_vector = krylov_vector - heights[i] * near[i]
            hmat = hmat.at[i, j].set(heights[i])
        nrm = jnp.sqrt(squared - jnp.sum(heights * heights))
        hmat = hmat.at[j + 1, j].set(nrm)
        if j + 1 < ITERS:
            basis.append(krylov_vector / nrm)
            rims.append(0)
    coef = least_squares(hmat, beta)
    update = field
    for j in range(ITERS):
        update = update + coef[j] * basis[j]
    return (update[None], flux[None])


def solution(mesh):
    in_specs = (
        P("comp", None, "gx", "gy"),
        P("comp", None, "gx", "gy"),
        P("comp"),
        P("comp", "gx", "gy"),
        P("comp", "gx", "gy"),
        P(),
        P(),
        P("comp", "gx"),
        P("comp", "gy", None),
    )
    out_specs = (P("comp", None, "gx", "gy"), P("comp", "gx", "gy"))
    return jax.shard_map(body, mesh=mesh, in_specs=in_specs, out_specs=out_specs, check_vma=False)
```

profile of v0, /device:TPU:0, one launch (start us, length us, event | category | flops | bytes accessed | tf_op | source)
XLA Modules:
  0.0 289.8 jit_solution(18306534450903827338)
XLA Ops:
  2.5 3.1 %collective-permute-start = (f32[6,32,256]{2,0,1:T(8,128)}, f32[6,32,256]{2,0,1:T(8,128)}, u32[]{:S(2)}, u32[]{:S(2)}) collective-permute-start(f32[6,32,256]{2,0,1:T(8,128)} %bitcast.108), channel_id=1, source_target_pairs={{0,16},{16,0},{1,17},{17,1},{2,18},{18,2},{3,19},{19,3},{4,20},{20... | collective-permute-start | bytes 589832 | tf_op jit(solution)/shard_map/ppermute | solution.py:15
  15.3 1.8 copy.131
  17.1 4.1 %collective-permute-start.3 = (f32[2,30,34,1]{2,0,3,1:T(2,128)S(1)}, f32[2,30,34,1]{2,0,3,1:T(2,128)}, u32[]{:S(2)}, u32[]{:S(2)}) collective-permute-start(f32[2,30,34,1]{2,0,3,1:T(2,128)S(1)} %copy.131), channel_id=1, source_target_pairs={{0,1},{1,2},{2,3},{4,5},{5,6},{6,7},{8,9},{9,10},{10,11},{12,13},{... | collective-permute-start | bytes 24488 | tf_op jit(solution)/shard_map/ppermute | solution.py:23
  26.2 2.2 collective-permute-done.4
  28.4 2.3 copy.134
  30.7 3.2 %pad_maximum_fusion = f32[2,30,34,258]{3,2,1,0:T(8,128)S(1)} fusion(f32[2,30,34,1]{3,2,1,0:T(8,128)} %copy.134, f32[2,30,1,256]{3,2,1,0:T(1,128)S(1)} %collective-permute-done.2, f32[1,30,32,256]{3,2,1,0:T(8,128)S(1)} %add_multiply_fusion, f32[1,30,32,256]{3,2,1,0:T(8,128)S(1)} %copy-done.2, f32[2,30,1,256]{3,2,1,0:T(1,128)S(1)} %collective-permute-done.1, ...), kind=kLoop, calls=%fused_computation.1 | loop fusion | flops 2631600 | bytes 4210560 | tf_op jit(solution)/shard_map/concatenate | solution.py:27
  35.4 1.7 gather_fusion
  39.7 5.6 %multiply_reduce_fusion.9 = (f32[]{:T(128)}, f32[30,32,256]{2,1,0:T(8,128)S(1)}, f32[30,32,256]{2,1,0:T(8,128)}, f32[30,32,256]{2,1,0:T(8,128)}, f32[30,32,256]{...) fusion(f32[30,32,256]{2,1,0:T(8,128)S(1)} %fusion.80, ...), kind=kLoop, calls=%fused_computation.156 | loop fusion | flops 7864319 | bytes 21381124 | tf_op jit(solution)/shard_map/reduce_sum | solution.py:113
  45.2 34.1 %psum.49 = f32[]{:T(128)} all-reduce(f32[]{:T(128)} %get-tuple-element.149), channel_id=1, replica_groups=mesh['comp'=2,'gx'=4,'gy'=4] {'gx','gy'}, use_global_device_ids=true, to_apply=%region_3.4 | all-reduce | flops 1 | bytes 8 | tf_op jit(solution)/shard_map/psum | solution.py:113
  82.9 4.0 %collective-permute-done.6 = f32[30,1,256]{2,1,0:T(1,128)S(1)} collective-permute-done((f32[30,1,256]{2,1,0:T(1,128)S(1)}, f32[30,1,256]{2,1,0:T(1,128)S(1)}, u32[]{:S(2)}, u32[]{:S(2)}) %collective-permute-start.6) | collective-permute-done | bytes 30752 | tf_op jit(solution)/shard_map/ppermute | solution.py:26
  87.6 2.4 collective-permute-start.7
  93.6 2.3 collective-permute-done.8
  97.1 2.4 select_maximum_fusion.8
  99.6 5.0 %multiply_reduce_fusion.8 = (f32[]{:T(128)}, f32[]{:T(128)}, f32[30,32,256]{2,1,0:T(8,128)}) fusion(f32[30,32,256]{2,1,0:T(8,128)S(1)} %broadcast_divide_fusion, f32[30,32,256]{2,1,0:T(8,128)} %get-tuple-element.156, f32[30,1,256]{2,1,0:T(1,128)S(1)} %collective-permute-done.6, f32[30,1,256]{2,1,0:T(1,128)S(1)} %collective-permute-done.5, ...), kind=kLoop, calls=%fused_computation.155 | loop fusion | flops 7618558 | bytes 9900012 | tf_op jit(solution)/shard_map/reduce_sum | solution.py:123
  104.6 30.7 %all-reduce.9 = (f32[]{:T(128)}, f32[1]{0:T(128)}) all-reduce(f32[]{:T(128)} %get-tuple-element.140, f32[1]{0:T(128)} %bitcast.21), channel_id=1, replica_groups=mesh['comp'=2,'gx'=4,'gy'=4] {'gx','gy'}, use_global_device_ids=true, to_apply=%region_7.8 | all-reduce | flops 2 | bytes 16 | tf_op jit(solution)/shard_map/psum | solution.py:124
  137.3 2.1 subtract_divide_fusion.1
  140.7 3.0 %collective-permute-start.9 = (f32[30,1,256]{2,1,0:T(1,128)S(1)}, f32[30,1,256]{2,1,0:T(1,128)S(1)}, u32[]{:S(2)}, u32[]{:S(2)}) collective-permute-start(f32[30,1,256]{2,1,0:T(1,128)S(1)} %get-tuple-element.173), channel_id=1, source_target_pairs={{0,4},{4,8},{8,12},{1,5},{5,9},{9,13},{2,6},{6,10},{10,14},{3,7},{... | collective-permute-start | bytes 92168 | tf_op jit(solution)/shard_map/ppermute | solution.py:23
  147.4 3.8 %collective-permute-start.11 = (f32[30,34,1]{1,2,0:T(1,128)S(1)}, f32[30,34,1]{1,2,0:T(1,128)S(1)}, u32[]{:S(2)}, u32[]{:S(2)}) collective-permute-start(f32[30,34,1]{1,2,0:T(1,128)S(1)} %copy.141), channel_id=1, source_target_pairs={{0,1},{1,2},{2,3},{4,5},{5,6},{6,7},{8,9},{9,10},{10,11},{12,13},{... | collective-permute-start | bytes 12248 | tf_op jit(solution)/shard_map/ppermute | solution.py:23
  155.7 2.5 collective-permute-done.12
  159.3 2.4 select_maximum_fusion.4
  161.8 4.9 %multiply_reduce_fusion.6 = (f32[]{:T(128)}, f32[]{:T(128)}, f32[]{:T(128)}, f32[30,32,256]{2,1,0:T(8,128)}) fusion(f32[30,32,256]{2,1,0:T(8,128)S(1)} %subtract_divide_fusion.1, f32[30,32,256]{2,1,0:T(8,128)} %get-tuple-element.156, f32[30,1,256]{2,1,0:T(1,128)S(1)} %collective-permute-done.10, f32[30,1,256]{2,1,0:T(1,128)S(1)} %collective-permute-done.9, ...), kind=kLoop, calls=%fused_computation.152 | loop fusion | flops 8355837 | bytes 10883060 | tf_op jit(solution)/shard_map/reduce_sum | solution.py:123
  168.1 30.8 %all-reduce.8 = (f32[]{:T(128)}, f32[2]{0:T(128)S(1)}) all-reduce(f32[]{:T(128)} %get-tuple-element.137, f32[2]{0:T(128)S(1)} %pad_maximum_fusion.31), channel_id=1, replica_groups=mesh['comp'=2,'gx'=4,'gy'=4] {'gx','gy'}, use_global_device_ids=true, to_apply=%region_12.13 | all-reduce | flops 3 | bytes 24 | tf_op jit(solution)/shard_map/psum | solution.py:124
  201.5 2.7 subtract_divide_fusion
  206.9 6.1 %collective-permute-done.14 = f32[30,1,256]{2,1,0:T(1,128)S(1)} collective-permute-done((f32[30,1,256]{2,1,0:T(1,128)S(1)}, f32[30,1,256]{2,1,0:T(1,128)S(1)}, u32[]{:S(2)}, u32[]{:S(2)}) %collective-permute-start.14) | collective-permute-done | bytes 30752 | tf_op jit(solution)/shard_map/ppermute | solution.py:26
  215.8 4.0 %collective-permute-start.15 = (f32[30,34,1]{1,2,0:T(1,128)S(1)}, f32[30,34,1]{1,2,0:T(1,128)S(1)}, u32[]{:S(2)}, u32[]{:S(2)}) collective-permute-start(f32[30,34,1]{1,2,0:T(1,128)S(1)} %copy.147), channel_id=1, source_target_pairs={{0,1},{1,2},{2,3},{4,5},{5,6},{6,7},{8,9},{9,10},{10,11},{12,13},{... | collective-permute-start | bytes 12248 | tf_op jit(solution)/shard_map/ppermute | solution.py:23
  224.5 1.9 scatter.34
  227.3 1.9 dynamic-slice.68
  231.6 2.4 select_maximum_fusion
  234.0 6.0 %multiply_reduce_fusion = (f32[]{:T(128)}, f32[]{:T(128)}, f32[]{:T(128)}, f32[]{:T(128)}) fusion(f32[30,32,256]{2,1,0:T(8,128)} %copy-done.4, f32[30,32,256]{2,1,0:T(8,128)S(1)} %subtract_divide_fusion.1, f32[30,32,256]{2,1,0:T(8,128)} %get-tuple-element.156, f32[30,1,256]{2,1,0:T(1,128)S(1)} %collective-permute-done.14, ...), kind=kLoop, calls=%fused_computation.145 | loop fusion | flops 8847356 | bytes 10883064 | tf_op jit(solution)/shard_map/reduce_sum | solution.py:125
  240.0 1.9 pad_maximum_fusion.32
  242.0 32.9 %all-reduce.7 = (f32[3]{0:T(128)S(1)}, f32[]{:T(128)}) all-reduce(f32[3]{0:T(128)S(1)} %pad_maximum_fusion.32, f32[]{:T(128)} %get-tuple-element.132), channel_id=1, replica_groups=mesh['comp'=2,'gx'=4,'gy'=4] {'gx','gy'}, use_global_device_ids=true, to_apply=%region_18.19 | all-reduce | flops 4 | bytes 32 | tf_op jit(solution)/shard_map/psum | solution.py:124
  285.4 4.4 %fusion.74 = f32[1,30,32,256]{3,2,1,0:T(8,128)} fusion(f32[1,30,32,256]{3,2,1,0:T(8,128)S(1)} %copy-done.3, f32[30,32,256]{2,1,0:T(8,128)} %copy-done.4, f32[30,32,256]{2,1,0:T(8,128)S(1)} %subtract_divide_fusion.1, f32[]{:T(128)} %bitcast.55, f32[]{:T(128)} %bitcast.54, f32[]{:T(128)} %bitcast.53, f32[30,32,256]{2,1,0:T(8,128)S(1)} %get-tuple-element.150, ...), kind=kLoop, calls=%fused_computation.144 | loop fusion | flops 1720320 | bytes 4915216 | tf_op jit(solution)/shard_map/broadcast_in_dim | solution.py:139
  (155 shorter events, 62.0 us)
Async XLA Ops:
  0.6 36.8 %copy-start = (f32[1,256,128]{2,1,0:T(8,128)S(1)}, f32[1,256,128]{2,1,0:T(8,128)}, u32[]{:S(2)}) copy-start(f32[1,256,128]{2,1,0:T(8,128)} %param.37) | copy-start | bytes 393220
  0.6 6.6 %copy-start.2 = (f32[1,30,32,256]{3,2,1,0:T(8,128)S(1)}, f32[1,30,32,256]{3,2,1,0:T(8,128)}, u32[]{:S(2)}) copy-start(f32[1,30,32,256]{3,2,1,0:T(8,128)} %param.29) | copy-start | bytes 2949124
  2.5 7.6 %copy-start.21 = (f32[2,16,6]{1,0,2:T(2,128)S(1)}, f32[2,16,6]{1,0,2:T(2,128)}, u32[]{:S(2)}) copy-start(f32[2,16,6]{1,0,2:T(2,128)} %param.35) | copy-start | bytes 2308
  2.5 7.6 %copy-start.24 = (s32[1,32]{1,0:T(1,128)S(1)}, s32[1,32]{1,0:T(1,128)}, u32[]{:S(2)}) copy-start(s32[1,32]{1,0:T(1,128)} %param.36) | copy-start | bytes 388
  2.5 8.2 %copy-start.18 = (s32[1,32,256]{2,1,0:T(8,128)S(1)}, s32[1,32,256]{2,1,0:T(8,128)}, u32[]{:S(2)}) copy-start(s32[1,32,256]{2,1,0:T(8,128)} %param.33) | copy-start | bytes 98308
  2.5 8.2 %copy-start.23 = (f32[16,2]{0,1:T(2,128)S(1)}, f32[16,2]{0,1:T(2,128)}, u32[]{:S(2)}) copy-start(f32[16,2]{0,1:T(2,128)} %param.34) | copy-start | bytes 388
  2.5 32.9 %collective-permute-start = (f32[6,32,256]{2,0,1:T(8,128)}, f32[6,32,256]{2,0,1:T(8,128)}, u32[]{:S(2)}, u32[]{:S(2)}) collective-permute-start(f32[6,32,256]{2,0,1:T(8,128)} %bitcast.108), channel_id=1, source_target_pairs={{0,16},{16,0},{1,17},{17,1},{2,18},{18,2},{3,19},{19,3},{4,20},{20... | collective-permute-start | bytes 589832 | tf_op jit(solution)/shard_map/ppermute | solution.py:15
  7.4 6.0 %collective-permute-start.1 = (f32[2,30,1,256]{3,2,1,0:T(1,128)S(1)}, f32[2,30,1,256]{3,2,1,0:T(1,128)S(1)}, u32[]{:S(2)}, u32[]{:S(2)}) collective-permute-start(f32[2,30,1,256]{3,2,1,0:T(1,128)S(1)} %get-tuple-element.163), channel_id=1, source_target_pairs={{0,4},{4,8},{8,12},{1,5},{5,9},{9,13},{2,6},{6,10},{10,14},{3,7},{... | collective-permute-start | bytes 184328 | tf_op jit(solution)/shard_map/ppermute | solution.py:23
  8.8 4.7 %collective-permute-start.2 = (f32[2,30,1,256]{3,2,1,0:T(1,128)S(1)}, f32[2,30,1,256]{3,2,1,0:T(1,128)S(1)}, u32[]{:S(2)}, u32[]{:S(2)}) collective-permute-start(f32[2,30,1,256]{3,2,1,0:T(1,128)S(1)} %get-tuple-element.164), channel_id=1, source_target_pairs={{4,0},{8,4},{12,8},{5,1},{9,5},{13,9},{6,2},{10,6},{14,10},{7,3},{... | collective-permute-start | bytes 184328 | tf_op jit(solution)/shard_map/ppermute | solution.py:26
  17.1 7.8 %collective-permute-start.3 = (f32[2,30,34,1]{2,0,3,1:T(2,128)S(1)}, f32[2,30,34,1]{2,0,3,1:T(2,128)}, u32[]{:S(2)}, u32[]{:S(2)}) collective-permute-start(f32[2,30,34,1]{2,0,3,1:T(2,128)S(1)} %copy.131), channel_id=1, source_target_pairs={{0,1},{1,2},{2,3},{4,5},{5,6},{6,7},{8,9},{9,10},{10,11},{12,13},{... | collective-permute-start | bytes 24488 | tf_op jit(solution)/shard_map/ppermute | solution.py:23
  22.3 6.1 %collective-permute-start.4 = (f32[2,30,34,1]{2,0,3,1:T(2,128)}, f32[2,30,34,1]{2,0,3,1:T(2,128)}, u32[]{:S(2)}, u32[]{:S(2)}) collective-permute-start(f32[2,30,34,1]{2,0,3,1:T(2,128)} %copy.132), channel_id=1, source_target_pairs={{1,0},{2,1},{3,2},{5,4},{6,5},{7,6},{9,8},{10,9},{11,10},{13,12},{... | collective-permute-start | bytes 24488 | tf_op jit(solution)/shard_map/ppermute | solution.py:26
  33.9 3.3 %copy-start.22 = (pred[32]{0:T(512)(128)(4,1)S(1)}, pred[32]{0:T(512)(128)(4,1)}, u32[]{:S(2)}) copy-start(pred[32]{0:T(512)(128)(4,1)} %compare_and_fusion) | copy-start | bytes 100
  35.4 3.1 %copy-start.19 = (f32[2,32,256]{2,0,1:T(2,128)S(1)}, f32[2,32,256]{2,0,1:T(2,128)}, u32[]{:S(2)}) copy-start(f32[2,32,256]{2,0,1:T(2,128)} %convolution_bitcast_fusion.1) | copy-start | bytes 196612
  35.4 3.2 %copy-start.17 = (f32[6,32,256]{2,0,1:T(8,128)S(1)}, f32[6,32,256]{2,0,1:T(8,128)}, u32[]{:S(2)}) copy-start(f32[6,32,256]{2,0,1:T(8,128)} %get-tuple-element.194) | copy-start | bytes 589828
  80.3 2.6 collective-permute-start.5
  81.6 5.3 %collective-permute-start.6 = (f32[30,1,256]{2,1,0:T(1,128)S(1)}, f32[30,1,256]{2,1,0:T(1,128)S(1)}, u32[]{:S(2)}, u32[]{:S(2)}) collective-permute-start(f32[30,1,256]{2,1,0:T(1,128)S(1)} %get-tuple-element.176), channel_id=1, source_target_pairs={{4,0},{8,4},{12,8},{5,1},{9,5},{13,9},{6,2},{10,6},{14,10},{7,3},{... | collective-permute-start | bytes 92168 | tf_op jit(solution)/shard_map/ppermute | solution.py:26
  87.6 4.9 %collective-permute-start.7 = (f32[30,34,1]{1,2,0:T(1,128)S(1)}, f32[30,34,1]{1,2,0:T(1,128)S(1)}, u32[]{:S(2)}, u32[]{:S(2)}) collective-permute-start(f32[30,34,1]{1,2,0:T(1,128)S(1)} %copy.135), channel_id=1, source_target_pairs={{0,1},{1,2},{2,3},{4,5},{5,6},{6,7},{8,9},{9,10},{10,11},{12,13},{... | collective-permute-start | bytes 12248 | tf_op jit(solution)/shard_map/ppermute | solution.py:23
  90.3 5.6 %collective-permute-start.8 = (f32[30,34,1]{1,2,0:T(1,128)S(1)}, f32[30,34,1]{1,2,0:T(1,128)S(1)}, u32[]{:S(2)}, u32[]{:S(2)}) collective-permute-start(f32[30,34,1]{1,2,0:T(1,128)S(1)} %copy.136), channel_id=1, source_target_pairs={{1,0},{2,1},{3,2},{5,4},{6,5},{7,6},{9,8},{10,9},{11,10},{13,12},{... | collective-permute-start | bytes 12248 | tf_op jit(solution)/shard_map/ppermute | solution.py:26
  97.1 2.5 copy-start.13
  104.6 39.2 %copy-start.25 = (s32[2]{0:T(128)S(1)}, s32[2]{0:T(128)}, u32[]{:S(2)}) copy-start(s32[2]{0:T(128)} %constant.341.clone.1) | copy-start | bytes 28
  139.4 5.0 %collective-permute-start.10 = (f32[30,1,256]{2,1,0:T(1,128)S(1)}, f32[30,1,256]{2,1,0:T(1,128)S(1)}, u32[]{:S(2)}, u32[]{:S(2)}) collective-permute-start(f32[30,1,256]{2,1,0:T(1,128)S(1)} %get-tuple-element.174), channel_id=1, source_target_pairs={{4,0},{8,4},{12,8},{5,1},{9,5},{13,9},{6,2},{10,6},{14,10},{7,3},{... | collective-permute-start | bytes 92168 | tf_op jit(solution)/shard_map/ppermute | solution.py:26
  140.7 3.9 %collective-permute-start.9 = (f32[30,1,256]{2,1,0:T(1,128)S(1)}, f32[30,1,256]{2,1,0:T(1,128)S(1)}, u32[]{:S(2)}, u32[]{:S(2)}) collective-permute-start(f32[30,1,256]{2,1,0:T(1,128)S(1)} %get-tuple-element.173), channel_id=1, source_target_pairs={{0,4},{4,8},{8,12},{1,5},{5,9},{9,13},{2,6},{6,10},{10,14},{3,7},{... | collective-permute-start | bytes 92168 | tf_op jit(solution)/shard_map/ppermute | solution.py:23
  147.4 7.2 %collective-permute-start.11 = (f32[30,34,1]{1,2,0:T(1,128)S(1)}, f32[30,34,1]{1,2,0:T(1,128)S(1)}, u32[]{:S(2)}, u32[]{:S(2)}) collective-permute-start(f32[30,34,1]{1,2,0:T(1,128)S(1)} %copy.141), channel_id=1, source_target_pairs={{0,1},{1,2},{2,3},{4,5},{5,6},{6,7},{8,9},{9,10},{10,11},{12,13},{... | collective-permute-start | bytes 12248 | tf_op jit(solution)/shard_map/ppermute | solution.py:23
  152.6 5.6 %collective-permute-start.12 = (f32[30,34,1]{1,2,0:T(1,128)S(1)}, f32[30,34,1]{1,2,0:T(1,128)S(1)}, u32[]{:S(2)}, u32[]{:S(2)}) collective-permute-start(f32[30,34,1]{1,2,0:T(1,128)S(1)} %copy.142), channel_id=1, source_target_pairs={{1,0},{2,1},{3,2},{5,4},{6,5},{7,6},{9,8},{10,9},{11,10},{13,12},{... | collective-permute-start | bytes 12248 | tf_op jit(solution)/shard_map/ppermute | solution.py:26
  159.3 2.5 copy-start.16
  204.3 27.3 %copy-start.4 = (f32[30,32,256]{2,1,0:T(8,128)}, f32[30,32,256]{2,1,0:T(8,128)S(1)}, u32[]{:S(2)}) copy-start(f32[30,32,256]{2,1,0:T(8,128)S(1)} %subtract_divide_fusion) | copy-start | bytes 2949124
  204.3 2.6 collective-permute-start.13
  205.6 7.4 %collective-permute-start.14 = (f32[30,1,256]{2,1,0:T(1,128)S(1)}, f32[30,1,256]{2,1,0:T(1,128)S(1)}, u32[]{:S(2)}, u32[]{:S(2)}) collective-permute-start(f32[30,1,256]{2,1,0:T(1,128)S(1)} %get-tuple-element.172), channel_id=1, source_target_pairs={{4,0},{8,4},{12,8},{5,1},{9,5},{13,9},{6,2},{10,6},{14,10},{7,3},{... | collective-permute-start | bytes 92168 | tf_op jit(solution)/shard_map/ppermute | solution.py:26
  215.8 13.4 %collective-permute-start.15 = (f32[30,34,1]{1,2,0:T(1,128)S(1)}, f32[30,34,1]{1,2,0:T(1,128)S(1)}, u32[]{:S(2)}, u32[]{:S(2)}) collective-permute-start(f32[30,34,1]{1,2,0:T(1,128)S(1)} %copy.147), channel_id=1, source_target_pairs={{0,1},{1,2},{2,3},{4,5},{5,6},{6,7},{8,9},{9,10},{10,11},{12,13},{... | collective-permute-start | bytes 12248 | tf_op jit(solution)/shard_map/ppermute | solution.py:23
  221.2 9.2 %collective-permute-start.16 = (f32[30,34,1]{1,2,0:T(1,128)S(1)}, f32[30,34,1]{1,2,0:T(1,128)S(1)}, u32[]{:S(2)}, u32[]{:S(2)}) collective-permute-start(f32[30,34,1]{1,2,0:T(1,128)S(1)} %copy.148), channel_id=1, source_target_pairs={{1,0},{2,1},{3,2},{5,4},{6,5},{7,6},{9,8},{10,9},{11,10},{13,12},{... | collective-permute-start | bytes 12248 | tf_op jit(solution)/shard_map/ppermute | solution.py:26
  231.6 2.5 copy-start.15
  234.0 51.3 %copy-start.3 = (f32[1,30,32,256]{3,2,1,0:T(8,128)S(1)}, f32[1,30,32,256]{3,2,1,0:T(8,128)}, u32[]{:S(2)}) copy-start(f32[1,30,32,256]{3,2,1,0:T(8,128)} %param.29) | copy-start | bytes 2949124
  (11 other events, 24.4 us)
where the time goes:
time: 291 us; the launch traced here: 290 us
  blocking collectives  129 us (44%)
  other arithmetic  53.6 us (18%)
  local copies, waits for them, and re-layouts  43 us (15%)
  starting transfers between devices  35 us (12%)
  waiting for transfers between devices  17.6 us (6%)
  between operations  9.11 us (3%)
  matrix products  2.96 us (1%)
    psum x3, blocking collectives, body(): lax.psum((partials, jnp.sum(interior_vector * interior_vector)), ('gx', '...  94.4 us
    psum x1, blocking collectives, body(): beta = jnp.sqrt(lax.psum(jnp.sum(rhs * rhs), ('gx', 'gy')))  34.1 us
    ppermute x8, starting transfers between devices, extended(): lax.ppermute(lax.slice_in_dim(block, block.shape[dim] - width, None, axis...  21.4 us
    ppermute x8, waiting for transfers between devices, extended(): lax.ppermute(lax.slice_in_dim(block, 0, width, axis=dim), axis, backward)  17.3 us
    concatenate x8, other arithmetic, extended(): block = jnp.concatenate([low, block, high], axis=dim)  11.1 us
    ppermute x8, starting transfers between devices, extended(): lax.ppermute(lax.slice_in_dim(block, 0, width, axis=dim), axis, backward)  10.5 us
    reduce_sum x2, other arithmetic, body(): jnp.sum(interior_vector * near[i])  9.97 us
    slice x7, local copies, waits for them, and re-layouts, extended(): lax.slice_in_dim(block, 0, width, axis=dim)  6.84 us
  transfers between devices with their start and end apart: 17, of which 7 were waited for; matrix products, arithmetic and copies ran while one was open for 12% of the time, Pallas kernels for 0%

commit v1 on v0

v1 whole, which is shorter than its diff:
```python
import jax
import jax.numpy as jnp
from jax import lax
from jax.experimental import pallas as pl
from jax.experimental.pallas import tpu as pltpu
from jax.sharding import PartitionSpec as P

NS = 6
PATCH = 128
PLANTS = 16
ITERS = 3
HALO = ITERS + 1
CENTRE = 8.0
LANES = 128
SUBLANES = 8
F32 = jnp.float32


def pairing(count, which):
    pairs = []
    for i in range(count):
        partner = i ^ 1 if which == 0 else (i + 1 if i % 2 else i - 1)
        pairs.append((i, partner if 0 <= partner < count else i))
    return pairs


def swap(value, axis, which):
    return lax.ppermute(value, axis, pairing(lax.axis_size(axis), which))


def iota(shape, dim):
    return lax.broadcasted_iota(jnp.int32, shape, dim)


VMEM_SPEC = pl.BlockSpec(memory_space=pltpu.VMEM)
SMEM_SPEC = pl.BlockSpec(memory_space=pltpu.SMEM)


def call(kernel, outs, ins, name, scratch=(), smem=()):
    specs = [SMEM_SPEC if i in smem else VMEM_SPEC for i in range(len(ins))]
    return pl.pallas_call(
        kernel,
        out_shape=[jax.ShapeDtypeStruct(s, F32) for s in outs],
        in_specs=specs,
        out_specs=[VMEM_SPEC] * len(outs),
        scratch_shapes=list(scratch),
        name=name,
    )(*ins)


def half_swap(v):
    return pltpu.roll(v, HALO, 0)


def pack_rows_kernel(meta, u_ref, k_ref, out0, out1):
    levels, rows, cols = u_ref.shape
    upper = iota((SUBLANES, cols), 0) < HALO

    def low(l):
        u = u_ref[l, :SUBLANES, :]
        k = k_ref[l, :SUBLANES, :]
        return jnp.where(upper, u, half_swap(k))

    def high(l):
        u = u_ref[l, rows - SUBLANES :, :]
        k = k_ref[l, rows - SUBLANES :, :]
        return jnp.where(upper, half_swap(u), k)

    odd = meta[1] % 2
    for parity in range(2):

        @pl.when(odd == parity)
        def _():
            for l in range(levels):
                a, b = (high(l), low(l)) if parity == 0 else (low(l), high(l))
                out0[l] = a
                out1[l] = b


def lookup(table, kinds):
    out = jnp.full(kinds.shape, table(0), F32)
    for p in range(1, PLANTS):
        out = jnp.where(kinds == p, table(p), out)
    return out


def split(v):
    hi = v.astype(jnp.bfloat16)
    lo = (v - hi.astype(F32)).astype(jnp.bfloat16)
    return hi, lo


def source_kernel(
    meta, rows_ref, table_ref, lw_ref, u_ref, part_ref, w_ref, kind_ref, surf_ref, flux_ref, src_ref, out0, out1, picked
):
    _, nx, ny = part_ref.shape
    comp = meta[0]
    for x in range(nx):
        r = rows_ref[0, x]
        picked[:, pl.ds(x, 1), :] = part_ref[:, pl.ds(r, 1), :]
    kinds = kind_ref[0]
    own = [lookup(lambda p: lw_ref[comp, p, l], kinds) for l in range(NS)]
    own_force = own[0] * u_ref[0, 0]
    for l in range(1, NS):
        own_force = own_force + own[l] * u_ref[0, l]
    other_prof = [lookup(lambda p: lw_ref[1 - comp, p, l], kinds) for l in range(NS)]
    forces = []
    for b in range(ny // PATCH):
        cols = slice(b * PATCH, (b + 1) * PATCH)
        x_hi, x_lo = split(picked[:, :, cols].reshape(NS * nx, PATCH))
        w_hi, w_lo = split(w_ref[0, cols, :])
        dims = (((1,), (1,)), ((), ()))
        y = lax.dot_general(x_hi, w_lo, dims, preferred_element_type=F32)
        y = y + lax.dot_general(x_lo, w_hi, dims, preferred_element_type=F32)
        y = y + lax.dot_general(x_hi, w_hi, dims, preferred_element_type=F32)
        y = y.reshape(NS, nx, PATCH)
        total = other_prof[0][:, cols] * y[0]
        for l in range(1, NS):
            total = total + other_prof[l][:, cols] * y[l]
        forces.append(total)
    other_force = jnp.concatenate(forces, axis=1)
    first = comp == 0
    atmos = jnp.where(first, own_force, other_force)
    soil = jnp.where(first, other_force, own_force)
    conductance = lookup(lambda p: table_ref[p, 0], kinds)
    factor = lookup(lambda p: table_ref[p, 1], kinds)
    flux = conductance * (factor * soil - atmos)
    flux_ref[0] = flux
    signed = jnp.where(first, flux, -flux)
    upper = iota((SUBLANES, ny), 0) < HALO
    odd = meta[1] % 2 == 1
    src = []
    for l in range(NS):
        s = signed * own[l]
        if l == 0:
            s = s + surf_ref[0]
        src_ref[l] = s
        src.append(s)
    for j in range(NS // 2):
        a, b = src[2 * j], src[2 * j + 1]
        low = jnp.where(upper, a[:SUBLANES], half_swap(b[:SUBLANES]))
        high = jnp.where(upper, half_swap(a[nx - SUBLANES :]), b[nx - SUBLANES :])
        out0[j] = jnp.where(odd, low, high)
        out1[j] = jnp.where(odd, high, low)


def pack_columns_kernel(meta, u_ref, k_ref, s_ref, x0, x1, s0, s1, halo_u, halo_k, halo_s, out0, out1):
    levels, nx, ny = u_ref.shape
    upper = iota((SUBLANES, ny), 0) < HALO
    gx, count = meta[1], meta[3]
    odd = gx % 2 == 1
    has_low, has_high = gx > 0, gx < count - 1
    keep = jnp.where(upper, jnp.where(has_high, 1.0, 0.0), jnp.where(has_low, 1.0, 0.0)) != 0.0

    def halves(first, second, j):
        a, b = first[j], second[j]
        high, low = jnp.where(odd, b, a), jnp.where(odd, a, b)
        one = jnp.where(upper, high, half_swap(low))
        two = jnp.where(upper, half_swap(high), low)
        return jnp.where(keep, one, 0.0), jnp.where(keep, two, 0.0)

    def level(l, _):
        u, k = halves(x0, x1, l)
        halo_u[l] = u
        halo_k[l] = k
        return 0

    lax.fori_loop(0, levels, level, 0, unroll=5)
    for j in range(NS // 2):
        a, b = halves(s0, s1, j)
        halo_s[2 * j] = a
        halo_s[2 * j + 1] = b

    group = iota((nx + 2 * HALO, LANES), 1) // HALO
    y_odd = meta[2] % 2

    def columns(main, halo, l, high):
        at = ny - LANES if high else 0
        tile = jnp.concatenate([main[l, :, at : at + LANES], halo[l, :, at : at + LANES]], axis=0)
        return tile

    for parity in range(2):

        @pl.when(y_odd == parity)
        def _():
            for f, (main, halo, n) in enumerate(((u_ref, halo_u, levels), (k_ref, halo_k, levels), (s_ref, halo_s, NS))):
                zero = jnp.zeros((nx + 2 * HALO, LANES), F32)
                first, second = zero, zero
                for l in range(n):
                    high = pltpu.roll(columns(main, halo, l, True), (HALO * l + HALO) % LANES, 1)
                    low = columns(main, halo, l, False)
                    low = pltpu.roll(low, HALO * l, 1) if l else low
                    a, b = (high, low) if parity == 0 else (low, high)
                    first = jnp.where(group == l, a, first)
                    second = jnp.where(group == l, b, second)
                out0[f] = first
                out1[f] = second


def chain_kernel(
    meta, storage_ref, u_ref, k_ref, s_ref, halo_u, halo_k, halo_s, y0, y1,
    r_out, p1_out, p2_out, moments,
    ext_a, ext_b, keff, cz, cx, cy, inside,
):
    levels, nx, ny = u_ref.shape
    rows, cols = nx + 2 * HALO, ny + LANES
    gx, gy, ngx, ngy = meta[1], meta[2], meta[3], meta[4]
    odd = gy % 2 == 1
    has_low, has_high = gy > 0, gy < ngy - 1
    lane = iota((rows, LANES), 1)
    keep_high = lane < jnp.where(has_high, HALO, 0)
    keep_low = lane >= jnp.where(has_low, LANES - HALO, LANES)

    row = iota((rows, cols), 0)
    col = iota((rows, cols), 1)
    ok = (row < nx) | ((row < nx + HALO) & (gx < ngx - 1)) | ((row >= nx + HALO) & (gx > 0))
    ok = ok & ((col < ny) | ((col < ny + HALO) & has_high) | ((col >= cols - HALO) & has_low))
    inside[...] = jnp.where(ok, 1.0, 0.0)

    def third(f, l):
        a, b = y0[f], y1[f]
        high, low = jnp.where(odd, b, a), jnp.where(odd, a, b)
        high = pltpu.roll(high, (LANES - HALO * l) % LANES, 1) if (HALO * l) % LANES else high
        low = pltpu.roll(low, (2 * LANES - HALO - HALO * l) % LANES, 1)
        return jnp.where(keep_high, high, jnp.where(keep_low, low, 0.0))

    def extend(main, halo, f, l):
        left = jnp.concatenate([main[l], halo[l]], axis=0)
        return jnp.concatenate([left, third(f, l)], axis=1)

    for l in range(levels):
        u = extend(u_ref, halo_u, 0, l)
        ext_a[l] = u
        keff[l] = extend(k_ref, halo_k, 1, l) * (1.0 + 0.5 * jnp.tanh(u))

    def faces(l, _):
        k = keff[l]
        below = keff[jnp.maximum(l - 1, 0)]
        cz[l] = 0.5 * jnp.where(l == 0, k, k + below)
        cx[l] = 0.5 * (k + pltpu.roll(k, rows - 1, 0))
        cy[l] = 0.5 * (k + pltpu.roll(k, cols - 1, 1))
        return 0

    lax.fori_loop(0, levels, faces, 0)
    cz[levels] = 0.5 * keff[levels - 1]

    def flux_sum(src, l, v, flow, xr, yr):
        nxt = src[jnp.minimum(l + 1, levels - 1), :xr, :yr]
        nxt = jnp.where(l == levels - 1, 0.0, nxt)
        up = cz[l + 1, :xr, :yr] * (v[:xr, :yr] - nxt)
        vx = v[:, :yr]
        fx = cx[l, :, :yr] * (vx - pltpu.roll(vx, rows - 1, 0))
        vy = v[:xr]
        fy = cy[l, :xr, :] * (vy - pltpu.roll(vy, cols - 1, 1))
        dx = fx - pltpu.roll(fx, 1, 0)
        dy = fy - pltpu.roll(fy, 1, 1)
        return (up - flow) + (dx[:xr] + dy[:, :yr]), up

    def fold(v):
        v = v[:, :LANES] + v[:, LANES:] if ny == 2 * LANES else sum(v[:, c : c + LANES] for c in range(0, ny, LANES))
        total = v[:SUBLANES]
        for r in range(SUBLANES, nx, SUBLANES):
            total = total + v[r : r + SUBLANES]
        return total

    zero_tile = jnp.zeros((SUBLANES, LANES), F32)

    def residual(l, carry):
        flow, m0 = carry
        v = ext_a[l]
        w, up = flux_sum(ext_a, l, v, flow, rows, cols)
        r = -w * inside[...]
        ext_b[l] = r
        return up, m0

    flow0 = -cz[0] * ext_a[0]
    lax.fori_loop(0, levels, residual, (flow0, zero_tile))
    for l in range(NS):
        ext_b[l] = ext_b[l] + extend(s_ref, halo_s, 2, l)

    def copy_out(l, m0):
        v = ext_b[l, :nx, :ny]
        r_out[l] = v
        return m0 + fold(v * v)

    m0 = lax.fori_loop(0, levels, copy_out, zero_tile)
    shift = storage_ref[0] - CENTRE

    def apply(src, dst, out):
        def step(l, carry):
            flow, cross, square = carry
            v = src[l]
            w, up = flux_sum(src, l, v, flow, rows, cols)
            w = (w + shift * v) * inside[...]
            dst[l] = w
            own = w[:nx, :ny]
            out[l] = own
            return up, cross + fold(own * v[:nx, :ny]), square + fold(own * own)

        return lax.fori_loop(0, levels, step, (-cz[0] * src[0], zero_tile, zero_tile))[1:]

    m1, m2 = apply(ext_b, ext_a, p1_out)
    m3, m4 = apply(ext_a, ext_b, p2_out)

    def last(l, carry):
        flow, cross, square = carry
        v = ext_b[l]
        w, up = flux_sum(ext_b, l, v, flow, nx, ny)
        own_v = v[:nx, :ny]
        own = w + shift * own_v
        return up, cross + fold(own * own_v), square + fold(own * own)

    first_flow = -cz[0, :nx, :ny] * ext_b[0, :nx, :ny]
    m5, m6 = lax.fori_loop(0, levels, last, (first_flow, zero_tile, zero_tile))[1:]
    which = iota((SUBLANES, LANES), 0)
    packed = zero_tile
    for i, m in enumerate((m0, m1, m2, m3, m4, m5, m6)):
        total = jnp.sum(jnp.sum(m, axis=1, keepdims=True), axis=0, keepdims=True)
        packed = jnp.where(which == i, total, packed)
    for d in range(moments.shape[0]):
        moments[d] = packed


def update_kernel(gathered, u_ref, r_ref, p1_ref, p2_ref, out):
    total = gathered[0]
    for d in range(1, gathered.shape[0]):
        total = total + gathered[d]
    m = [total[i : i + 1, :] for i in range(7)]
    theta = CENTRE

    def gram(i, j):
        return m[i + j + 2] + 2.0 * theta * m[i + j + 1] + theta * theta * m[i + j]

    b = [m[i + 1] + theta * m[i] for i in range(3)]
    l00 = jnp.sqrt(gram(0, 0))
    l10 = gram(1, 0) / l00
    l20 = gram(2, 0) / l00
    l11 = jnp.sqrt(gram(1, 1) - l10 * l10)
    l21 = (gram(2, 1) - l20 * l10) / l11
    l22 = jnp.sqrt(gram(2, 2) - l20 * l20 - l21 * l21)
    z0 = b[0] / l00
    z1 = (b[1] - l10 * z0) / l11
    z2 = (b[2] - l20 * z0 - l21 * z1) / l22
    c2 = z2 / l22
    c1 = (z1 - l21 * c2) / l11
    c0 = (z0 - l10 * c1 - l20 * c2) / l00
    levels, nx, ny = r_ref.shape
    wide = lambda c: jnp.broadcast_to(jnp.concatenate([c] * (ny // LANES), axis=1), (nx, ny))
    c0, c1, c2 = wide(c0), wide(c1), wide(c2)

    def step(l, _):
        out[0, l] = u_ref[0, l] + c0 * r_ref[l] + c1 * p1_ref[l] + c2 * p2_ref[l]
        return 0

    lax.fori_loop(0, levels, step, 0, unroll=2)


def body(
    state, conduct, storage, surface_source, plant_type, plant_table, layer_weights, remap_rows, remap_weights
):
    levels, nx, ny = state.shape[1:]
    ngx, ngy = lax.axis_size("gx"), lax.axis_size("gy")
    meta = jnp.stack(
        [lax.axis_index("comp"), lax.axis_index("gx"), lax.axis_index("gy"), jnp.int32(ngx), jnp.int32(ngy)]
    ).astype(jnp.int32)
    field, cond = state[0], conduct[0]
    partner = lax.ppermute(field[:NS], "comp", [(i, i ^ 1) for i in range(lax.axis_size("comp"))])
    x0, x1 = call(pack_rows_kernel, [(levels, SUBLANES, ny)] * 2, [meta, field, cond], "pack_rows", smem=(0,))
    x0, x1 = swap(x0, "gx", 0), swap(x1, "gx", 1)
    flux, src, s0, s1 = call(
        source_kernel,
        [(1, nx, ny), (NS, nx, ny)] + [(NS // 2, SUBLANES, ny)] * 2,
        [meta, remap_rows, plant_table, layer_weights, state, partner, remap_weights, plant_type, surface_source],
        "source",
        scratch=[pltpu.VMEM((NS, nx, ny), F32)],
        smem=(0, 1, 2, 3),
    )
    s0, s1 = swap(s0, "gx", 0), swap(s1, "gx", 1)
    rows, cols = nx + 2 * HALO, ny + LANES
    halo_u, halo_k, halo_s, y0, y1 = call(
        pack_columns_kernel,
        [(levels, SUBLANES, ny)] * 2 + [(NS, SUBLANES, ny)] + [(3, rows, LANES)] * 2,
        [meta, field, cond, src, x0, x1, s0, s1],
        "pack_columns",
        smem=(0,),
    )
    y0, y1 = swap(y0, "gy", 0), swap(y1, "gy", 1)
    group = ngx * ngy
    full = pltpu.VMEM((levels, rows, cols), F32)
    r, p1, p2, moments = call(
        chain_kernel,
        [(levels, nx, ny)] * 3 + [(group, SUBLANES, LANES)],
        [meta, storage, field, cond, src, halo_u, halo_k, halo_s, y0, y1],
        "chain",
        scratch=[full, full, full, pltpu.VMEM((levels + 1, rows, cols), F32), full, full, pltpu.VMEM((rows, cols), F32)],
        smem=(0, 1),
    )
    gathered = lax.all_to_all(moments, ("gx", "gy"), 0, 0)
    (new_state,) = call(update_kernel, [state.shape], [gathered, state, r, p1, p2], "update")
    return new_state, flux


def solution(mesh):
    in_specs = (
        P("comp", None, "gx", "gy"),
        P("comp", None, "gx", "gy"),
        P("comp"),
        P("comp", "gx", "gy"),
        P("comp", "gx", "gy"),
        P(),
        P(),
        P("comp", "gx"),
        P("comp", "gy", None),
    )
    out_specs = (P("comp", None, "gx", "gy"), P("comp", "gx", "gy"))
    return jax.shard_map(body, mesh=mesh, in_specs=in_specs, out_specs=out_specs, check_vma=False)
```

time: 291 us -> 79.7 us (0.27)
  blocking collectives: 129 us -> 19.2 us
  other arithmetic: 53.6 us -> 0.67 us
  Pallas kernels: 0 us -> 39.3 us
  local copies, waits for them, and re-layouts: 43 us -> 4.38 us
  starting transfers between devices: 35 us -> 11 us
  waiting for transfers between devices: 17.6 us -> 3.27 us
  between operations: 9.11 us -> 1.37 us
  matrix products: 2.96 us -> 0 us
    psum x4 -> x0, blocking collectives: 129 us -> none  [the longest x3 94.4 us: body(): lax.psum((partials, jnp.sum(interior_vector * interior_vector)), ('gx', '...]
    pallas_call x0 -> x5, Pallas kernels: none -> 39.3 us  [call(): pl.pallas_call(kernel, out_shape=[jax.ShapeDtypeStruct(s, F32) for s in o...]
    ppermute x17 -> x7, starting transfers between devices: 35 us -> 11 us  [the longest x6 8.39 us: swap(): return lax.ppermute(value, axis, pairing(lax.axis_size(axis), which))]
    reduce_sum x7 -> x0, other arithmetic: 22.9 us -> none  [the longest x2 9.97 us: body(): jnp.sum(interior_vector * near[i])]
    all_to_all x0 -> x1, blocking collectives: none -> 19.2 us  [body(): gathered = lax.all_to_all(moments, ('gx', 'gy'), 0, 0)]
    slice x20 -> x1, local copies, waits for them, and re-layouts: 16.2 us -> 0.94 us  [body(): field[:NS]]
    ppermute x17 -> x7, waiting for transfers between devices: 17.6 us -> 3.27 us  [the longest x1 2.97 us: body(): lax.ppermute(field[:NS], 'comp', [(i, i ^ 1) for i in range(lax.axis_size...]
    concatenate x8 -> x0, other arithmetic: 11.1 us -> none  [extended(): block = jnp.concatenate([low, block, high], axis=dim)]
  transfers between devices with their start and end apart: 17 -> 7, of which waited for: 7 -> 2; matrix products, arithmetic and copies ran while one was open for 12% -> 3% of each run, Pallas kernels for 0% -> 4%
where the time goes in v1:
time: 79.7 us; the launch traced here: 79.2 us
  Pallas kernels  39.3 us (49%)
  blocking collectives  19.2 us (24%)
  starting transfers between devices  11 us (14%)
  local copies, waits for them, and re-layouts  4.38 us (5%)
  waiting for transfers between devices  3.27 us (4%)
  between operations  1.37 us (2%)
    pallas_call x5, Pallas kernels, call(): pl.pallas_call(kernel, out_shape=[jax.ShapeDtypeStruct(s, F32) for s in o...  39.3 us
    all_to_all x1, blocking collectives, body(): gathered = lax.all_to_all(moments, ('gx', 'gy'), 0, 0)  19.2 us
    ppermute x6, starting transfers between devices, swap(): return lax.ppermute(value, axis, pairing(lax.axis_size(axis), which))  8.39 us
    unnamed x20, local copies, waits for them, and re-layouts  3.44 us
    ppermute x1, waiting for transfers between devices, body(): lax.ppermute(field[:NS], 'comp', [(i, i ^ 1) for i in range(lax.axis_size...  2.97 us
    ppermute x1, starting transfers between devices, body(): lax.ppermute(field[:NS], 'comp', [(i, i ^ 1) for i in range(lax.axis_size...  2.57 us
  transfers between devices with their start and end apart: 7, of which 2 were waited for; matrix products, arithmetic and copies ran while one was open for 3% of the time, Pallas kernels for 4%

profile of v1, /device:TPU:0, one launch (start us, length us, event | category | flops | bytes accessed | tf_op | source)
XLA Modules:
  0.0 79.2 jit_solution(9993621736151418532)
XLA Ops:
  0.6 0.7 pad_add_fusion.meta
  1.3 2.3 %pack_rows.1 = (f32[30,8,256]{2,1,0:T(8,128)}, f32[30,8,256]{2,1,0:T(8,128)}) custom-call(s32[5]{0:T(128)} %pad_add_fusion.meta, f32[30,32,256]{2,1,0:T(8,128)} %bitcast.7, f32[30,32,256]{2,1,0:T(8,128)} %bitcast.10), custom_call_target="tpu_custom_call" | custom-call | tf_op jit(solution)/shard_map/pack_rows/pallas_call | solution.py:41
  3.7 0.5 collective-permute-start.1
  4.2 1.7 %collective-permute-start.2 = (f32[30,8,256]{2,1,0:T(8,128)}, f32[30,8,256]{2,1,0:T(8,128)S(1)}, u32[]{:S(2)}, u32[]{:S(2)}) collective-permute-start(f32[30,8,256]{2,1,0:T(8,128)} %get-tuple-element.19), channel_id=1, source_target_pairs={{0,0},{4,8},{8,4},{12,12},{1,1},{5,9},{9,5},{13,13},{2,2},{6,10},{... | collective-permute-start | bytes 737288 | tf_op jit(solution)/shard_map/ppermute | solution.py:28
  5.9 0.9 %slice_bitcast_fusion = f32[6,32,256]{2,1,0:T(8,128)S(1)} fusion(f32[1,30,32,256]{3,2,1,0:T(8,128)} %u_ref.3), kind=kLoop, calls=%fused_computation | loop fusion | bytes 393216 | tf_op jit(solution)/shard_map/slice | solution.py:367
  6.8 0.0 copy-start.7
  6.8 2.6 %collective-permute-start = (f32[6,32,256]{2,1,0:T(8,128)S(1)}, f32[6,32,256]{2,1,0:T(8,128)S(1)}, u32[]{:S(2)}, u32[]{:S(2)}) collective-permute-start(f32[6,32,256]{2,1,0:T(8,128)S(1)} %slice_bitcast_fusion), channel_id=1, source_target_pairs={{0,16},{16,0},{1,17},{17,1},{2,18},{18,2},{3,19},{19,3},{4,20},{20... | collective-permute-start | bytes 589832 | tf_op jit(solution)/shard_map/ppermute | solution.py:367
  9.4 0.7 copy.11.table_ref
  10.1 0.7 copy.12.lw_ref
  10.8 3.0 %collective-permute-done.part_ref = f32[6,32,256]{2,1,0:T(8,128)S(1)} collective-permute-done((f32[6,32,256]{2,1,0:T(8,128)S(1)}, f32[6,32,256]{2,1,0:T(8,128)S(1)}, u32[]{:S(2)}, u32[]{:S(2)}) %collective-permute-start) | collective-permute-done | bytes 196640 | tf_op jit(solution)/shard_map/ppermute | solution.py:367
  13.7 0.7 copy-done.2
  14.4 2.8 %source.1 = (f32[1,32,256]{2,1,0:T(8,128)}, f32[6,32,256]{2,1,0:T(8,128)}, f32[3,8,256]{2,1,0:T(8,128)}, f32[3,8,256]{2,1,0:T(8,128)}) custom-call(s32[5]{0:T(128)} %pad_add_fusion.meta, s32[1,32]{1,0:T(1,128)} %rows_ref.1, f32[16,2]{1,0:T(8,128)} %copy.11.table_ref, f32[2,16,6]{2,1,0:T(8,128)} %copy.12.lw_ref, f32[1,30,32,256]{3,2,1,0:T(8,128)} %u_ref.3, ...), custom_call_target="tpu_custom_call" | custom-call | tf_op jit(solution)/shard_map/source/pallas_call | solution.py:41
  17.2 1.2 %collective-permute-start.3 = (f32[3,8,256]{2,1,0:T(8,128)}, f32[3,8,256]{2,1,0:T(8,128)S(1)}, u32[]{:S(2)}, u32[]{:S(2)}) collective-permute-start(f32[3,8,256]{2,1,0:T(8,128)} %get-tuple-element.20), channel_id=1, source_target_pairs={{0,4},{4,0},{8,12},{12,8},{1,5},{5,1},{9,13},{13,9},{2,6},{6,2},{1... | collective-permute-start | bytes 73736 | tf_op jit(solution)/shard_map/ppermute | solution.py:28
  18.5 1.4 %collective-permute-start.4 = (f32[3,8,256]{2,1,0:T(8,128)}, f32[3,8,256]{2,1,0:T(8,128)S(1)}, u32[]{:S(2)}, u32[]{:S(2)}) collective-permute-start(f32[3,8,256]{2,1,0:T(8,128)} %get-tuple-element.21), channel_id=1, source_target_pairs={{0,0},{4,8},{8,4},{12,12},{1,1},{5,9},{9,5},{13,13},{2,2},{6,10},{... | collective-permute-start | bytes 73736 | tf_op jit(solution)/shard_map/ppermute | solution.py:28
  19.8 0.0 collective-permute-done.3.s0
  19.8 0.0 collective-permute-done.4.s1
  19.9 0.0 collective-permute-done.1.x0
  19.9 0.0 copy-start
  19.9 0.0 collective-permute-done.2.x1
  19.9 0.5 copy-done.5
  20.4 0.0 copy-done.6
  20.5 0.1 copy-done
  20.6 0.1 copy-done.1
  20.6 3.4 %pack_columns.1 = (f32[30,8,256]{2,1,0:T(8,128)}, f32[30,8,256]{2,1,0:T(8,128)}, f32[6,8,256]{2,1,0:T(8,128)}, f32[3,40,128]{2,1,0:T(8,128)}, f32[3,40,128]{2,1,0:T(8,128)}) custom-call(s32[5]{0:T(128)} %pad_add_fusion.meta, f32[30,32,256]{2,1,0:T(8,128)} %bitcast.8, f32[30,32,256]{2,1,0:T(8,128)} %bitcast.11, f32[6,32,256]{2,1,0:T(8,128)} %get-tuple-element.17.s_ref, ...), custom_call_target="tpu_custom_call" | custom-call | tf_op jit(solution)/shard_map/pack_columns/pallas_call | solution.py:41
  24.1 2.1 %collective-permute-start.5 = (f32[3,40,128]{2,1,0:T(8,128)}, f32[3,40,128]{2,1,0:T(8,128)S(1)}, u32[]{:S(2)}, u32[]{:S(2)}) collective-permute-start(f32[3,40,128]{2,1,0:T(8,128)} %get-tuple-element.25), channel_id=1, source_target_pairs={{0,1},{1,0},{2,3},{3,2},{4,5},{5,4},{6,7},{7,6},{8,9},{9,8},{10,11... | collective-permute-start | bytes 184328 | tf_op jit(solution)/shard_map/ppermute | solution.py:28
  26.2 1.5 %collective-permute-start.6 = (f32[3,40,128]{2,1,0:T(8,128)}, f32[3,40,128]{2,1,0:T(8,128)S(1)}, u32[]{:S(2)}, u32[]{:S(2)}) collective-permute-start(f32[3,40,128]{2,1,0:T(8,128)} %get-tuple-element.26), channel_id=1, source_target_pairs={{0,0},{1,2},{2,1},{3,3},{4,4},{5,6},{6,5},{7,7},{8,8},{9,10},{10,9... | collective-permute-start | bytes 184328 | tf_op jit(solution)/shard_map/ppermute | solution.py:28
  28.3 0.3 collective-permute-done.5.y0
  28.6 0.6 copy-done.3
  29.2 0.0 copy-done.4
  29.2 27.4 %chain.1 = (f32[30,32,256]{2,1,0:T(8,128)}, f32[30,32,256]{2,1,0:T(8,128)}, f32[30,32,256]{2,1,0:T(8,128)}, f32[16,8,128]{2,1,0:T(8,128)}) custom-call(s32[5]{0:T(128)} %pad_add_fusion.meta, f32[1]{0:T(128)S(6)} %copy.13.storage_ref, f32[30,32,256]{2,1,0:T(8,128)} %bitcast.9, f32[30,32,256]{2,1,0:T(8,128)} %bitcast.12, ...), custom_call_target="tpu_custom_call" | custom-call | tf_op jit(solution)/shard_map/chain/pallas_call | solution.py:41
  56.6 19.2 %all_to_all.5.gathered = f32[16,8,128]{2,1,0:T(8,128)} all-to-all(f32[16,8,128]{2,1,0:T(8,128)} %get-tuple-element.27), channel_id=1, replica_groups=mesh['comp'=2,'gx'=4,'gy'=4] {'gx','gy'}, dimensions={0} | all-to-all | bytes 131072 | tf_op jit(solution)/shard_map/all_to_all | solution.py:398
  75.7 3.4 %update.1 = f32[1,30,32,256]{3,2,1,0:T(8,128)} custom-call(f32[16,8,128]{2,1,0:T(8,128)} %all_to_all.5.gathered, f32[1,30,32,256]{3,2,1,0:T(8,128)} %u_ref.3, f32[30,32,256]{2,1,0:T(8,128)} %get-tuple-element.28.r_ref, f32[30,32,256]{2,1,0:T(8,128)} %get-tuple-element.29.p1_ref, f32[30,32,256]{2,1,0:T(8,128)} %get-tuple-element.30.p2_ref), custom_call_target="tpu_custom_call" | custom-call | tf_op jit(solution)/shard_map/update/pallas_call | solution.py:41
  (11 shorter events, 0.0 us)
Async XLA Ops:
  3.7 16.2 %collective-permute-start.1 = (f32[30,8,256]{2,1,0:T(8,128)}, f32[30,8,256]{2,1,0:T(8,128)S(1)}, u32[]{:S(2)}, u32[]{:S(2)}) collective-permute-start(f32[30,8,256]{2,1,0:T(8,128)} %get-tuple-element.18), channel_id=1, source_target_pairs={{0,4},{4,0},{8,12},{12,8},{1,5},{5,1},{9,13},{13,9},{2,6},{6,2},{1... | collective-permute-start | bytes 737288 | tf_op jit(solution)/shard_map/ppermute | solution.py:28
  4.1 5.3 %copy-start.8 = (f32[16,2]{0,1:T(2,128)S(1)}, f32[16,2]{0,1:T(2,128)}, u32[]{:S(2)}) copy-start(f32[16,2]{0,1:T(2,128)} %param.14) | copy-start | bytes 388
  4.2 15.7 %collective-permute-start.2 = (f32[30,8,256]{2,1,0:T(8,128)}, f32[30,8,256]{2,1,0:T(8,128)S(1)}, u32[]{:S(2)}, u32[]{:S(2)}) collective-permute-start(f32[30,8,256]{2,1,0:T(8,128)} %get-tuple-element.19), channel_id=1, source_target_pairs={{0,0},{4,8},{8,4},{12,12},{1,1},{5,9},{9,5},{13,13},{2,2},{6,10},{... | collective-permute-start | bytes 737288 | tf_op jit(solution)/shard_map/ppermute | solution.py:28
  6.8 3.3 %copy-start.7 = (f32[2,16,6]{1,0,2:T(2,128)S(1)}, f32[2,16,6]{1,0,2:T(2,128)}, u32[]{:S(2)}) copy-start(f32[2,16,6]{1,0,2:T(2,128)} %param.15) | copy-start | bytes 2308
  6.8 6.9 %collective-permute-start = (f32[6,32,256]{2,1,0:T(8,128)S(1)}, f32[6,32,256]{2,1,0:T(8,128)S(1)}, u32[]{:S(2)}, u32[]{:S(2)}) collective-permute-start(f32[6,32,256]{2,1,0:T(8,128)S(1)} %slice_bitcast_fusion), channel_id=1, source_target_pairs={{0,16},{16,0},{1,17},{17,1},{2,18},{18,2},{3,19},{19,3},{4,20},{20... | collective-permute-start | bytes 589832 | tf_op jit(solution)/shard_map/ppermute | solution.py:367
  13.7 0.7 copy-start.2
  17.2 2.6 %collective-permute-start.3 = (f32[3,8,256]{2,1,0:T(8,128)}, f32[3,8,256]{2,1,0:T(8,128)S(1)}, u32[]{:S(2)}, u32[]{:S(2)}) collective-permute-start(f32[3,8,256]{2,1,0:T(8,128)} %get-tuple-element.20), channel_id=1, source_target_pairs={{0,4},{4,0},{8,12},{12,8},{1,5},{5,1},{9,13},{13,9},{2,6},{6,2},{1... | collective-permute-start | bytes 73736 | tf_op jit(solution)/shard_map/ppermute | solution.py:28
  18.5 1.4 %collective-permute-start.4 = (f32[3,8,256]{2,1,0:T(8,128)}, f32[3,8,256]{2,1,0:T(8,128)S(1)}, u32[]{:S(2)}, u32[]{:S(2)}) collective-permute-start(f32[3,8,256]{2,1,0:T(8,128)} %get-tuple-element.21), channel_id=1, source_target_pairs={{0,0},{4,8},{8,4},{12,12},{1,1},{5,9},{9,5},{13,13},{2,2},{6,10},{... | collective-permute-start | bytes 73736 | tf_op jit(solution)/shard_map/ppermute | solution.py:28
  19.8 0.6 copy-start.5
  19.9 0.6 copy-start.6
  19.9 0.7 copy-start
  19.9 0.8 copy-start.1
  24.1 4.5 %collective-permute-start.5 = (f32[3,40,128]{2,1,0:T(8,128)}, f32[3,40,128]{2,1,0:T(8,128)S(1)}, u32[]{:S(2)}, u32[]{:S(2)}) collective-permute-start(f32[3,40,128]{2,1,0:T(8,128)} %get-tuple-element.25), channel_id=1, source_target_pairs={{0,1},{1,0},{2,3},{3,2},{4,5},{5,4},{6,7},{7,6},{8,9},{9,8},{10,11... | collective-permute-start | bytes 184328 | tf_op jit(solution)/shard_map/ppermute | solution.py:28
  26.2 2.4 %collective-permute-start.6 = (f32[3,40,128]{2,1,0:T(8,128)}, f32[3,40,128]{2,1,0:T(8,128)S(1)}, u32[]{:S(2)}, u32[]{:S(2)}) collective-permute-start(f32[3,40,128]{2,1,0:T(8,128)} %get-tuple-element.26), channel_id=1, source_target_pairs={{0,0},{1,2},{2,1},{3,3},{4,4},{5,6},{6,5},{7,7},{8,8},{9,10},{10,9... | collective-permute-start | bytes 184328 | tf_op jit(solution)/shard_map/ppermute | solution.py:28
  28.6 0.6 copy-start.3
  28.6 0.6 copy-start.4

commit v2 on v1

v2 whole, which is shorter than its diff:
```python
import jax
import jax.numpy as jnp
from jax import lax
from jax.experimental import pallas as pl
from jax.experimental.pallas import tpu as pltpu
from jax.sharding import PartitionSpec as P

NS = 6
PATCH = 128
PLANTS = 16
ITERS = 3
HALO = ITERS + 1
CENTRE = 8.0
LANES = 128
SUB = 8
MOMENTS = 2 * ITERS + 1
PROFILES = 2 * NS + 3
F32 = jnp.float32
MIB = 1 << 20


def pairing(count, which):
    pairs = []
    for i in range(count):
        partner = i ^ 1 if which == 0 else (i + 1 if i % 2 else i - 1)
        pairs.append((i, partner if 0 <= partner < count else i))
    return pairs


def swap(value, axis, which):
    return lax.ppermute(value, axis, pairing(lax.axis_size(axis), which))


def everyone(value, axis):
    n = lax.axis_size(axis)
    return [value] + [lax.ppermute(value, axis, [(i, i ^ d) for i in range(n)]) for d in range(1, n)]


def iota(shape, dim):
    return lax.broadcasted_iota(jnp.int32, shape, dim)


VMEM_SPEC = pl.BlockSpec(memory_space=pltpu.VMEM)
SMEM_SPEC = pl.BlockSpec(memory_space=pltpu.SMEM)
HBM_SPEC = pl.BlockSpec(memory_space=pltpu.HBM)


def call(kernel, outs, ins, name, scratch=(), smem=(), hbm=(), hbm_outs=(), limit=2, alias=None):
    def spec(i):
        return SMEM_SPEC if i in smem else HBM_SPEC if i in hbm else VMEM_SPEC

    def place(i, v):
        if i in smem:
            return v
        return pltpu.with_memory_space_constraint(v, pltpu.HBM if i in hbm else pltpu.VMEM)

    return pl.pallas_call(
        kernel,
        out_shape=[jax.ShapeDtypeStruct(s, F32) if i in hbm_outs else pltpu.VMEM(s, F32) for i, s in enumerate(outs)],
        in_specs=[spec(i) for i in range(len(ins))],
        out_specs=[HBM_SPEC if i in hbm_outs else VMEM_SPEC for i in range(len(outs))],
        scratch_shapes=list(scratch),
        input_output_aliases=alias or {},
        name=name,
        compiler_params=pltpu.CompilerParams(vmem_limit_bytes=limit * MIB),
    )(*[place(i, v) for i, v in enumerate(ins)])


def half_swap(v):
    return pltpu.roll(v, HALO, 0)


def layers_kernel(u_hbm, layers, sem):
    copy = pltpu.make_async_copy(u_hbm.at[0, pl.ds(0, NS)], layers, sem)
    copy.start()
    copy.wait()


def edges_kernel(u_hbm, k_hbm, out0, out1, low_u, low_k, high_u, high_k, sems):
    _, levels, rows, cols = u_hbm.shape
    copies = [
        pltpu.make_async_copy(u_hbm.at[0, :, pl.ds(0, SUB)], low_u, sems.at[0]),
        pltpu.make_async_copy(k_hbm.at[0, :, pl.ds(0, SUB)], low_k, sems.at[1]),
        pltpu.make_async_copy(u_hbm.at[0, :, pl.ds(rows - SUB, SUB)], high_u, sems.at[2]),
        pltpu.make_async_copy(k_hbm.at[0, :, pl.ds(rows - SUB, SUB)], high_k, sems.at[3]),
    ]
    for c in copies:
        c.start()
    upper = iota((SUB, cols), 0) < HALO
    odd = lax.axis_index("gx") % 2 == 1
    for c in copies:
        c.wait()
    for l in range(levels):
        low = jnp.where(upper, low_u[l], half_swap(low_k[l]))
        high = jnp.where(upper, half_swap(high_u[l]), high_k[l])
        out0[l] = jnp.where(odd, low, high)
        out1[l] = jnp.where(odd, high, low)


def own_kernel(
    table_hbm, lw_hbm, u_hbm, k_hbm, kind_hbm, ext_u, ext_k, prof, table, lw, u_ref, k_ref, kind_ref, sems, field_sems
):
    _, levels, nx, ny = u_ref.shape
    tiles = ny // LANES
    comp = lax.axis_index("comp")
    small = [
        pltpu.make_async_copy(table_hbm, table, sems.at[0]),
        pltpu.make_async_copy(lw_hbm, lw, sems.at[1]),
        pltpu.make_async_copy(kind_hbm, kind_ref, sems.at[2]),
    ]
    for copy in small:
        copy.start()
    pieces = field_sems.shape[0]
    bounds = [levels * i // pieces for i in range(pieces + 1)]
    fields = []
    for i in range(pieces):
        part = pl.ds(bounds[i], bounds[i + 1] - bounds[i])
        pair = [
            pltpu.make_async_copy(u_hbm.at[0, part], u_ref.at[0, part], field_sems.at[i, 0]),
            pltpu.make_async_copy(k_hbm.at[0, part], k_ref.at[0, part], field_sems.at[i, 1]),
        ]
        for copy in pair:
            copy.start()
        fields.append(pair)
    blank = jnp.zeros((nx + 2 * SUB, LANES), F32)
    for t in range(tiles + 1):
        for ext in (ext_u, ext_k):
            ext[0, t] = blank
            ext[levels + 1, t] = blank
    for copy in small:
        copy.wait()
    for x in range(0, nx, SUB):
        rows = slice(x, x + SUB)
        kinds = kind_ref[0, rows]
        tables = [lambda p, l=l: lw[l, comp, p] for l in range(NS)]
        tables += [lambda p, l=l: lw[l, 1 - comp, p] for l in range(NS)]
        tables += [lambda p, q=q: table[q, p] for q in range(2)]
        found = [jnp.full(kinds.shape, t(0), F32) for t in tables]
        for p in range(1, PLANTS):
            here = kinds == p
            found = [jnp.where(here, t(p), f) for t, f in zip(tables, found)]
        for i, f in enumerate(found):
            prof[i, rows] = f

    for i in range(pieces):
        for copy in fields[i]:
            copy.wait()

        def level(l, _):
            for t in range(tiles):
                u = u_ref[0, l, :, t * LANES : (t + 1) * LANES]
                k = k_ref[0, l, :, t * LANES : (t + 1) * LANES]
                ext_u[l + 1, t, SUB : SUB + nx] = u
                ext_k[l + 1, t, SUB : SUB + nx] = k * (0.5 + 0.25 * jnp.tanh(u))
            return 0

        lax.fori_loop(bounds[i], bounds[i + 1], level, 0, unroll=2)
    force = prof[0] * u_ref[0, 0]
    for l in range(1, NS):
        force = force + prof[l] * u_ref[0, l]
    prof[2 * NS + 2] = force


def split(v):
    hi = v.astype(jnp.bfloat16)
    lo = (v - hi.astype(F32)).astype(jnp.bfloat16)
    return hi, lo


def source_kernel(rows_ref, part_ref, w_ref, prof, surf_ref, flux_ref, src_ref, out0, out1, picked):
    _, nx, ny = part_ref.shape
    first = lax.axis_index("comp") == 0
    odd = lax.axis_index("gx") % 2 == 1
    for x in range(nx):
        r = rows_ref[0, x]
        picked[:, pl.ds(x, 1), :] = part_ref[:, pl.ds(r, 1), :]
    forces = []
    for b in range(ny // PATCH):
        cols = slice(b * PATCH, (b + 1) * PATCH)
        x_hi, x_lo = split(picked[:, :, cols].reshape(NS * nx, PATCH))
        w_hi, w_lo = split(w_ref[0, cols, :])
        dims = (((1,), (1,)), ((), ()))
        y = lax.dot_general(x_hi, w_lo, dims, preferred_element_type=F32)
        y = y + lax.dot_general(x_lo, w_hi, dims, preferred_element_type=F32)
        y = y + lax.dot_general(x_hi, w_hi, dims, preferred_element_type=F32)
        y = y.reshape(NS, nx, PATCH)
        total = prof[NS, :, cols] * y[0]
        for l in range(1, NS):
            total = total + prof[NS + l, :, cols] * y[l]
        forces.append(total)
    other_force = jnp.concatenate(forces, axis=1)
    own_force = prof[2 * NS + 2]
    atmos = jnp.where(first, own_force, other_force)
    soil = jnp.where(first, other_force, own_force)
    flux = prof[2 * NS] * (prof[2 * NS + 1] * soil - atmos)
    flux_ref[0] = flux
    signed = jnp.where(first, flux, -flux)
    upper = iota((SUB, ny), 0) < HALO
    src = []
    for l in range(NS):
        s = signed * prof[l]
        if l == 0:
            s = s + surf_ref[0]
        src_ref[l] = s
        src.append(s)
    for j in range(NS // 2):
        a, b = src[2 * j], src[2 * j + 1]
        low = jnp.where(upper, a[:SUB], half_swap(b[:SUB]))
        high = jnp.where(upper, half_swap(a[nx - SUB :]), b[nx - SUB :])
        out0[j] = jnp.where(odd, low, high)
        out1[j] = jnp.where(odd, high, low)


def columns_kernel(start, ext_u_in, ext_k_in, s_ref, x0, x1, s0, s1, ext_u, ext_k, ext_s, out0, out1):
    levels = ext_u.shape[0] - 2
    nx, ny = s_ref.shape[1:]
    tiles = ny // LANES
    upper = iota((SUB, LANES), 0) < HALO
    gx, count = lax.axis_index("gx"), lax.axis_size("gx")
    odd = gx % 2 == 1
    keep_low = upper & (gx < 0) | ~upper & (gx > 0)
    keep_high = upper & (gx < count - 1)

    def halves(first, second, j, cols):
        a, b = first[j, :, cols], second[j, :, cols]
        high, low = jnp.where(odd, b, a), jnp.where(odd, a, b)
        lows = jnp.where(keep_low, half_swap(low), 0.0), jnp.where(keep_low, low, 0.0)
        highs = jnp.where(keep_high, high, 0.0), jnp.where(keep_high, half_swap(high), 0.0)
        return lows, highs

    def level(l, _):
        for t in range(tiles):
            lows, highs = halves(x0, x1, l, slice(t * LANES, (t + 1) * LANES))
            for rows, (u, k) in ((slice(0, SUB), lows), (slice(SUB + nx, 2 * SUB + nx), highs)):
                ext_u[l + 1, t, rows] = u
                ext_k[l + 1, t, rows] = k * (0.5 + 0.25 * jnp.tanh(u))
        return 0

    lax.fori_loop(0, levels, level, 0, unroll=2)
    for j in range(NS // 2):
        for t in range(tiles):
            cols = slice(t * LANES, (t + 1) * LANES)
            lows, highs = halves(s0, s1, j, cols)
            for i in range(2):
                ext_s[2 * j + i, t, :SUB] = lows[i]
                ext_s[2 * j + i, t, SUB : SUB + nx] = s_ref[2 * j + i, :, cols]
                ext_s[2 * j + i, t, SUB + nx :] = highs[i]

    y_odd = lax.axis_index("gy") % 2
    window = nx + 2 * HALO
    group = iota((window, LANES), 1) // HALO
    first_high = y_odd == 0
    tile0 = jnp.where(first_high, tiles - 1, 0)
    tile1 = tiles - 1 - tile0
    move0 = jnp.where(first_high, HALO, 0)
    move1 = HALO - move0
    for f, (ext, base, n) in enumerate(((ext_u, 1, levels), (ext_k, 1, levels), (ext_s, 0, NS))):
        for out, tile, move in ((out0, tile0, move0), (out1, tile1, move1)):
            packed = jnp.zeros((window, LANES), F32)
            for l in range(n):
                v = ext[l + base, tile, pl.ds(start[0], window)]
                v = pltpu.roll(v, (HALO * l + move) % LANES, 1)
                packed = jnp.where(group == l, v, packed)
            out[f] = packed


def chain_kernel(
    start, storage_ref, ext_u_in, ext_k_in, ext_s, y0, y1, flux,
    ext_u, r, p1, p2, moments, flux_out,
    cz, cx, cy, cy_low, diag, inside, sem,
):
    flux_copy = pltpu.make_async_copy(flux, flux_out, sem)
    flux_copy.start()
    levels = ext_u.shape[0] - 2
    tiles, all_rows = ext_u.shape[1] - 1, ext_u.shape[2]
    nx = all_rows - 2 * SUB
    window = nx + 2 * HALO
    gx, gy, ngx, ngy = lax.axis_index("gx"), lax.axis_index("gy"), lax.axis_size("gx"), lax.axis_size("gy")
    odd = gy % 2 == 1
    has_low, has_high = gy > 0, gy < ngy - 1
    lane = iota((window, LANES), 1)
    keep_high = lane < jnp.where(has_high, HALO, 0)
    keep_low = lane >= jnp.where(has_low, LANES - HALO, LANES)
    base = start[0]
    ext_k = ext_k_in

    def third(f, l):
        a, b = y0[f], y1[f]
        high, low = jnp.where(odd, b, a), jnp.where(odd, a, b)
        high = pltpu.roll(high, (LANES - HALO * l) % LANES, 1) if (HALO * l) % LANES else high
        low = pltpu.roll(low, (2 * LANES - HALO - HALO * l) % LANES, 1)
        return jnp.where(keep_high, high, jnp.where(keep_low, low, 0.0))

    zero_tile = jnp.zeros((SUB, LANES), F32)
    for l in range(levels):
        for f, ext in enumerate((ext_u, ext_k)):
            ext[l + 1, tiles, :SUB] = zero_tile
            ext[l + 1, tiles, SUB + nx :] = zero_tile
            ext[l + 1, tiles, pl.ds(base, window)] = third(f, l)
    blank = jnp.zeros((all_rows, LANES), F32)
    for t in range(tiles + 1):
        for ext in (r, p1, p2):
            ext[0, t] = blank
            ext[levels + 1, t] = blank

    row = iota((all_rows, LANES), 0) - SUB
    col = iota((all_rows, LANES), 1)
    row_ok = ((row >= 0) & (row < nx)) | ((row >= nx) & (gx < ngx - 1)) | ((row < 0) & (gx > 0))
    col_ok = ((col < HALO) & has_high) | ((col >= LANES - HALO) & has_low)
    inside[0] = jnp.where(row_ok, 1.0, 0.0)
    inside[1] = jnp.where(row_ok & col_ok, 1.0, 0.0)

    lane8 = iota((SUB, LANES), 1)
    at_end, at_start = lane8 == LANES - 1, lane8 == 0

    def beside(vs):
        n = len(vs)
        up = [pltpu.roll(v, LANES - 1, 1) for v in vs]
        down = [pltpu.roll(v, 1, 1) for v in vs]
        ups = [jnp.where(at_end, up[(t + 1) % n], up[t]) for t in range(n)]
        downs = [jnp.where(at_start, down[(t - 1) % n], down[t]) for t in range(n)]
        return ups, downs

    def masked(w, t, at, chunk):
        if t == tiles:
            return w * inside[1, pl.ds(at, SUB)]
        if chunk in (0, chunks - 1):
            return w * inside[0, pl.ds(at, SUB)]
        return w

    shift = storage_ref[0] - CENTRE
    chunks = window // SUB
    every = range(tiles + 1)
    few = next(n for n in (3, 2, 1) if levels % n == 0)
    many = next(n for n in (6, 5, 4, 3, 2, 1) if levels % n == 0)

    def prepare(j, _):
        first = j * few
        for c in range(chunks):
            at = base + SUB * c
            rows = pl.ds(at, SUB)

            def load(ext, plane, dx=0):
                return [ext[first + plane, t, pl.ds(at + dx, SUB)] for t in every]

            k_last, u_last = load(ext_k, 0), load(ext_u, 0)
            k, u = load(ext_k, 1), load(ext_u, 1)
            below = [k[t] + k_last[t] for t in every]
            for i in range(few):
                l = first + i
                k_next, u_next = load(ext_k, i + 2), load(ext_u, i + 2)
                ks = [load(ext_k, i + 1, dx) for dx in (1, -1)]
                us = [load(ext_u, i + 1, dx) for dx in (1, -1)]
                yk, yu = beside(k), beside(u)
                above = [k[t] + k_next[t] for t in every]
                for t in every:
                    y_up, y_down = yk[0][t] + k[t], yk[1][t] + k[t]
                    x_up, x_down = ks[0][t] + k[t], ks[1][t] + k[t]
                    total = ((y_up + y_down) + (x_up + x_down)) + (above[t] + below[t])
                    flow = (y_up * yu[0][t] + y_down * yu[1][t]) + (x_up * us[0][t] + x_down * us[1][t])
                    flow = flow + (above[t] * u_next[t] + below[t] * u_last[t])
                    cy[l, t, rows] = y_up
                    cy_low[l, t, rows] = y_down
                    cx[l, t, rows] = x_up
                    cz[l, t, rows] = below[t]
                    diag[l, t, rows] = total + shift
                    r[l + 1, t, rows] = masked(flow - total * u[t], t, at, c)
                k_last, u_last, k, u, below = k, u, k_next, u_next, above
        return 0

    lax.fori_loop(0, levels // few, prepare, 0)
    for c in range(chunks):
        at = base + SUB * c
        for t in every:
            cz[levels, t, pl.ds(at, SUB)] = zero_tile
    for l in range(NS):
        for t in range(tiles):
            rows = pl.ds(base, window)
            r[l + 1, t, rows] = r[l + 1, t, rows] + ext_s[l, t, rows]
        rows = pl.ds(base, window)
        r[l + 1, tiles, rows] = r[l + 1, tiles, rows] + third(2, l)

    def operator(src, l, at, outs, unroll):
        rows = pl.ds(at, SUB)
        planes = [[src[l + i, t, rows] for t in every] for i in range(unroll + 2)]
        faces = [[cz[l + i, t, rows] for t in outs] for i in range(unroll + 1)]
        for i in range(unroll):
            v = planes[i + 1]
            v_up, v_down = beside(v)
            ws = []
            for t in outs:
                z = faces[i + 1][t] * planes[i + 2][t] + faces[i][t] * planes[i][t]
                x = cx[l + i, t, rows] * src[l + i + 1, t, pl.ds(at + 1, SUB)]
                x = x + cx[l + i, t, pl.ds(at - 1, SUB)] * src[l + i + 1, t, pl.ds(at - 1, SUB)]
                y = cy[l + i, t, rows] * v_up[t] + cy_low[l + i, t, rows] * v_down[t]
                ws.append((diag[l + i, t, rows] * v[t] - z) - (x + y))
            yield i, v, ws

    def apply(src, dst):
        def step(j, _):
            l = j * many
            for c in range(chunks):
                at = base + SUB * c
                for i, _, ws in operator(src, l, at, every, many):
                    for t, w in enumerate(ws):
                        dst[l + i + 1, t, pl.ds(at, SUB)] = masked(w, t, at, c)
            return 0

        lax.fori_loop(0, levels // many, step, 0)

    apply(r, p1)
    apply(p1, p2)

    def last(j, sums):
        l = j * many
        sums = list(sums)
        for c in range(nx // SUB):
            at = SUB + SUB * c
            for i, v, ws in operator(p2, l, at, range(tiles), many):
                for t in range(tiles):
                    rows = pl.ds(at, SUB)
                    a, b, w = r[l + i + 1, t, rows], p1[l + i + 1, t, rows], ws[t]
                    for q, term in enumerate((a * a, a * b, b * b, b * v[t], v[t] * v[t], v[t] * w, w * w)):
                        sums[q] = sums[q] + term
        return tuple(sums)

    sums = lax.fori_loop(0, levels // many, last, (zero_tile,) * MOMENTS)
    which = iota((SUB, LANES), 0)
    packed = zero_tile
    for i, m in enumerate(sums):
        total = jnp.sum(jnp.sum(m, axis=1, keepdims=True), axis=0, keepdims=True)
        packed = jnp.where(which == i, total, packed)
    moments[...] = packed
    flux_copy.wait()


def add_kernel(*refs):
    *ins, out = refs
    total = ins[0][...]
    for x in ins[1:]:
        total = total + x[...]
    out[...] = total


def update_kernel(*refs):
    *parts, u_ref, r, p1, p2, out, stage, sems = refs
    total = parts[0][...]
    for x in parts[1:]:
        total = total + x[...]
    m = [total[i : i + 1, :] for i in range(MOMENTS)]

    def gram(i, j):
        return m[i + j + 2] + 2.0 * CENTRE * m[i + j + 1] + CENTRE * CENTRE * m[i + j]

    b = [m[i + 1] + CENTRE * m[i] for i in range(ITERS)]
    l00 = jnp.sqrt(gram(0, 0))
    l10 = gram(1, 0) / l00
    l20 = gram(2, 0) / l00
    l11 = jnp.sqrt(gram(1, 1) - l10 * l10)
    l21 = (gram(2, 1) - l20 * l10) / l11
    l22 = jnp.sqrt(gram(2, 2) - l20 * l20 - l21 * l21)
    z0 = b[0] / l00
    z1 = (b[1] - l10 * z0) / l11
    z2 = (b[2] - l20 * z0 - l21 * z1) / l22
    c2 = z2 / l22
    c1 = (z1 - l21 * c2) / l11
    c0 = (z0 - l10 * c1 - l20 * c2) / l00
    _, levels, nx, ny = stage.shape
    c0, c1, c2 = (jnp.broadcast_to(c, (nx, LANES)) for c in (c0, c1, c2))
    pieces = sems.shape[0]
    per = levels // pieces
    copies = []
    for piece in range(pieces):
        lo = piece * per
        n = per if piece < pieces - 1 else levels - lo

        def step(l, _):
            for t in range(ny // LANES):
                rows = slice(SUB, SUB + nx)
                v = u_ref[l + 1, t, rows] + c0 * r[l + 1, t, rows]
                v = v + (c1 * p1[l + 1, t, rows] + c2 * p2[l + 1, t, rows])
                stage[0, l, :, t * LANES : (t + 1) * LANES] = v
            return 0

        lax.fori_loop(lo, lo + n, step, 0, unroll=2)
        copy = pltpu.make_async_copy(stage.at[0, pl.ds(lo, n)], out.at[0, pl.ds(lo, n)], sems.at[piece])
        copy.start()
        copies.append(copy)
    for copy in copies:
        copy.wait()


def body(
    state, conduct, storage, surface_source, plant_type, plant_table, layer_weights, remap_rows, remap_weights
):
    levels, nx, ny = state.shape[1:]
    tiles = ny // LANES
    window = nx + 2 * HALO
    start = jnp.full((1,), SUB - HALO, jnp.int32)
    edge = pltpu.VMEM((levels, SUB, ny), F32)
    (layers,) = call(
        layers_kernel, [(NS, nx, ny)], [state], "layers", scratch=[pltpu.SemaphoreType.DMA(())], hbm=(0,)
    )
    partner = lax.ppermute(layers, "comp", [(i, i ^ 1) for i in range(lax.axis_size("comp"))])
    x0, x1 = call(
        edges_kernel,
        [(levels, SUB, ny)] * 2,
        [state, conduct],
        "edges",
        scratch=[edge] * 4 + [pltpu.SemaphoreType.DMA((4,))],
        hbm=(0, 1),
    )
    x0, x1 = swap(x0, "gx", 0), swap(x1, "gx", 1)
    ext = (levels + 2, tiles + 1, nx + 2 * SUB, LANES)
    ext_s = (NS, tiles, nx + 2 * SUB, LANES)
    table, weights = plant_table.T, layer_weights.transpose(2, 0, 1)
    ext_u, ext_k, prof = call(
        own_kernel,
        [ext, ext, (PROFILES, nx, ny)],
        [table, weights, state, conduct, plant_type],
        "own",
        scratch=[
            pltpu.SMEM(table.shape, F32),
            pltpu.SMEM(weights.shape, F32),
            pltpu.VMEM(state.shape, F32),
            pltpu.VMEM(state.shape, F32),
            pltpu.VMEM(plant_type.shape, jnp.int32),
            pltpu.SemaphoreType.DMA((3,)),
            pltpu.SemaphoreType.DMA((3, 2)),
        ],
        hbm=(0, 1, 2, 3, 4),
        limit=4,
    )
    flux, src, s0, s1 = call(
        source_kernel,
        [(1, nx, ny), (NS, nx, ny)] + [(NS // 2, SUB, ny)] * 2,
        [remap_rows, partner, remap_weights, prof, surface_source],
        "source",
        scratch=[pltpu.VMEM((NS, nx, ny), F32)],
        smem=(0,),
    )
    s0, s1 = swap(s0, "gx", 0), swap(s1, "gx", 1)
    ext_u, ext_k, ext_s, y0, y1 = call(
        columns_kernel,
        [ext, ext, ext_s] + [(3, window, LANES)] * 2,
        [start, ext_u, ext_k, src, x0, x1, s0, s1],
        "columns",
        smem=(0,),
        alias={1: 0, 2: 1},
    )
    y0, y1 = swap(y0, "gy", 0), swap(y1, "gy", 1)
    coef = pltpu.VMEM((levels,) + ext[1:], F32)
    ext_u, r, p1, p2, moments, flux = call(
        chain_kernel,
        [ext] * 4 + [(SUB, LANES), (1, nx, ny)],
        [start, storage, ext_u, ext_k, ext_s, y0, y1, flux],
        "chain",
        scratch=[pltpu.VMEM((levels + 1,) + ext[1:], F32)]
        + [coef] * 4
        + [pltpu.VMEM((2, nx + 2 * SUB, LANES), F32), pltpu.SemaphoreType.DMA(())],
        hbm_outs=(5,),
        smem=(0, 1),
        limit=16,
        alias={2: 0},
    )
    (moments,) = call(add_kernel, [(SUB, LANES)], everyone(moments, "gx"), "add")
    parts = everyone(moments, "gy")
    (new_state,) = call(
        update_kernel,
        [state.shape],
        parts + [ext_u, r, p1, p2],
        "update",
        scratch=[pltpu.VMEM(state.shape, F32), pltpu.SemaphoreType.DMA((3,))],
        hbm_outs=(0,),
    )
    return new_state, flux


def solution(mesh):
    in_specs = (
        P("comp", None, "gx", "gy"),
        P("comp", None, "gx", "gy"),
        P("comp"),
        P("comp", "gx", "gy"),
        P("comp", "gx", "gy"),
        P(),
        P(),
        P("comp", "gx"),
        P("comp", "gy", None),
    )
    out_specs = (P("comp", None, "gx", "gy"), P("comp", "gx", "gy"))
    return jax.shard_map(body, mesh=mesh, in_specs=in_specs, out_specs=out_specs, check_vma=False)
```

time: 79.7 us -> 47.8 us (0.60)
  Pallas kernels: 39.3 us -> 16.8 us
  blocking collectives: 19.2 us -> 0 us
  starting transfers between devices: 11 us -> 22.1 us
  local copies, waits for them, and re-layouts: 4.38 us -> 0.01 us
  waiting for transfers between devices: 3.27 us -> 7.26 us
    pallas_call x5 -> x8, Pallas kernels: 39.3 us -> 16.8 us  [call(): pl.pallas_call(kernel, out_shape=[jax.ShapeDtypeStruct(s, F32) if i in hb...]
    all_to_all x1 -> x0, blocking collectives: 19.2 us -> none  [body(): gathered = lax.all_to_all(moments, ('gx', 'gy'), 0, 0)]
    ppermute x1 -> x7, starting transfers between devices: 2.57 us -> 15.4 us  [the longest x6 12.8 us: everyone(): lax.ppermute(value, axis, [(i, i ^ d) for i in range(n)])]
    unnamed x20 -> x6, local copies, waits for them, and re-layouts: 3.44 us -> 0.01 us
    ppermute x1 -> x7, waiting for transfers between devices: 2.97 us -> 5.96 us  [the longest x6 4.67 us: everyone(): lax.ppermute(value, axis, [(i, i ^ d) for i in range(n)])]
    ppermute x6, starting transfers between devices: 8.39 us -> 6.66 us  [swap(): return lax.ppermute(value, axis, pairing(lax.axis_size(axis), which))]
    ppermute x6, waiting for transfers between devices: 0.3 us -> 1.3 us  [swap(): return lax.ppermute(value, axis, pairing(lax.axis_size(axis), which))]
    slice x1 -> x0, local copies, waits for them, and re-layouts: 0.94 us -> none  [body(): field[:NS]]
  transfers between devices with their start and end apart: 7 -> 13, of which waited for: 2 -> 6; matrix products, arithmetic and copies ran while one was open for 3% -> 0% of each run, Pallas kernels for 4% -> 9%
where the time goes in v2:
time: 47.8 us; the launch traced here: 47.5 us
  starting transfers between devices  22.1 us (46%)
  Pallas kernels  16.8 us (35%)
  waiting for transfers between devices  7.26 us (15%)
  between operations  1.39 us (3%)
    pallas_call x8, Pallas kernels, call(): pl.pallas_call(kernel, out_shape=[jax.ShapeDtypeStruct(s, F32) if i in hb...  16.8 us
    ppermute x6, starting transfers between devices, everyone(): lax.ppermute(value, axis, [(i, i ^ d) for i in range(n)])  12.8 us
    ppermute x6, starting transfers between devices, swap(): return lax.ppermute(value, axis, pairing(lax.axis_size(axis), which))  6.66 us
    ppermute x6, waiting for transfers between devices, everyone(): lax.ppermute(value, axis, [(i, i ^ d) for i in range(n)])  4.67 us
    ppermute x1, starting transfers between devices, body(): lax.ppermute(layers, 'comp', [(i, i ^ 1) for i in range(lax.axis_size('co...  2.59 us
    ppermute x6, waiting for transfers between devices, swap(): return lax.ppermute(value, axis, pairing(lax.axis_size(axis), which))  1.3 us
    ppermute x1, waiting for transfers between devices, body(): lax.ppermute(layers, 'comp', [(i, i ^ 1) for i in range(lax.axis_size('co...  1.29 us
  transfers between devices with their start and end apart: 13, of which 6 were waited for; matrix products, arithmetic and copies ran while one was open for 0% of the time, Pallas kernels for 9%

profile of v2, /device:TPU:0, one launch (start us, length us, event | category | flops | bytes accessed | tf_op | source)
XLA Modules:
  0.0 47.5 jit_solution(15407827113856319624)
XLA Ops:
  0.7 1.5 %edges.1 = (f32[30,8,256]{2,1,0:T(8,128)S(1)}, f32[30,8,256]{2,1,0:T(8,128)S(1)}) custom-call(f32[1,30,32,256]{3,2,1,0:T(8,128)} %u_hbm.5, f32[1,30,32,256]{3,2,1,0:T(8,128)} %k_hbm.3), custom_call_target="tpu_custom_call" | custom-call | tf_op jit(solution)/shard_map/edges/pallas_call | solution.py:57
  2.1 0.6 %collective-permute-start.1 = (f32[30,8,256]{2,1,0:T(8,128)S(1)}, f32[30,8,256]{2,1,0:T(8,128)S(1)}, u32[]{:S(2)}, u32[]{:S(2)}) collective-permute-start(f32[30,8,256]{2,1,0:T(8,128)S(1)} %get-tuple-element.26), channel_id=1, source_target_pairs={{0,4},{4,0},{8,12},{12,8},{1,5},{5,1},{9,13},{13,9},{2,6},{6,2},{1... | collective-permute-start | bytes 737288 | tf_op jit(solution)/shard_map/ppermute | solution.py:31
  2.7 0.7 %collective-permute-start.2 = (f32[30,8,256]{2,1,0:T(8,128)S(1)}, f32[30,8,256]{2,1,0:T(8,128)S(1)}, u32[]{:S(2)}, u32[]{:S(2)}) collective-permute-start(f32[30,8,256]{2,1,0:T(8,128)S(1)} %get-tuple-element.27), channel_id=1, source_target_pairs={{0,0},{4,8},{8,4},{12,12},{1,1},{5,9},{9,5},{13,13},{2,2},{6,10},{... | collective-permute-start | bytes 737288 | tf_op jit(solution)/shard_map/ppermute | solution.py:31
  3.4 0.9 %layers.1 = f32[6,32,256]{2,1,0:T(8,128)S(1)} custom-call(f32[1,30,32,256]{3,2,1,0:T(8,128)} %u_hbm.5), custom_call_target="tpu_custom_call" | custom-call | tf_op jit(solution)/shard_map/layers/pallas_call | solution.py:57
  4.3 2.6 %collective-permute-start = (f32[6,32,256]{2,1,0:T(8,128)S(1)}, f32[6,32,256]{2,1,0:T(8,128)S(1)}, u32[]{:S(2)}, u32[]{:S(2)}) collective-permute-start(f32[6,32,256]{2,1,0:T(8,128)S(1)} %layers.1), channel_id=1, source_target_pairs={{0,16},{16,0},{1,17},{17,1},{2,18},{18,2},{3,19},{19,3},{4,20},{20... | collective-permute-start | bytes 589832 | tf_op jit(solution)/shard_map/ppermute | solution.py:504
  6.9 2.4 %own.1 = (f32[32,3,48,128]{3,2,1,0:T(8,128)S(1)}, f32[32,3,48,128]{3,2,1,0:T(8,128)S(1)}, f32[15,32,256]{2,1,0:T(8,128)S(1)}) custom-call(f32[2,16]{1,0:T(2,128)} %bitcast.3, f32[6,2,16]{2,1,0:T(2,128)} %bitcast.2, f32[1,30,32,256]{3,2,1,0:T(8,128)} %u_hbm.5, f32[1,30,32,256]{3,2,1,0:T(8,128)} %k_hbm.3, s32[1,32,256]{2,1,0:T(8,128)} %kind_hbm.1), custom_call_target="tpu_custom_call" | custom-call | tf_op jit(solution)/shard_map/own/pallas_call | solution.py:57
  9.3 1.3 %collective-permute-done.part_ref = f32[6,32,256]{2,1,0:T(8,128)S(1)} collective-permute-done((f32[6,32,256]{2,1,0:T(8,128)S(1)}, f32[6,32,256]{2,1,0:T(8,128)S(1)}, u32[]{:S(2)}, u32[]{:S(2)}) %collective-permute-start) | collective-permute-done | bytes 196640 | tf_op jit(solution)/shard_map/ppermute | solution.py:504
  10.6 0.9 %source.1 = (f32[1,32,256]{2,1,0:T(8,128)S(1)}, f32[6,32,256]{2,1,0:T(8,128)S(1)}, f32[3,8,256]{2,1,0:T(8,128)S(1)}, f32[3,8,256]{2,1,0:T(8,128)S(1)}) custom-call(s32[1,32]{1,0:T(1,128)S(1)} %copy-done.2, f32[6,32,256]{2,1,0:T(8,128)S(1)} %collective-permute-done.part_ref, f32[1,256,128]{2,1,0:T(8,128)S(1)} %copy-done, ...), custom_call_target="tpu_custom_call" | custom-call | tf_op jit(solution)/shard_map/source/pallas_call | solution.py:57
  11.5 2.3 %collective-permute-start.3 = (f32[3,8,256]{2,1,0:T(8,128)S(1)}, f32[3,8,256]{2,1,0:T(8,128)S(1)}, u32[]{:S(2)}, u32[]{:S(2)}) collective-permute-start(f32[3,8,256]{2,1,0:T(8,128)S(1)} %get-tuple-element.28), channel_id=1, source_target_pairs={{0,4},{4,0},{8,12},{12,8},{1,5},{5,1},{9,13},{13,9},{2,6},{6,2},{1... | collective-permute-start | bytes 73736 | tf_op jit(solution)/shard_map/ppermute | solution.py:31
  13.7 0.7 %collective-permute-start.4 = (f32[3,8,256]{2,1,0:T(8,128)S(1)}, f32[3,8,256]{2,1,0:T(8,128)S(1)}, u32[]{:S(2)}, u32[]{:S(2)}) collective-permute-start(f32[3,8,256]{2,1,0:T(8,128)S(1)} %get-tuple-element.29), channel_id=1, source_target_pairs={{0,0},{4,8},{8,4},{12,12},{1,1},{5,9},{9,5},{13,13},{2,2},{6,10},{... | collective-permute-start | bytes 73736 | tf_op jit(solution)/shard_map/ppermute | solution.py:31
  14.4 0.2 collective-permute-done.3.s0
  14.6 0.0 collective-permute-done.4.s1
  14.6 0.0 collective-permute-done.1.x0
  14.6 0.0 collective-permute-done.2.x1
  14.6 1.1 %columns.1 = (f32[32,3,48,128]{3,2,1,0:T(8,128)S(1)}, f32[32,3,48,128]{3,2,1,0:T(8,128)S(1)}, f32[6,2,48,128]{3,2,1,0:T(8,128)S(1)}, f32[3,40,128]{2,1,0:T(8,128)S(1)}, f32[3,40,128]{2,1,0:T(8,128)S(1)}) custom-call(s32[1]{0:T(128)} %constant.0.clone.1.start, ...), custom_call_target="tpu_custom_call", output_to_operand_aliasing={{0}: (1, {}), {1}: (2, {})} | custom-call | tf_op jit(solution)/shard_map/columns/pallas_call | solution.py:57
  15.7 1.9 %collective-permute-start.5 = (f32[3,40,128]{2,1,0:T(8,128)S(1)}, f32[3,40,128]{2,1,0:T(8,128)S(1)}, u32[]{:S(2)}, u32[]{:S(2)}) collective-permute-start(f32[3,40,128]{2,1,0:T(8,128)S(1)} %get-tuple-element.33), channel_id=1, source_target_pairs={{0,1},{1,0},{2,3},{3,2},{4,5},{5,4},{6,7},{7,6},{8,9},{9,8},{10,11... | collective-permute-start | bytes 184328 | tf_op jit(solution)/shard_map/ppermute | solution.py:31
  17.6 0.7 %collective-permute-start.6 = (f32[3,40,128]{2,1,0:T(8,128)S(1)}, f32[3,40,128]{2,1,0:T(8,128)S(1)}, u32[]{:S(2)}, u32[]{:S(2)}) collective-permute-start(f32[3,40,128]{2,1,0:T(8,128)S(1)} %get-tuple-element.34), channel_id=1, source_target_pairs={{0,0},{1,2},{2,1},{3,3},{4,4},{5,6},{6,5},{7,7},{8,8},{9,10},{10,9... | collective-permute-start | bytes 184328 | tf_op jit(solution)/shard_map/ppermute | solution.py:31
  18.9 1.1 %collective-permute-done.5.y0 = f32[3,40,128]{2,1,0:T(8,128)S(1)} collective-permute-done((f32[3,40,128]{2,1,0:T(8,128)S(1)}, f32[3,40,128]{2,1,0:T(8,128)S(1)}, u32[]{:S(2)}, u32[]{:S(2)}) %collective-permute-start.5) | collective-permute-done | bytes 61472 | tf_op jit(solution)/shard_map/ppermute | solution.py:31
  20.0 0.0 collective-permute-done.6.y1
  20.0 8.9 %chain.1 = (f32[32,3,48,128]{3,2,1,0:T(8,128)S(1)}, f32[32,3,48,128]{3,2,1,0:T(8,128)S(1)}, f32[32,3,48,128]{3,2,1,0:T(8,128)S(1)}, f32[32,3,48,128]{3,2,1,0:T(8...) custom-call(s32[1]{0:T(128)} %constant.0.clone.1.start, ...), custom_call_target="tpu_custom_call", output_to_operand_aliasing={{0}: (2, {})} | custom-call | tf_op jit(solution)/shard_map/chain/pallas_call | solution.py:57
  28.9 0.5 %collective-permute-start.9 = (f32[8,128]{1,0:T(8,128)S(1)}, f32[8,128]{1,0:T(8,128)S(1)}, u32[]{:S(2)}, u32[]{:S(2)}) collective-permute-start(f32[8,128]{1,0:T(8,128)S(1)} %get-tuple-element.36.refs_0_), channel_id=1, source_target_pairs={{0,12},{4,8},{8,4},{12,0},{1,13},{5,9},{9,5},{13,1},{2,14},{6,10},... | collective-permute-start | bytes 12296 | tf_op jit(solution)/shard_map/ppermute | solution.py:36
  29.4 5.3 %collective-permute-start.8 = (f32[8,128]{1,0:T(8,128)S(1)}, f32[8,128]{1,0:T(8,128)S(1)}, u32[]{:S(2)}, u32[]{:S(2)}) collective-permute-start(f32[8,128]{1,0:T(8,128)S(1)} %get-tuple-element.36.refs_0_), channel_id=1, source_target_pairs={{0,8},{4,12},{8,0},{12,4},{1,9},{5,13},{9,1},{13,5},{2,10},{6,14},... | collective-permute-start | bytes 12296 | tf_op jit(solution)/shard_map/ppermute | solution.py:36
  34.8 0.0 collective-permute-start.7
  34.8 0.0 collective-permute-done.9.refs_3_
  34.8 1.5 %collective-permute-done.8.refs_2_ = f32[8,128]{1,0:T(8,128)S(1)} collective-permute-done((f32[8,128]{1,0:T(8,128)S(1)}, f32[8,128]{1,0:T(8,128)S(1)}, u32[]{:S(2)}, u32[]{:S(2)}) %collective-permute-start.8) | collective-permute-done | bytes 4128 | tf_op jit(solution)/shard_map/ppermute | solution.py:36
  36.3 0.0 collective-permute-done.7.refs_1_
  36.4 3.9 %collective-permute-start.12 = (f32[8,128]{1,0:T(8,128)S(1)}, f32[8,128]{1,0:T(8,128)S(1)}, u32[]{:S(2)}, u32[]{:S(2)}) collective-permute-start(f32[8,128]{1,0:T(8,128)S(1)} %add.1.refs_0_), channel_id=1, source_target_pairs={{0,3},{1,2},{2,1},{3,0},{4,7},{5,6},{6,5},{7,4},{8,11},{9,10},{10,... | collective-permute-start | bytes 12296 | tf_op jit(solution)/shard_map/ppermute | solution.py:36
  40.3 2.5 %collective-permute-start.11 = (f32[8,128]{1,0:T(8,128)S(1)}, f32[8,128]{1,0:T(8,128)S(1)}, u32[]{:S(2)}, u32[]{:S(2)}) collective-permute-start(f32[8,128]{1,0:T(8,128)S(1)} %add.1.refs_0_), channel_id=1, source_target_pairs={{0,2},{1,3},{2,0},{3,1},{4,6},{5,7},{6,4},{7,5},{8,10},{9,11},{10,... | collective-permute-start | bytes 12296 | tf_op jit(solution)/shard_map/ppermute | solution.py:36
  42.8 0.5 %collective-permute-start.10 = (f32[8,128]{1,0:T(8,128)S(1)}, f32[8,128]{1,0:T(8,128)S(1)}, u32[]{:S(2)}, u32[]{:S(2)}) collective-permute-start(f32[8,128]{1,0:T(8,128)S(1)} %add.1.refs_0_), channel_id=1, source_target_pairs={{0,1},{1,0},{2,3},{3,2},{4,5},{5,4},{6,7},{7,6},{8,9},{9,8},{10,11... | collective-permute-start | bytes 12296 | tf_op jit(solution)/shard_map/ppermute | solution.py:36
  43.3 1.5 %collective-permute-done.11.refs_2_ = f32[8,128]{1,0:T(8,128)S(1)} collective-permute-done((f32[8,128]{1,0:T(8,128)S(1)}, f32[8,128]{1,0:T(8,128)S(1)}, u32[]{:S(2)}, u32[]{:S(2)}) %collective-permute-start.11) | collective-permute-done | bytes 4128 | tf_op jit(solution)/shard_map/ppermute | solution.py:36
  44.8 1.6 %collective-permute-done.10.refs_1_ = f32[8,128]{1,0:T(8,128)S(1)} collective-permute-done((f32[8,128]{1,0:T(8,128)S(1)}, f32[8,128]{1,0:T(8,128)S(1)}, u32[]{:S(2)}, u32[]{:S(2)}) %collective-permute-start.10) | collective-permute-done | bytes 4128 | tf_op jit(solution)/shard_map/ppermute | solution.py:36
  46.4 1.1 %update.1 = f32[1,30,32,256]{3,2,1,0:T(8,128)} custom-call(f32[8,128]{1,0:T(8,128)S(1)} %add.1.refs_0_, f32[8,128]{1,0:T(8,128)S(1)} %collective-permute-done.10.refs_1_, f32[8,128]{1,0:T(8,128)S(1)} %collective-permute-done.11.refs_2_, f32[8,128]{1,0:T(8,128)S(1)} %collective-permute-done.12.refs_3_, f32[32,3,48,128]{3,2,1,0:T(8,128)S(1)} %get-tuple-element.37.refs_4_, ...), custom_call_target="tpu_custom_call" | custom-call | tf_op jit(solution)/shard_map/update/pallas_call | solution.py:57
  (8 shorter events, 0.0 us)
Async XLA Ops:
  0.6 9.9 %copy-start = (f32[1,256,128]{2,1,0:T(8,128)S(1)}, f32[1,256,128]{2,1,0:T(8,128)}, u32[]{:S(2)}) copy-start(f32[1,256,128]{2,1,0:T(8,128)} %w_ref.1) | copy-start | bytes 393220
  0.6 9.9 %copy-start.2 = (s32[1,32]{1,0:T(1,128)S(1)}, s32[1,32]{1,0:T(1,128)}, u32[]{:S(2)}) copy-start(s32[1,32]{1,0:T(1,128)} %rows_ref.1) | copy-start | bytes 388
  0.7 9.9 %copy-start.1 = (f32[1,32,256]{2,1,0:T(8,128)S(1)}, f32[1,32,256]{2,1,0:T(8,128)}, u32[]{:S(2)}) copy-start(f32[1,32,256]{2,1,0:T(8,128)} %surf_ref.1) | copy-start | bytes 98308
  2.1 12.5 %collective-permute-start.1 = (f32[30,8,256]{2,1,0:T(8,128)S(1)}, f32[30,8,256]{2,1,0:T(8,128)S(1)}, u32[]{:S(2)}, u32[]{:S(2)}) collective-permute-start(f32[30,8,256]{2,1,0:T(8,128)S(1)} %get-tuple-element.26), channel_id=1, source_target_pairs={{0,4},{4,0},{8,12},{12,8},{1,5},{5,1},{9,13},{13,9},{2,6},{6,2},{1... | collective-permute-start | bytes 737288 | tf_op jit(solution)/shard_map/ppermute | solution.py:31
  2.7 11.9 %collective-permute-start.2 = (f32[30,8,256]{2,1,0:T(8,128)S(1)}, f32[30,8,256]{2,1,0:T(8,128)S(1)}, u32[]{:S(2)}, u32[]{:S(2)}) collective-permute-start(f32[30,8,256]{2,1,0:T(8,128)S(1)} %get-tuple-element.27), channel_id=1, source_target_pairs={{0,0},{4,8},{8,4},{12,12},{1,1},{5,9},{9,5},{13,13},{2,2},{6,10},{... | collective-permute-start | bytes 737288 | tf_op jit(solution)/shard_map/ppermute | solution.py:31
  4.3 6.2 %collective-permute-start = (f32[6,32,256]{2,1,0:T(8,128)S(1)}, f32[6,32,256]{2,1,0:T(8,128)S(1)}, u32[]{:S(2)}, u32[]{:S(2)}) collective-permute-start(f32[6,32,256]{2,1,0:T(8,128)S(1)} %layers.1), channel_id=1, source_target_pairs={{0,16},{16,0},{1,17},{17,1},{2,18},{18,2},{3,19},{19,3},{4,20},{20... | collective-permute-start | bytes 589832 | tf_op jit(solution)/shard_map/ppermute | solution.py:504
  11.5 3.1 %collective-permute-start.3 = (f32[3,8,256]{2,1,0:T(8,128)S(1)}, f32[3,8,256]{2,1,0:T(8,128)S(1)}, u32[]{:S(2)}, u32[]{:S(2)}) collective-permute-start(f32[3,8,256]{2,1,0:T(8,128)S(1)} %get-tuple-element.28), channel_id=1, source_target_pairs={{0,4},{4,0},{8,12},{12,8},{1,5},{5,1},{9,13},{13,9},{2,6},{6,2},{1... | collective-permute-start | bytes 73736 | tf_op jit(solution)/shard_map/ppermute | solution.py:31
  13.7 0.9 %collective-permute-start.4 = (f32[3,8,256]{2,1,0:T(8,128)S(1)}, f32[3,8,256]{2,1,0:T(8,128)S(1)}, u32[]{:S(2)}, u32[]{:S(2)}) collective-permute-start(f32[3,8,256]{2,1,0:T(8,128)S(1)} %get-tuple-element.29), channel_id=1, source_target_pairs={{0,0},{4,8},{8,4},{12,12},{1,1},{5,9},{9,5},{13,13},{2,2},{6,10},{... | collective-permute-start | bytes 73736 | tf_op jit(solution)/shard_map/ppermute | solution.py:31
  15.7 4.3 %collective-permute-start.5 = (f32[3,40,128]{2,1,0:T(8,128)S(1)}, f32[3,40,128]{2,1,0:T(8,128)S(1)}, u32[]{:S(2)}, u32[]{:S(2)}) collective-permute-start(f32[3,40,128]{2,1,0:T(8,128)S(1)} %get-tuple-element.33), channel_id=1, source_target_pairs={{0,1},{1,0},{2,3},{3,2},{4,5},{5,4},{6,7},{7,6},{8,9},{9,8},{10,11... | collective-permute-start | bytes 184328 | tf_op jit(solution)/shard_map/ppermute | solution.py:31
  17.6 2.4 %collective-permute-start.6 = (f32[3,40,128]{2,1,0:T(8,128)S(1)}, f32[3,40,128]{2,1,0:T(8,128)S(1)}, u32[]{:S(2)}, u32[]{:S(2)}) collective-permute-start(f32[3,40,128]{2,1,0:T(8,128)S(1)} %get-tuple-element.34), channel_id=1, source_target_pairs={{0,0},{1,2},{2,1},{3,3},{4,4},{5,6},{6,5},{7,7},{8,8},{9,10},{10,9... | collective-permute-start | bytes 184328 | tf_op jit(solution)/shard_map/ppermute | solution.py:31
  28.9 5.9 %collective-permute-start.9 = (f32[8,128]{1,0:T(8,128)S(1)}, f32[8,128]{1,0:T(8,128)S(1)}, u32[]{:S(2)}, u32[]{:S(2)}) collective-permute-start(f32[8,128]{1,0:T(8,128)S(1)} %get-tuple-element.36.refs_0_), channel_id=1, source_target_pairs={{0,12},{4,8},{8,4},{12,0},{1,13},{5,9},{9,5},{13,1},{2,14},{6,10},... | collective-permute-start | bytes 12296 | tf_op jit(solution)/shard_map/ppermute | solution.py:36
  29.4 6.9 %collective-permute-start.8 = (f32[8,128]{1,0:T(8,128)S(1)}, f32[8,128]{1,0:T(8,128)S(1)}, u32[]{:S(2)}, u32[]{:S(2)}) collective-permute-start(f32[8,128]{1,0:T(8,128)S(1)} %get-tuple-element.36.refs_0_), channel_id=1, source_target_pairs={{0,8},{4,12},{8,0},{12,4},{1,9},{5,13},{9,1},{13,5},{2,10},{6,14},... | collective-permute-start | bytes 12296 | tf_op jit(solution)/shard_map/ppermute | solution.py:36
  34.8 1.6 %collective-permute-start.7 = (f32[8,128]{1,0:T(8,128)S(1)}, f32[8,128]{1,0:T(8,128)S(1)}, u32[]{:S(2)}, u32[]{:S(2)}) collective-permute-start(f32[8,128]{1,0:T(8,128)S(1)} %get-tuple-element.36.refs_0_), channel_id=1, source_target_pairs={{0,4},{4,0},{8,12},{12,8},{1,5},{5,1},{9,13},{13,9},{2,6},{6,2},{1... | collective-permute-start | bytes 12296 | tf_op jit(solution)/shard_map/ppermute | solution.py:36
  36.4 6.9 %collective-permute-start.12 = (f32[8,128]{1,0:T(8,128)S(1)}, f32[8,128]{1,0:T(8,128)S(1)}, u32[]{:S(2)}, u32[]{:S(2)}) collective-permute-start(f32[8,128]{1,0:T(8,128)S(1)} %add.1.refs_0_), channel_id=1, source_target_pairs={{0,3},{1,2},{2,1},{3,0},{4,7},{5,6},{6,5},{7,4},{8,11},{9,10},{10,... | collective-permute-start | bytes 12296 | tf_op jit(solution)/shard_map/ppermute | solution.py:36
  40.3 4.5 %collective-permute-start.11 = (f32[8,128]{1,0:T(8,128)S(1)}, f32[8,128]{1,0:T(8,128)S(1)}, u32[]{:S(2)}, u32[]{:S(2)}) collective-permute-start(f32[8,128]{1,0:T(8,128)S(1)} %add.1.refs_0_), channel_id=1, source_target_pairs={{0,2},{1,3},{2,0},{3,1},{4,6},{5,7},{6,4},{7,5},{8,10},{9,11},{10,... | collective-permute-start | bytes 12296 | tf_op jit(solution)/shard_map/ppermute | solution.py:36
  42.8 3.6 %collective-permute-start.10 = (f32[8,128]{1,0:T(8,128)S(1)}, f32[8,128]{1,0:T(8,128)S(1)}, u32[]{:S(2)}, u32[]{:S(2)}) collective-permute-start(f32[8,128]{1,0:T(8,128)S(1)} %add.1.refs_0_), channel_id=1, source_target_pairs={{0,1},{1,0},{2,3},{3,2},{4,5},{5,4},{6,7},{7,6},{8,9},{9,8},{10,11... | collective-permute-start | bytes 12296 | tf_op jit(solution)/shard_map/ppermute | solution.py:36

commit v3 on v2

--- a/solution.py
+++ b/solution.py
@@ -19,16 +19,23 @@
 MIB = 1 << 20
 
 
-def pairing(count, which):
-    pairs = []
-    for i in range(count):
-        partner = i ^ 1 if which == 0 else (i + 1 if i % 2 else i - 1)
-        pairs.append((i, partner if 0 <= partner < count else i))
-    return pairs
-
-
 def swap(value, axis, which):
-    return lax.ppermute(value, axis, pairing(lax.axis_size(axis), which))
+    nx, ny = lax.axis_size("gx"), lax.axis_size("gy")
+
+    def partner(i, count):
+        p = i ^ 1 if which == 0 else (i + 1 if i % 2 else i - 1)
+        return p if 0 <= p < count else None
+
+    def target(i, j):
+        p = partner(i, nx) if axis == "gx" else partner(j, ny)
+        if axis == "gx":
+            i, j = (p, j) if p is not None else (i, j ^ 1 if ny % 2 == 0 else j)
+        else:
+            i, j = (i, p) if p is not None else (i ^ 1 if nx % 2 == 0 else i, j)
+        return i * ny + j
+
+    pairs = [(i * ny + j, target(i, j)) for i in range(nx) for j in range(ny)]
+    return lax.ppermute(value, ("gx", "gy"), pairs)
 
 
 def everyone(value, axis):
@@ -45,7 +52,7 @@
 HBM_SPEC = pl.BlockSpec(memory_space=pltpu.HBM)
 
 
-def call(kernel, outs, ins, name, scratch=(), smem=(), hbm=(), hbm_outs=(), limit=2, alias=None):
+def call(kernel, outs, ins, scratch=(), smem=(), hbm=(), hbm_outs=(), limit=2, alias=None):
     def spec(i):
         return SMEM_SPEC if i in smem else HBM_SPEC if i in hbm else VMEM_SPEC
 
@@ -61,7 +68,6 @@
         out_specs=[HBM_SPEC if i in hbm_outs else VMEM_SPEC for i in range(len(outs))],
         scratch_shapes=list(scratch),
         input_output_aliases=alias or {},
-        name=name,
         compiler_params=pltpu.CompilerParams(vmem_limit_bytes=limit * MIB),
     )(*[place(i, v) for i, v in enumerate(ins)])
 
@@ -76,7 +82,7 @@
     copy.wait()
 
 
-def edges_kernel(u_hbm, k_hbm, out0, out1, low_u, low_k, high_u, high_k, sems):
+def edges_kernel(after, u_hbm, k_hbm, out0, out1, low_u, low_k, high_u, high_k, sems):
     _, levels, rows, cols = u_hbm.shape
     copies = [
         pltpu.make_async_copy(u_hbm.at[0, :, pl.ds(0, SUB)], low_u, sems.at[0]),
@@ -97,37 +103,17 @@
         out1[l] = jnp.where(odd, high, low)
 
 
-def own_kernel(
-    table_hbm, lw_hbm, u_hbm, k_hbm, kind_hbm, ext_u, ext_k, prof, table, lw, u_ref, k_ref, kind_ref, sems, field_sems
-):
-    _, levels, nx, ny = u_ref.shape
-    tiles = ny // LANES
+def profile_kernel(table_hbm, lw_hbm, kind_hbm, layers, prof, table, lw, kind_ref, sems):
+    nx = layers.shape[1]
     comp = lax.axis_index("comp")
-    small = [
+    copies = [
         pltpu.make_async_copy(table_hbm, table, sems.at[0]),
         pltpu.make_async_copy(lw_hbm, lw, sems.at[1]),
         pltpu.make_async_copy(kind_hbm, kind_ref, sems.at[2]),
     ]
-    for copy in small:
+    for copy in copies:
         copy.start()
-    pieces = field_sems.shape[0]
-    bounds = [levels * i // pieces for i in range(pieces + 1)]
-    fields = []
-    for i in range(pieces):
-        part = pl.ds(bounds[i], bounds[i + 1] - bounds[i])
-        pair = [
-            pltpu.make_async_copy(u_hbm.at[0, part], u_ref.at[0, part], field_sems.at[i, 0]),
-            pltpu.make_async_copy(k_hbm.at[0, part], k_ref.at[0, part], field_sems.at[i, 1]),
-        ]
-        for copy in pair:
-            copy.start()
-        fields.append(pair)
-    blank = jnp.zeros((nx + 2 * SUB, LANES), F32)
-    for t in range(tiles + 1):
-        for ext in (ext_u, ext_k):
-            ext[0, t] = blank
-            ext[levels + 1, t] = blank
-    for copy in small:
+    for copy in copies:
         copy.wait()
     for x in range(0, nx, SUB):
         rows = slice(x, x + SUB)
@@ -139,26 +125,71 @@
         for p in range(1, PLANTS):
             here = kinds == p
             found = [jnp.where(here, t(p), f) for t, f in zip(tables, found)]
-        for i, f in enumerate(found):
+        force = found[0] * layers[0, rows]
+        for l in range(1, NS):
+            force = force + found[l] * layers[l, rows]
+        for i, f in enumerate(found + [force]):
             prof[i, rows] = f
 
-    for i in range(pieces):
-        for copy in fields[i]:
-            copy.wait()
-
-        def level(l, _):
-            for t in range(tiles):
-                u = u_ref[0, l, :, t * LANES : (t + 1) * LANES]
-                k = k_ref[0, l, :, t * LANES : (t + 1) * LANES]
-                ext_u[l + 1, t, SUB : SUB + nx] = u
-                ext_k[l + 1, t, SUB : SUB + nx] = k * (0.5 + 0.25 * jnp.tanh(u))
-            return 0
-
-        lax.fori_loop(bounds[i], bounds[i + 1], level, 0, unroll=2)
-    force = prof[0] * u_ref[0, 0]
-    for l in range(1, NS):
-        force = force + prof[l] * u_ref[0, l]
-    prof[2 * NS + 2] = force
+
+def received_rows(count):
+    upper = iota((SUB, LANES), 0) < HALO
+    gx = lax.axis_index("gx")
+    odd = gx % 2 == 1
+    keep_low = ~upper & (gx > 0)
+    keep_high = upper & (gx < count - 1)
+
+    def halves(first, second, j, cols):
+        a, b = first[j, :, cols], second[j, :, cols]
+        high, low = jnp.where(odd, b, a), jnp.where(odd, a, b)
+        lows = jnp.where(keep_low, half_swap(low), 0.0), jnp.where(keep_low, low, 0.0)
+        highs = jnp.where(keep_high, high, 0.0), jnp.where(keep_high, half_swap(high), 0.0)
+        return lows, highs
+
+    return halves
+
+
+def pack_columns(ext, plane, count, base, window, tiles, outs, slot):
+    group = iota((window, LANES), 1) // HALO
+    first_high = lax.axis_index("gy") % 2 == 0
+    tile0 = jnp.where(first_high, tiles - 1, 0)
+    move0 = jnp.where(first_high, HALO, 0)
+    for out, tile, move in ((outs[0], tile0, move0), (outs[1], tiles - 1 - tile0, HALO - move0)):
+        packed = jnp.zeros((window, LANES), F32)
+        for l in range(count):
+            v = ext[l + plane, tile, pl.ds(base, window)]
+            v = pltpu.roll(v, (HALO * l + move) % LANES, 1)
+            packed = jnp.where(group == l, v, packed)
+        out[slot] = packed
+
+
+def fields_kernel(start, after, u_ref, k_ref, x0, x1, ext_u, ext_k, out0, out1):
+    _, levels, nx, ny = u_ref.shape
+    tiles = ny // LANES
+    blank = jnp.zeros((nx + 2 * SUB, LANES), F32)
+    for t in range(tiles + 1):
+        for ext in (ext_u, ext_k):
+            ext[0, t] = blank
+            ext[levels + 1, t] = blank
+    halves = received_rows(lax.axis_size("gx"))
+
+    def level(l, _):
+        for t in range(tiles):
+            cols = slice(t * LANES, (t + 1) * LANES)
+            lows, highs = halves(x0, x1, l, cols)
+            own = u_ref[0, l, :, cols], k_ref[0, l, :, cols]
+            for rows, (u, k) in (
+                (slice(0, SUB), lows),
+                (slice(SUB, SUB + nx), own),
+                (slice(SUB + nx, 2 * SUB + nx), highs),
+            ):
+                ext_u[l + 1, t, rows] = u
+                ext_k[l + 1, t, rows] = k * (0.5 + 0.25 * jnp.tanh(u))
+        return 0
+
+    lax.fori_loop(0, levels, level, 0, unroll=2)
+    for slot, ext in enumerate((ext_u, ext_k)):
+        pack_columns(ext, 1, levels, start[0], nx + 2 * HALO, tiles, (out0, out1), slot)
 
 
 def split(v):
@@ -211,32 +242,10 @@
         out1[j] = jnp.where(odd, high, low)
 
 
-def columns_kernel(start, ext_u_in, ext_k_in, s_ref, x0, x1, s0, s1, ext_u, ext_k, ext_s, out0, out1):
-    levels = ext_u.shape[0] - 2
+def columns_kernel(start, s_ref, s0, s1, in0, in1, ext_s, out0, out1):
     nx, ny = s_ref.shape[1:]
     tiles = ny // LANES
-    upper = iota((SUB, LANES), 0) < HALO
-    gx, count = lax.axis_index("gx"), lax.axis_size("gx")
-    odd = gx % 2 == 1
-    keep_low = upper & (gx < 0) | ~upper & (gx > 0)
-    keep_high = upper & (gx < count - 1)
-
-    def halves(first, second, j, cols):
-        a, b = first[j, :, cols], second[j, :, cols]
-        high, low = jnp.where(odd, b, a), jnp.where(odd, a, b)
-        lows = jnp.where(keep_low, half_swap(low), 0.0), jnp.where(keep_low, low, 0.0)
-        highs = jnp.where(keep_high, high, 0.0), jnp.where(keep_high, half_swap(high), 0.0)
-        return lows, highs
-
-    def level(l, _):
-        for t in range(tiles):
-            lows, highs = halves(x0, x1, l, slice(t * LANES, (t + 1) * LANES))
-            for rows, (u, k) in ((slice(0, SUB), lows), (slice(SUB + nx, 2 * SUB + nx), highs)):
-                ext_u[l + 1, t, rows] = u
-                ext_k[l + 1, t, rows] = k * (0.5 + 0.25 * jnp.tanh(u))
-        return 0
-
-    lax.fori_loop(0, levels, level, 0, unroll=2)
+    halves = received_rows(lax.axis_size("gx"))
     for j in range(NS // 2):
         for t in range(tiles):
             cols = slice(t * LANES, (t + 1) * LANES)
@@ -245,29 +254,77 @@
                 ext_s[2 * j + i, t, :SUB] = lows[i]
                 ext_s[2 * j + i, t, SUB : SUB + nx] = s_ref[2 * j + i, :, cols]
                 ext_s[2 * j + i, t, SUB + nx :] = highs[i]
-
-    y_odd = lax.axis_index("gy") % 2
-    window = nx + 2 * HALO
-    group = iota((window, LANES), 1) // HALO
-    first_high = y_odd == 0
-    tile0 = jnp.where(first_high, tiles - 1, 0)
-    tile1 = tiles - 1 - tile0
-    move0 = jnp.where(first_high, HALO, 0)
-    move1 = HALO - move0
-    for f, (ext, base, n) in enumerate(((ext_u, 1, levels), (ext_k, 1, levels), (ext_s, 0, NS))):
-        for out, tile, move in ((out0, tile0, move0), (out1, tile1, move1)):
-            packed = jnp.zeros((window, LANES), F32)
-            for l in range(n):
-                v = ext[l + base, tile, pl.ds(start[0], window)]
-                v = pltpu.roll(v, (HALO * l + move) % LANES, 1)
-                packed = jnp.where(group == l, v, packed)
-            out[f] = packed
+    pack_columns(ext_s, 0, NS, start[0], nx + 2 * HALO, tiles, (out0, out1), 2)
+
+
+def coefficients_kernel(start, storage_ref, after, ext_u, ext_k, r, cz, cx, cy, cy_low, diag):
+    levels = ext_u.shape[0] - 2
+    tiles = ext_u.shape[1] - 1
+    nx = ext_u.shape[2] - 2 * SUB
+    gx, ngx = lax.axis_index("gx"), lax.axis_size("gx")
+    base = start[0]
+    shift = storage_ref[0] - CENTRE
+    chunks = (nx + 2 * HALO) // SUB
+    few = next(n for n in (3, 2, 1) if levels % n == 0)
+    own = range(tiles)
+    lane, row = iota((SUB, LANES), 1), iota((SUB, LANES), 0)
+    at_end, at_start = lane == LANES - 1, lane == 0
+    low_rows = (row >= HALO) | (gx > 0)
+    high_rows = (row < HALO) | (gx < ngx - 1)
+
+    def beside(vs):
+        up = [pltpu.roll(v, LANES - 1, 1) for v in vs] + [0.0]
+        down = [0.0] + [pltpu.roll(v, 1, 1) for v in vs]
+        ups = [jnp.where(at_end, up[t + 1], up[t]) for t in own]
+        downs = [jnp.where(at_start, down[t], down[t + 1]) for t in own]
+        return ups, downs
+
+    def prepare(j, _):
+        first = j * few
+        for c in range(chunks):
+            at = base + SUB * c
+            rows = pl.ds(at, SUB)
+
+            def load(ext, plane, dx=0):
+                return [ext[first + plane, t, pl.ds(at + dx, SUB)] for t in own]
+
+            k_last, u_last = load(ext_k, 0), load(ext_u, 0)
+            k, u = load(ext_k, 1), load(ext_u, 1)
+            below = [k[t] + k_last[t] for t in own]
+            for i in range(few):
+                l = first + i
+                k_next, u_next = load(ext_k, i + 2), load(ext_u, i + 2)
+                ks = [load(ext_k, i + 1, dx) for dx in (1, -1)]
+                us = [load(ext_u, i + 1, dx) for dx in (1, -1)]
+                yk, yu = beside(k), beside(u)
+                above = [k[t] + k_next[t] for t in own]
+                for t in own:
+                    y_up, y_down = yk[0][t] + k[t], yk[1][t] + k[t]
+                    x_up, x_down = ks[0][t] + k[t], ks[1][t] + k[t]
+                    total = ((y_up + y_down) + (x_up + x_down)) + (above[t] + below[t])
+                    flow = (y_up * yu[0][t] + y_down * yu[1][t]) + (x_up * us[0][t] + x_down * us[1][t])
+                    flow = flow + (above[t] * u_next[t] + below[t] * u_last[t])
+                    flow = flow - total * u[t]
+                    if c == 0:
+                        flow = jnp.where(low_rows, flow, 0.0)
+                    if c == chunks - 1:
+                        flow = jnp.where(high_rows, flow, 0.0)
+                    cy[l, t, rows] = y_up
+                    cy_low[l, t, rows] = y_down
+                    cx[l, t, rows] = x_up
+                    cz[l, t, rows] = below[t]
+                    diag[l, t, rows] = total + shift
+                    r[l + 1, t, rows] = flow
+                k_last, u_last, k, u, below = k, u, k_next, u_next, above
+        return 0
+
+    lax.fori_loop(0, levels // few, prepare, 0)
 
 
 def chain_kernel(
-    start, storage_ref, ext_u_in, ext_k_in, ext_s, y0, y1, flux,
-    ext_u, r, p1, p2, moments, flux_out,
-    cz, cx, cy, cy_low, diag, inside, sem,
+    start, storage_ref, ext_u_in, ext_k, ext_s, y0, y1, flux, r_in, cz_in, cx_in, cy_in, cy_low_in, diag_in,
+    ext_u, p1, p2, moments, flux_out, r, cz, cx, cy, cy_low, diag,
+    inside, sem,
 ):
     flux_copy = pltpu.make_async_copy(flux, flux_out, sem)
     flux_copy.start()
@@ -282,7 +339,6 @@
     keep_high = lane < jnp.where(has_high, HALO, 0)
     keep_low = lane >= jnp.where(has_low, LANES - HALO, LANES)
     base = start[0]
-    ext_k = ext_k_in
 
     def third(f, l):
         a, b = y0[f], y1[f]
@@ -341,30 +397,41 @@
             rows = pl.ds(at, SUB)
 
             def load(ext, plane, dx=0):
-                return [ext[first + plane, t, pl.ds(at + dx, SUB)] for t in every]
+                return ext[first + plane, tiles, pl.ds(at + dx, SUB)]
 
             k_last, u_last = load(ext_k, 0), load(ext_u, 0)
             k, u = load(ext_k, 1), load(ext_u, 1)
-            below = [k[t] + k_last[t] for t in every]
+            below = k + k_last
             for i in range(few):
                 l = first + i
                 k_next, u_next = load(ext_k, i + 2), load(ext_u, i + 2)
-                ks = [load(ext_k, i + 1, dx) for dx in (1, -1)]
-                us = [load(ext_u, i + 1, dx) for dx in (1, -1)]
-                yk, yu = beside(k), beside(u)
-                above = [k[t] + k_next[t] for t in every]
-                for t in every:
-                    y_up, y_down = yk[0][t] + k[t], yk[1][t] + k[t]
-                    x_up, x_down = ks[0][t] + k[t], ks[1][t] + k[t]
-                    total = ((y_up + y_down) + (x_up + x_down)) + (above[t] + below[t])
-                    flow = (y_up * yu[0][t] + y_down * yu[1][t]) + (x_up * us[0][t] + x_down * us[1][t])
-                    flow = flow + (above[t] * u_next[t] + below[t] * u_last[t])
-                    cy[l, t, rows] = y_up
-                    cy_low[l, t, rows] = y_down
-                    cx[l, t, rows] = x_up
-                    cz[l, t, rows] = below[t]
-                    diag[l, t, rows] = total + shift
-                    r[l + 1, t, rows] = masked(flow - total * u[t], t, at, c)
+                edge = [[ext[l + 1, t, rows] for ext in (ext_k, ext_u)] for t in (0, tiles - 1)]
+                k_up, u_up = pltpu.roll(k, LANES - 1, 1), pltpu.roll(u, LANES - 1, 1)
+                k_down, u_down = pltpu.roll(k, 1, 1), pltpu.roll(u, 1, 1)
+                ahead = [pltpu.roll(v, LANES - 1, 1) for v in edge[0]]
+                behind = [pltpu.roll(v, 1, 1) for v in edge[1]]
+                y_up = k + jnp.where(at_end, ahead[0], k_up)
+                y_down = k + jnp.where(at_start, behind[0], k_down)
+                x_up, x_down = k + load(ext_k, i + 1, 1), k + load(ext_k, i + 1, -1)
+                above = k + k_next
+                total = ((y_up + y_down) + (x_up + x_down)) + (above + below)
+                flow = y_up * jnp.where(at_end, ahead[1], u_up) + y_down * jnp.where(at_start, behind[1], u_down)
+                flow = flow + (x_up * load(ext_u, i + 1, 1) + x_down * load(ext_u, i + 1, -1))
+                flow = flow + (above * u_next + below * u_last)
+                cy[l, tiles, rows] = y_up
+                cy_low[l, tiles, rows] = y_down
+                cx[l, tiles, rows] = x_up
+                cz[l, tiles, rows] = below
+                diag[l, tiles, rows] = total + shift
+                r[l + 1, tiles, rows] = masked(flow - total * u, tiles, at, c)
+                for t, (ko, uo), here, kn, un, face in (
+                    (0, edge[0], at_start, k_down, u_down, cy_low),
+                    (tiles - 1, edge[1], at_end, k_up, u_up, cy),
+                ):
+                    kn, un = jnp.where(here, kn, 0.0), jnp.where(here, un, 0.0)
+                    face[l, t, rows] = face[l, t, rows] + kn
+                    diag[l, t, rows] = diag[l, t, rows] + kn
+                    r[l + 1, t, rows] = r[l + 1, t, rows] + ((ko + kn) * un - kn * uo)
                 k_last, u_last, k, u, below = k, u, k_next, u_next, above
         return 0
 
@@ -490,7 +557,7 @@
         copy.wait()
 
 
-def body(
+def step(
     state, conduct, storage, surface_source, plant_type, plant_table, layer_weights, remap_rows, remap_weights
 ):
     levels, nx, ny = state.shape[1:]
@@ -498,78 +565,71 @@
     window = nx + 2 * HALO
     start = jnp.full((1,), SUB - HALO, jnp.int32)
     edge = pltpu.VMEM((levels, SUB, ny), F32)
-    (layers,) = call(
-        layers_kernel, [(NS, nx, ny)], [state], "layers", scratch=[pltpu.SemaphoreType.DMA(())], hbm=(0,)
-    )
+    (layers,) = call(layers_kernel, [(NS, nx, ny)], [state], scratch=[pltpu.SemaphoreType.DMA(())], hbm=(0,))
     partner = lax.ppermute(layers, "comp", [(i, i ^ 1) for i in range(lax.axis_size("comp"))])
     x0, x1 = call(
         edges_kernel,
         [(levels, SUB, ny)] * 2,
-        [state, conduct],
-        "edges",
+        [layers, state, conduct],
         scratch=[edge] * 4 + [pltpu.SemaphoreType.DMA((4,))],
-        hbm=(0, 1),
+        hbm=(1, 2),
     )
     x0, x1 = swap(x0, "gx", 0), swap(x1, "gx", 1)
-    ext = (levels + 2, tiles + 1, nx + 2 * SUB, LANES)
-    ext_s = (NS, tiles, nx + 2 * SUB, LANES)
     table, weights = plant_table.T, layer_weights.transpose(2, 0, 1)
-    ext_u, ext_k, prof = call(
-        own_kernel,
-        [ext, ext, (PROFILES, nx, ny)],
-        [table, weights, state, conduct, plant_type],
-        "own",
+    (prof,) = call(
+        profile_kernel,
+        [(PROFILES, nx, ny)],
+        [table, weights, plant_type, layers],
         scratch=[
             pltpu.SMEM(table.shape, F32),
             pltpu.SMEM(weights.shape, F32),
-            pltpu.VMEM(state.shape, F32),
-            pltpu.VMEM(state.shape, F32),
             pltpu.VMEM(plant_type.shape, jnp.int32),
             pltpu.SemaphoreType.DMA((3,)),
-            pltpu.SemaphoreType.DMA((3, 2)),
         ],
-        hbm=(0, 1, 2, 3, 4),
-        limit=4,
+        hbm=(0, 1, 2),
     )
     flux, src, s0, s1 = call(
         source_kernel,
         [(1, nx, ny), (NS, nx, ny)] + [(NS // 2, SUB, ny)] * 2,
         [remap_rows, partner, remap_weights, prof, surface_source],
-        "source",
         scratch=[pltpu.VMEM((NS, nx, ny), F32)],
         smem=(0,),
     )
     s0, s1 = swap(s0, "gx", 0), swap(s1, "gx", 1)
-    ext_u, ext_k, ext_s, y0, y1 = call(
+    ext = (levels + 2, tiles + 1, nx + 2 * SUB, LANES)
+    ext_u, ext_k, y0, y1 = call(
+        fields_kernel, [ext, ext] + [(3, window, LANES)] * 2, [start, src, state, conduct, x0, x1], smem=(0,)
+    )
+    ext_s, y0, y1 = call(
         columns_kernel,
-        [ext, ext, ext_s] + [(3, window, LANES)] * 2,
-        [start, ext_u, ext_k, src, x0, x1, s0, s1],
-        "columns",
+        [(NS, tiles, nx + 2 * SUB, LANES)] + [(3, window, LANES)] * 2,
+        [start, src, s0, s1, y0, y1],
         smem=(0,),
-        alias={1: 0, 2: 1},
+        alias={4: 1, 5: 2},
+    )
+    coef = (levels,) + ext[1:]
+    coefs = call(
+        coefficients_kernel,
+        [ext, (levels + 1,) + ext[1:]] + [coef] * 4,
+        [start, storage, ext_s, ext_u, ext_k],
+        smem=(0, 1),
     )
     y0, y1 = swap(y0, "gy", 0), swap(y1, "gy", 1)
-    coef = pltpu.VMEM((levels,) + ext[1:], F32)
-    ext_u, r, p1, p2, moments, flux = call(
+    ext_u, p1, p2, moments, flux, r, *_ = call(
         chain_kernel,
-        [ext] * 4 + [(SUB, LANES), (1, nx, ny)],
-        [start, storage, ext_u, ext_k, ext_s, y0, y1, flux],
-        "chain",
-        scratch=[pltpu.VMEM((levels + 1,) + ext[1:], F32)]
-        + [coef] * 4
-        + [pltpu.VMEM((2, nx + 2 * SUB, LANES), F32), pltpu.SemaphoreType.DMA(())],
-        hbm_outs=(5,),
+        [ext] * 3 + [(SUB, LANES), (1, nx, ny)] + [c.shape for c in coefs],
+        [start, storage, ext_u, ext_k, ext_s, y0, y1, flux, *coefs],
+        scratch=[pltpu.VMEM((2, nx + 2 * SUB, LANES), F32), pltpu.SemaphoreType.DMA(())],
+        hbm_outs=(4,),
         smem=(0, 1),
-        limit=16,
-        alias={2: 0},
-    )
-    (moments,) = call(add_kernel, [(SUB, LANES)], everyone(moments, "gx"), "add")
+        alias={2: 0, **{8 + i: 5 + i for i in range(len(coefs))}},
+    )
+    (moments,) = call(add_kernel, [(SUB, LANES)], everyone(moments, "gx"))
     parts = everyone(moments, "gy")
     (new_state,) = call(
         update_kernel,
         [state.shape],
         parts + [ext_u, r, p1, p2],
-        "update",
         scratch=[pltpu.VMEM(state.shape, F32), pltpu.SemaphoreType.DMA((3,))],
         hbm_outs=(0,),
     )
@@ -589,4 +649,4 @@
         P("comp", "gy", None),
     )
     out_specs = (P("comp", None, "gx", "gy"), P("comp", "gx", "gy"))
-    return jax.shard_map(body, mesh=mesh, in_specs=in_specs, out_specs=out_specs, check_vma=False)
+    return jax.shard_map(step, mesh=mesh, in_specs=in_specs, out_specs=out_specs, check_vma=False)

time: 47.8 us -> 43.2 us (0.904)
  starting transfers between devices: 22.1 us -> 12.8 us
  waiting for transfers between devices: 7.26 us -> 11.9 us
    ppermute x6, starting transfers between devices: 12.8 us -> 6.38 us  [everyone(): lax.ppermute(value, axis, [(i, i ^ d) for i in range(n)])]
    ppermute x7, waiting for transfers between devices: 2.59 us -> 6.38 us  [the longest x1 3.8 us: step(): lax.ppermute(layers, 'comp', [(i, i ^ 1) for i in range(lax.axis_size('co...]
    ppermute x7, starting transfers between devices: 9.25 us -> 6.44 us  [the longest x6 4.93 us: swap(): return lax.ppermute(value, ('gx', 'gy'), pairs)]
    ppermute x6, waiting for transfers between devices: 4.67 us -> 5.47 us  [everyone(): lax.ppermute(value, axis, [(i, i ^ d) for i in range(n)])]
    pallas_call x8 -> x10, Pallas kernels: 16.8 us -> 16.8 us  [call(): pl.pallas_call(kernel, out_shape=[jax.ShapeDtypeStruct(s, F32) if i in hb...]
  transfers between devices with their start and end apart: 13 -> 13, of which waited for: 6 -> 8; matrix products, arithmetic and copies ran while one was open for 0% -> 0% of each run, Pallas kernels for 9% -> 13%
where the time goes in v3:
time: 43.2 us; the launch traced here: 42.9 us
  Pallas kernels  16.8 us (39%)
  starting transfers between devices  12.8 us (30%)
  waiting for transfers between devices  11.9 us (28%)
  between operations  1.43 us (3%)
    pallas_call x10, Pallas kernels, call(): pl.pallas_call(kernel, out_shape=[jax.ShapeDtypeStruct(s, F32) if i in hb...  16.8 us
    ppermute x6, starting transfers between devices, everyone(): lax.ppermute(value, axis, [(i, i ^ d) for i in range(n)])  6.38 us
    ppermute x6, waiting for transfers between devices, everyone(): lax.ppermute(value, axis, [(i, i ^ d) for i in range(n)])  5.47 us
    ppermute x6, starting transfers between devices, swap(): return lax.ppermute(value, ('gx', 'gy'), pairs)  4.93 us
    ppermute x1, waiting for transfers between devices, step(): lax.ppermute(layers, 'comp', [(i, i ^ 1) for i in range(lax.axis_size('co...  3.8 us
    ppermute x6, waiting for transfers between devices, swap(): return lax.ppermute(value, ('gx', 'gy'), pairs)  2.58 us
    ppermute x1, starting transfers between devices, step(): lax.ppermute(layers, 'comp', [(i, i ^ 1) for i in range(lax.axis_size('co...  1.52 us
  transfers between devices with their start and end apart: 13, of which 8 were waited for; matrix products, arithmetic and copies ran while one was open for 0% of the time, Pallas kernels for 13%

profile of v3, /device:TPU:0, one launch (start us, length us, event | category | flops | bytes accessed | tf_op | source)
XLA Modules:
  0.0 42.9 jit_solution(14213380155671499041)
XLA Ops:
  0.6 0.0 copy-start
  0.6 0.0 copy-start.1
  0.7 1.1 %shard_map.104.layers.after = f32[6,32,256]{2,1,0:T(8,128)S(1)} custom-call(f32[1,30,32,256]{3,2,1,0:T(8,128)} %u_ref.1), custom_call_target="tpu_custom_call" | custom-call | tf_op jit(solution)/shard_map/pallas_call | solution.py:64
  1.8 1.4 %shard_map.107 = (f32[30,8,256]{2,1,0:T(8,128)S(1)}, f32[30,8,256]{2,1,0:T(8,128)S(1)}) custom-call(f32[6,32,256]{2,1,0:T(8,128)S(1)} %shard_map.104.layers.after, f32[1,30,32,256]{3,2,1,0:T(8,128)} %u_ref.1, f32[1,30,32,256]{3,2,1,0:T(8,128)} %k_ref.1), custom_call_target="tpu_custom_call" | custom-call | tf_op jit(solution)/shard_map/pallas_call | solution.py:64
  3.2 0.6 %collective-permute-start.1 = (f32[30,8,256]{2,1,0:T(8,128)S(1)}, f32[30,8,256]{2,1,0:T(8,128)S(1)}, u32[]{:S(2)}, u32[]{:S(2)}) collective-permute-start(f32[30,8,256]{2,1,0:T(8,128)S(1)} %get-tuple-element.28), channel_id=1, source_target_pairs={{0,4},{1,5},{2,6},{3,7},{4,0},{5,1},{6,2},{7,3},{8,12},{9,13},{10,... | collective-permute-start | bytes 737288 | tf_op jit(solution)/shard_map/ppermute | solution.py:38
  3.7 2.6 %collective-permute-start.2 = (f32[30,8,256]{2,1,0:T(8,128)S(1)}, f32[30,8,256]{2,1,0:T(8,128)S(1)}, u32[]{:S(2)}, u32[]{:S(2)}) collective-permute-start(f32[30,8,256]{2,1,0:T(8,128)S(1)} %get-tuple-element.29), channel_id=1, source_target_pairs={{0,1},{1,0},{2,3},{3,2},{4,8},{5,9},{6,10},{7,11},{8,4},{9,5},{10,... | collective-permute-start | bytes 737288 | tf_op jit(solution)/shard_map/ppermute | solution.py:38
  6.4 1.5 %collective-permute-start = (f32[6,32,256]{2,1,0:T(8,128)S(1)}, f32[6,32,256]{2,1,0:T(8,128)S(1)}, u32[]{:S(2)}, u32[]{:S(2)}) collective-permute-start(f32[6,32,256]{2,1,0:T(8,128)S(1)} %shard_map.104.layers.after), channel_id=1, source_target_pairs={{0,16},{16,0},{1,17},{17,1},{2,18},{18,2},{3,19},{19,3},{4,20},{20... | collective-permute-start | bytes 589832 | tf_op jit(solution)/shard_map/ppermute | solution.py:569
  7.9 1.5 %shard_map.105.prof = f32[15,32,256]{2,1,0:T(8,128)S(1)} custom-call(f32[2,16]{1,0:T(2,128)} %bitcast.3, f32[6,2,16]{2,1,0:T(2,128)} %bitcast.2, s32[1,32,256]{2,1,0:T(8,128)} %kind_hbm.1, f32[6,32,256]{2,1,0:T(8,128)S(1)} %shard_map.104.layers.after), custom_call_target="tpu_custom_call" | custom-call | tf_op jit(solution)/shard_map/pallas_call | solution.py:64
  9.4 3.8 %collective-permute-done.part_ref = f32[6,32,256]{2,1,0:T(8,128)S(1)} collective-permute-done((f32[6,32,256]{2,1,0:T(8,128)S(1)}, f32[6,32,256]{2,1,0:T(8,128)S(1)}, u32[]{:S(2)}, u32[]{:S(2)}) %collective-permute-start) | collective-permute-done | bytes 196640 | tf_op jit(solution)/shard_map/ppermute | solution.py:569
  13.2 0.9 %shard_map.106 = (f32[1,32,256]{2,1,0:T(8,128)S(1)}, f32[6,32,256]{2,1,0:T(8,128)S(1)}, f32[3,8,256]{2,1,0:T(8,128)S(1)}, f32[3,8,256]{2,1,0:T(8,128)S(1)}) custom-call(s32[1,32]{1,0:T(1,128)S(1)} %copy-done.4, f32[6,32,256]{2,1,0:T(8,128)S(1)} %collective-permute-done.part_ref, f32[1,256,128]{2,1,0:T(8,128)S(1)} %copy-done.2, ...), custom_call_target="tpu_custom_call" | custom-call | tf_op jit(solution)/shard_map/pallas_call | solution.py:64
  14.2 0.1 collective-permute-start.3
  14.2 0.8 %collective-permute-start.4 = (f32[3,8,256]{2,1,0:T(8,128)S(1)}, f32[3,8,256]{2,1,0:T(8,128)S(1)}, u32[]{:S(2)}, u32[]{:S(2)}) collective-permute-start(f32[3,8,256]{2,1,0:T(8,128)S(1)} %get-tuple-element.33), channel_id=1, source_target_pairs={{0,1},{1,0},{2,3},{3,2},{4,8},{5,9},{6,10},{7,11},{8,4},{9,5},{10,... | collective-permute-start | bytes 73736 | tf_op jit(solution)/shard_map/ppermute | solution.py:38
  15.1 1.1 %shard_map.108 = (f32[32,3,48,128]{3,2,1,0:T(8,128)S(1)}, f32[32,3,48,128]{3,2,1,0:T(8,128)S(1)}, f32[3,40,128]{2,1,0:T(8,128)S(1)}, f32[3,40,128]{2,1,0:T(8,128)S(1)}) custom-call(s32[1]{0:T(128)} %constant.0.clone.1.start, f32[6,32,256]{2,1,0:T(8,128)S(1)} %get-tuple-element.27.after.s_ref, f32[1,30,32,256]{3,2,1,0:T(8,128)S(1)} %copy-done, ...), custom_call_target="tpu_custom_call" | custom-call | tf_op jit(solution)/shard_map/pallas_call | solution.py:64
  16.2 1.9 %collective-permute-done.4.s1 = f32[3,8,256]{2,1,0:T(8,128)S(1)} collective-permute-done((f32[3,8,256]{2,1,0:T(8,128)S(1)}, f32[3,8,256]{2,1,0:T(8,128)S(1)}, u32[]{:S(2)}, u32[]{:S(2)}) %collective-permute-start.4) | collective-permute-done | bytes 24608 | tf_op jit(solution)/shard_map/ppermute | solution.py:38
  18.1 0.1 shard_map.109
  18.3 0.8 %collective-permute-start.5 = (f32[3,40,128]{2,1,0:T(8,128)S(1)}, f32[3,40,128]{2,1,0:T(8,128)S(1)}, u32[]{:S(2)}, u32[]{:S(2)}) collective-permute-start(f32[3,40,128]{2,1,0:T(8,128)S(1)} %get-tuple-element.37), channel_id=1, source_target_pairs={{0,1},{1,0},{2,3},{3,2},{4,5},{5,4},{6,7},{7,6},{8,9},{9,8},{10,11... | collective-permute-start | bytes 184328 | tf_op jit(solution)/shard_map/ppermute | solution.py:38
  19.8 2.1 %shard_map.110 = (f32[32,3,48,128]{3,2,1,0:T(8,128)S(1)}, f32[31,3,48,128]{3,2,1,0:T(8,128)S(1)}, f32[30,3,48,128]{3,2,1,0:T(8,128)S(1)}, f32[30,3,48,128]{3,2,1...) custom-call(s32[1]{0:T(128)} %constant.0.clone.1.start, f32[1]{0:T(128)S(6)} %copy.29.storage_ref, ...), custom_call_target="tpu_custom_call" | custom-call | tf_op jit(solution)/shard_map/pallas_call | solution.py:64
  21.9 0.7 %collective-permute-done.5.y0 = f32[3,40,128]{2,1,0:T(8,128)S(1)} collective-permute-done((f32[3,40,128]{2,1,0:T(8,128)S(1)}, f32[3,40,128]{2,1,0:T(8,128)S(1)}, u32[]{:S(2)}, u32[]{:S(2)}) %collective-permute-start.5) | collective-permute-done | bytes 61472 | tf_op jit(solution)/shard_map/ppermute | solution.py:38
  22.6 0.0 collective-permute-done.6.y1
  22.6 7.4 %shard_map.111 = (f32[32,3,48,128]{3,2,1,0:T(8,128)S(1)}, f32[32,3,48,128]{3,2,1,0:T(8,128)S(1)}, f32[32,3,48,128]{3,2,1,0:T(8,128)S(1)}, f32[8,128]{1,0:T(8,128...) custom-call(s32[1]{0:T(128)} %constant.0.clone.1.start, ...), custom_call_target="tpu_custom_call", output_to_operand_aliasing={{0}: (2, {}), {5}: (8, {}), {6}: (9, {}), {7}: (10, {}), {8... | custom-call | tf_op jit(solution)/shard_map/pallas_call | solution.py:64
  29.9 0.2 collective-permute-start.9
  30.2 1.3 %collective-permute-start.8 = (f32[8,128]{1,0:T(8,128)S(1)}, f32[8,128]{1,0:T(8,128)S(1)}, u32[]{:S(2)}, u32[]{:S(2)}) collective-permute-start(f32[8,128]{1,0:T(8,128)S(1)} %get-tuple-element.46.refs_0_), channel_id=1, source_target_pairs={{0,8},{4,12},{8,0},{12,4},{1,9},{5,13},{9,1},{13,5},{2,10},{6,14},... | collective-permute-start | bytes 12296 | tf_op jit(solution)/shard_map/ppermute | solution.py:43
  31.5 0.4 collective-permute-start.7
  31.9 1.2 %collective-permute-done.9.refs_3_ = f32[8,128]{1,0:T(8,128)S(1)} collective-permute-done((f32[8,128]{1,0:T(8,128)S(1)}, f32[8,128]{1,0:T(8,128)S(1)}, u32[]{:S(2)}, u32[]{:S(2)}) %collective-permute-start.9) | collective-permute-done | bytes 4128 | tf_op jit(solution)/shard_map/ppermute | solution.py:43
  33.0 0.7 %collective-permute-done.8.refs_2_ = f32[8,128]{1,0:T(8,128)S(1)} collective-permute-done((f32[8,128]{1,0:T(8,128)S(1)}, f32[8,128]{1,0:T(8,128)S(1)}, u32[]{:S(2)}, u32[]{:S(2)}) %collective-permute-start.8) | collective-permute-done | bytes 4128 | tf_op jit(solution)/shard_map/ppermute | solution.py:43
  33.8 3.3 %collective-permute-start.12 = (f32[8,128]{1,0:T(8,128)S(1)}, f32[8,128]{1,0:T(8,128)S(1)}, u32[]{:S(2)}, u32[]{:S(2)}) collective-permute-start(f32[8,128]{1,0:T(8,128)S(1)} %shard_map.112.refs_0_), channel_id=1, source_target_pairs={{0,3},{1,2},{2,1},{3,0},{4,7},{5,6},{6,5},{7,4},{8,11},{9,10},{10,... | collective-permute-start | bytes 12296 | tf_op jit(solution)/shard_map/ppermute | solution.py:43
  37.1 1.1 %collective-permute-start.11 = (f32[8,128]{1,0:T(8,128)S(1)}, f32[8,128]{1,0:T(8,128)S(1)}, u32[]{:S(2)}, u32[]{:S(2)}) collective-permute-start(f32[8,128]{1,0:T(8,128)S(1)} %shard_map.112.refs_0_), channel_id=1, source_target_pairs={{0,2},{1,3},{2,0},{3,1},{4,6},{5,7},{6,4},{7,5},{8,10},{9,11},{10,... | collective-permute-start | bytes 12296 | tf_op jit(solution)/shard_map/ppermute | solution.py:43
  38.2 0.1 collective-permute-start.10
  38.3 1.0 %collective-permute-done.12.refs_3_ = f32[8,128]{1,0:T(8,128)S(1)} collective-permute-done((f32[8,128]{1,0:T(8,128)S(1)}, f32[8,128]{1,0:T(8,128)S(1)}, u32[]{:S(2)}, u32[]{:S(2)}) %collective-permute-start.12) | collective-permute-done | bytes 4128 | tf_op jit(solution)/shard_map/ppermute | solution.py:43
  39.3 2.4 %collective-permute-done.11.refs_2_ = f32[8,128]{1,0:T(8,128)S(1)} collective-permute-done((f32[8,128]{1,0:T(8,128)S(1)}, f32[8,128]{1,0:T(8,128)S(1)}, u32[]{:S(2)}, u32[]{:S(2)}) %collective-permute-start.11) | collective-permute-done | bytes 4128 | tf_op jit(solution)/shard_map/ppermute | solution.py:43
  41.6 0.2 collective-permute-done.10.refs_1_
  41.8 1.1 %shard_map.113 = f32[1,30,32,256]{3,2,1,0:T(8,128)} custom-call(f32[8,128]{1,0:T(8,128)S(1)} %shard_map.112.refs_0_, f32[8,128]{1,0:T(8,128)S(1)} %collective-permute-done.10.refs_1_, f32[8,128]{1,0:T(8,128)S(1)} %collective-permute-done.11.refs_2_, f32[8,128]{1,0:T(8,128)S(1)} %collective-permute-done.12.refs_3_, ...), custom_call_target="tpu_custom_call" | custom-call | tf_op jit(solution)/shard_map/pallas_call | solution.py:64
  (14 shorter events, 0.0 us)
Async XLA Ops:
  0.6 14.4 %copy-start = (f32[1,30,32,256]{3,2,1,0:T(8,128)S(1)}, f32[1,30,32,256]{3,2,1,0:T(8,128)}, u32[]{:S(2)}) copy-start(f32[1,30,32,256]{3,2,1,0:T(8,128)} %u_ref.1) | copy-start | bytes 2949124
  0.6 14.4 %copy-start.1 = (f32[1,30,32,256]{3,2,1,0:T(8,128)S(1)}, f32[1,30,32,256]{3,2,1,0:T(8,128)}, u32[]{:S(2)}) copy-start(f32[1,30,32,256]{3,2,1,0:T(8,128)} %k_ref.1) | copy-start | bytes 2949124
  0.7 12.6 %copy-start.2 = (f32[1,256,128]{2,1,0:T(8,128)S(1)}, f32[1,256,128]{2,1,0:T(8,128)}, u32[]{:S(2)}) copy-start(f32[1,256,128]{2,1,0:T(8,128)} %w_ref.1) | copy-start | bytes 393220
  0.7 12.6 %copy-start.4 = (s32[1,32]{1,0:T(1,128)S(1)}, s32[1,32]{1,0:T(1,128)}, u32[]{:S(2)}) copy-start(s32[1,32]{1,0:T(1,128)} %rows_ref.1) | copy-start | bytes 388
  0.7 12.6 %copy-start.3 = (f32[1,32,256]{2,1,0:T(8,128)S(1)}, f32[1,32,256]{2,1,0:T(8,128)}, u32[]{:S(2)}) copy-start(f32[1,32,256]{2,1,0:T(8,128)} %surf_ref.1) | copy-start | bytes 98308
  3.2 11.9 %collective-permute-start.1 = (f32[30,8,256]{2,1,0:T(8,128)S(1)}, f32[30,8,256]{2,1,0:T(8,128)S(1)}, u32[]{:S(2)}, u32[]{:S(2)}) collective-permute-start(f32[30,8,256]{2,1,0:T(8,128)S(1)} %get-tuple-element.28), channel_id=1, source_target_pairs={{0,4},{1,5},{2,6},{3,7},{4,0},{5,1},{6,2},{7,3},{8,12},{9,13},{10,... | collective-permute-start | bytes 737288 | tf_op jit(solution)/shard_map/ppermute | solution.py:38
  3.7 11.3 %collective-permute-start.2 = (f32[30,8,256]{2,1,0:T(8,128)S(1)}, f32[30,8,256]{2,1,0:T(8,128)S(1)}, u32[]{:S(2)}, u32[]{:S(2)}) collective-permute-start(f32[30,8,256]{2,1,0:T(8,128)S(1)} %get-tuple-element.29), channel_id=1, source_target_pairs={{0,1},{1,0},{2,3},{3,2},{4,8},{5,9},{6,10},{7,11},{8,4},{9,5},{10,... | collective-permute-start | bytes 737288 | tf_op jit(solution)/shard_map/ppermute | solution.py:38
  6.4 6.8 %collective-permute-start = (f32[6,32,256]{2,1,0:T(8,128)S(1)}, f32[6,32,256]{2,1,0:T(8,128)S(1)}, u32[]{:S(2)}, u32[]{:S(2)}) collective-permute-start(f32[6,32,256]{2,1,0:T(8,128)S(1)} %shard_map.104.layers.after), channel_id=1, source_target_pairs={{0,16},{16,0},{1,17},{17,1},{2,18},{18,2},{3,19},{19,3},{4,20},{20... | collective-permute-start | bytes 589832 | tf_op jit(solution)/shard_map/ppermute | solution.py:569
  14.2 2.1 %collective-permute-start.3 = (f32[3,8,256]{2,1,0:T(8,128)S(1)}, f32[3,8,256]{2,1,0:T(8,128)S(1)}, u32[]{:S(2)}, u32[]{:S(2)}) collective-permute-start(f32[3,8,256]{2,1,0:T(8,128)S(1)} %get-tuple-element.32), channel_id=1, source_target_pairs={{0,4},{1,5},{2,6},{3,7},{4,0},{5,1},{6,2},{7,3},{8,12},{9,13},{10,... | collective-permute-start | bytes 73736 | tf_op jit(solution)/shard_map/ppermute | solution.py:38
  14.2 3.9 %collective-permute-start.4 = (f32[3,8,256]{2,1,0:T(8,128)S(1)}, f32[3,8,256]{2,1,0:T(8,128)S(1)}, u32[]{:S(2)}, u32[]{:S(2)}) collective-permute-start(f32[3,8,256]{2,1,0:T(8,128)S(1)} %get-tuple-element.33), channel_id=1, source_target_pairs={{0,1},{1,0},{2,3},{3,2},{4,8},{5,9},{6,10},{7,11},{8,4},{9,5},{10,... | collective-permute-start | bytes 73736 | tf_op jit(solution)/shard_map/ppermute | solution.py:38
  18.3 4.3 %collective-permute-start.5 = (f32[3,40,128]{2,1,0:T(8,128)S(1)}, f32[3,40,128]{2,1,0:T(8,128)S(1)}, u32[]{:S(2)}, u32[]{:S(2)}) collective-permute-start(f32[3,40,128]{2,1,0:T(8,128)S(1)} %get-tuple-element.37), channel_id=1, source_target_pairs={{0,1},{1,0},{2,3},{3,2},{4,5},{5,4},{6,7},{7,6},{8,9},{9,8},{10,11... | collective-permute-start | bytes 184328 | tf_op jit(solution)/shard_map/ppermute | solution.py:38
  19.1 3.5 %collective-permute-start.6 = (f32[3,40,128]{2,1,0:T(8,128)S(1)}, f32[3,40,128]{2,1,0:T(8,128)S(1)}, u32[]{:S(2)}, u32[]{:S(2)}) collective-permute-start(f32[3,40,128]{2,1,0:T(8,128)S(1)} %get-tuple-element.38), channel_id=1, source_target_pairs={{0,4},{1,2},{2,1},{3,7},{4,0},{5,6},{6,5},{7,3},{8,12},{9,10},{10,... | collective-permute-start | bytes 184328 | tf_op jit(solution)/shard_map/ppermute | solution.py:38
  29.9 3.1 %collective-permute-start.9 = (f32[8,128]{1,0:T(8,128)S(1)}, f32[8,128]{1,0:T(8,128)S(1)}, u32[]{:S(2)}, u32[]{:S(2)}) collective-permute-start(f32[8,128]{1,0:T(8,128)S(1)} %get-tuple-element.46.refs_0_), channel_id=1, source_target_pairs={{0,12},{4,8},{8,4},{12,0},{1,13},{5,9},{9,5},{13,1},{2,14},{6,10},... | collective-permute-start | bytes 12296 | tf_op jit(solution)/shard_map/ppermute | solution.py:43
  30.2 3.6 %collective-permute-start.8 = (f32[8,128]{1,0:T(8,128)S(1)}, f32[8,128]{1,0:T(8,128)S(1)}, u32[]{:S(2)}, u32[]{:S(2)}) collective-permute-start(f32[8,128]{1,0:T(8,128)S(1)} %get-tuple-element.46.refs_0_), channel_id=1, source_target_pairs={{0,8},{4,12},{8,0},{12,4},{1,9},{5,13},{9,1},{13,5},{2,10},{6,14},... | collective-permute-start | bytes 12296 | tf_op jit(solution)/shard_map/ppermute | solution.py:43
  31.5 2.3 %collective-permute-start.7 = (f32[8,128]{1,0:T(8,128)S(1)}, f32[8,128]{1,0:T(8,128)S(1)}, u32[]{:S(2)}, u32[]{:S(2)}) collective-permute-start(f32[8,128]{1,0:T(8,128)S(1)} %get-tuple-element.46.refs_0_), channel_id=1, source_target_pairs={{0,4},{4,0},{8,12},{12,8},{1,5},{5,1},{9,13},{13,9},{2,6},{6,2},{1... | collective-permute-start | bytes 12296 | tf_op jit(solution)/shard_map/ppermute | solution.py:43
  33.8 5.5 %collective-permute-start.12 = (f32[8,128]{1,0:T(8,128)S(1)}, f32[8,128]{1,0:T(8,128)S(1)}, u32[]{:S(2)}, u32[]{:S(2)}) collective-permute-start(f32[8,128]{1,0:T(8,128)S(1)} %shard_map.112.refs_0_), channel_id=1, source_target_pairs={{0,3},{1,2},{2,1},{3,0},{4,7},{5,6},{6,5},{7,4},{8,11},{9,10},{10,... | collective-permute-start | bytes 12296 | tf_op jit(solution)/shard_map/ppermute | solution.py:43
  37.1 4.5 %collective-permute-start.11 = (f32[8,128]{1,0:T(8,128)S(1)}, f32[8,128]{1,0:T(8,128)S(1)}, u32[]{:S(2)}, u32[]{:S(2)}) collective-permute-start(f32[8,128]{1,0:T(8,128)S(1)} %shard_map.112.refs_0_), channel_id=1, source_target_pairs={{0,2},{1,3},{2,0},{3,1},{4,6},{5,7},{6,4},{7,5},{8,10},{9,11},{10,... | collective-permute-start | bytes 12296 | tf_op jit(solution)/shard_map/ppermute | solution.py:43
  38.2 3.6 %collective-permute-start.10 = (f32[8,128]{1,0:T(8,128)S(1)}, f32[8,128]{1,0:T(8,128)S(1)}, u32[]{:S(2)}, u32[]{:S(2)}) collective-permute-start(f32[8,128]{1,0:T(8,128)S(1)} %shard_map.112.refs_0_), channel_id=1, source_target_pairs={{0,1},{1,0},{2,3},{3,2},{4,5},{5,4},{6,7},{7,6},{8,9},{9,8},{10,11... | collective-permute-start | bytes 12296 | tf_op jit(solution)/shard_map/ppermute | solution.py:43

commit v4 on v3

--- a/solution.py
+++ b/solution.py
@@ -1,3 +1,5 @@
+import functools
+
 import jax
 import jax.numpy as jnp
 from jax import lax
@@ -17,6 +19,16 @@
 PROFILES = 2 * NS + 3
 F32 = jnp.float32
 MIB = 1 << 20
+EARLY = (2, 5)
+
+
+def store(ext, plane, t, chunk, chunks, value):
+    at = SUB + SUB * chunk
+    ext[plane, t, at : at + SUB] = value
+    if chunk == chunks - 1:
+        ext[plane, t, :SUB] = value
+    if chunk == 0:
+        ext[plane, t, SUB + SUB * chunks :] = value
 
 
 def swap(value, axis, which):
@@ -41,6 +53,10 @@
 def everyone(value, axis):
     n = lax.axis_size(axis)
     return [value] + [lax.ppermute(value, axis, [(i, i ^ d) for i in range(n)]) for d in range(1, n)]
+
+
+def steps(levels, most):
+    return max(n for n in range(1, most + 1) if levels % n == 0)
 
 
 def iota(shape, dim):
@@ -103,7 +119,9 @@
         out1[l] = jnp.where(odd, high, low)
 
 
-def profile_kernel(table_hbm, lw_hbm, kind_hbm, layers, prof, table, lw, kind_ref, sems):
+def profile_kernel(
+    table_hbm, lw_hbm, kind_hbm, layers, prof, table, lw, kind_ref, sems
+):
     nx = layers.shape[1]
     comp = lax.axis_index("comp")
     copies = [
@@ -136,60 +154,60 @@
     upper = iota((SUB, LANES), 0) < HALO
     gx = lax.axis_index("gx")
     odd = gx % 2 == 1
-    keep_low = ~upper & (gx > 0)
-    keep_high = upper & (gx < count - 1)
+    keep = (upper & (gx < count - 1)) | (~upper & (gx > 0))
 
     def halves(first, second, j, cols):
         a, b = first[j, :, cols], second[j, :, cols]
         high, low = jnp.where(odd, b, a), jnp.where(odd, a, b)
-        lows = jnp.where(keep_low, half_swap(low), 0.0), jnp.where(keep_low, low, 0.0)
-        highs = jnp.where(keep_high, high, 0.0), jnp.where(keep_high, half_swap(high), 0.0)
-        return lows, highs
+        one, two = jnp.where(upper, high, half_swap(low)), jnp.where(upper, half_swap(high), low)
+        return jnp.where(keep, one, 0.0), jnp.where(keep, two, 0.0)
 
     return halves
 
 
 def pack_columns(ext, plane, count, base, window, tiles, outs, slot):
-    group = iota((window, LANES), 1) // HALO
+    lane = iota((window, LANES), 1)
+    group = lane // HALO
+    groups = LANES // HALO
+    packs = [jnp.zeros((window, LANES), F32) for _ in range(2)]
+    for l in range(count):
+        rows = pl.ds(base, window)
+        v = jnp.where(lane < LANES // 2, ext[l + plane, 0, rows], ext[l + plane, tiles - 1, rows])
+        v = pltpu.roll(v, HALO * l, 1) if l else v
+        packs[l % 2] = jnp.where((group == l) | (group == (l - 1) % groups), v, packs[l % 2])
+    even = group % 2 == 0
+    low = jnp.where(even, packs[0], packs[1])
+    high = jnp.where(even, packs[1], packs[0])
     first_high = lax.axis_index("gy") % 2 == 0
-    tile0 = jnp.where(first_high, tiles - 1, 0)
-    move0 = jnp.where(first_high, HALO, 0)
-    for out, tile, move in ((outs[0], tile0, move0), (outs[1], tiles - 1 - tile0, HALO - move0)):
-        packed = jnp.zeros((window, LANES), F32)
-        for l in range(count):
-            v = ext[l + plane, tile, pl.ds(base, window)]
-            v = pltpu.roll(v, (HALO * l + move) % LANES, 1)
-            packed = jnp.where(group == l, v, packed)
-        out[slot] = packed
-
-
-def fields_kernel(start, after, u_ref, k_ref, x0, x1, ext_u, ext_k, out0, out1):
+    outs[0][slot] = jnp.where(first_high, high, low)
+    outs[1][slot] = jnp.where(first_high, low, high)
+
+
+def fields_kernel(after, u_ref, k_ref, x0, x1, ext_u, ext_k, out0, out1):
     _, levels, nx, ny = u_ref.shape
     tiles = ny // LANES
-    blank = jnp.zeros((nx + 2 * SUB, LANES), F32)
+    blank = jnp.zeros(ext_u.shape[2:], F32)
     for t in range(tiles + 1):
         for ext in (ext_u, ext_k):
             ext[0, t] = blank
             ext[levels + 1, t] = blank
     halves = received_rows(lax.axis_size("gx"))
+    chunks = nx // SUB + 1
 
     def level(l, _):
         for t in range(tiles):
             cols = slice(t * LANES, (t + 1) * LANES)
-            lows, highs = halves(x0, x1, l, cols)
-            own = u_ref[0, l, :, cols], k_ref[0, l, :, cols]
-            for rows, (u, k) in (
-                (slice(0, SUB), lows),
-                (slice(SUB, SUB + nx), own),
-                (slice(SUB + nx, 2 * SUB + nx), highs),
-            ):
-                ext_u[l + 1, t, rows] = u
-                ext_k[l + 1, t, rows] = k * (0.5 + 0.25 * jnp.tanh(u))
+            halo = halves(x0, x1, l, cols)
+            for c in range(chunks):
+                rows = slice(SUB * c, SUB * c + SUB)
+                u, k = halo if c == chunks - 1 else (u_ref[0, l, rows, cols], k_ref[0, l, rows, cols])
+                store(ext_u, l + 1, t, c, chunks, u)
+                store(ext_k, l + 1, t, c, chunks, k * (0.5 + 0.25 * jnp.tanh(u)))
         return 0
 
     lax.fori_loop(0, levels, level, 0, unroll=2)
     for slot, ext in enumerate((ext_u, ext_k)):
-        pack_columns(ext, 1, levels, start[0], nx + 2 * HALO, tiles, (out0, out1), slot)
+        pack_columns(ext, 1, levels, SUB, nx + SUB, tiles, (out0, out1), slot)
 
 
 def split(v):
@@ -242,47 +260,41 @@
         out1[j] = jnp.where(odd, high, low)
 
 
-def columns_kernel(start, s_ref, s0, s1, in0, in1, ext_s, out0, out1):
+def columns_kernel(s_ref, s0, s1, in0, in1, after, ext_s, out0, out1):
     nx, ny = s_ref.shape[1:]
     tiles = ny // LANES
     halves = received_rows(lax.axis_size("gx"))
     for j in range(NS // 2):
         for t in range(tiles):
             cols = slice(t * LANES, (t + 1) * LANES)
-            lows, highs = halves(s0, s1, j, cols)
-            for i in range(2):
-                ext_s[2 * j + i, t, :SUB] = lows[i]
-                ext_s[2 * j + i, t, SUB : SUB + nx] = s_ref[2 * j + i, :, cols]
-                ext_s[2 * j + i, t, SUB + nx :] = highs[i]
-    pack_columns(ext_s, 0, NS, start[0], nx + 2 * HALO, tiles, (out0, out1), 2)
-
-
-def coefficients_kernel(start, storage_ref, after, ext_u, ext_k, r, cz, cx, cy, cy_low, diag):
-    levels = ext_u.shape[0] - 2
+            for i, halo in enumerate(halves(s0, s1, j, cols)):
+                ext_s[2 * j + i, t, :nx] = s_ref[2 * j + i, :, cols]
+                ext_s[2 * j + i, t, nx:] = halo
+    pack_columns(ext_s, 0, NS, 0, nx + SUB, tiles, (out0, out1), 2)
+
+
+def coefficients_kernel(lo, hi, after, ext_u, ext_k, *refs):
+    r, cz, cx, cy, cy_low, diag, beyond = refs[-7:]
     tiles = ext_u.shape[1] - 1
-    nx = ext_u.shape[2] - 2 * SUB
     gx, ngx = lax.axis_index("gx"), lax.axis_size("gx")
-    base = start[0]
-    shift = storage_ref[0] - CENTRE
-    chunks = (nx + 2 * HALO) // SUB
-    few = next(n for n in (3, 2, 1) if levels % n == 0)
+    chunks = ext_u.shape[2] // SUB - 2
+    few = steps(hi - lo, 6)
     own = range(tiles)
     lane, row = iota((SUB, LANES), 1), iota((SUB, LANES), 0)
     at_end, at_start = lane == LANES - 1, lane == 0
-    low_rows = (row >= HALO) | (gx > 0)
-    high_rows = (row < HALO) | (gx < ngx - 1)
+    keep = ((row < HALO) & (gx < ngx - 1)) | ((row >= HALO) & (gx > 0))
 
     def beside(vs):
         up = [pltpu.roll(v, LANES - 1, 1) for v in vs] + [0.0]
         down = [0.0] + [pltpu.roll(v, 1, 1) for v in vs]
         ups = [jnp.where(at_end, up[t + 1], up[t]) for t in own]
         downs = [jnp.where(at_start, down[t], down[t + 1]) for t in own]
-        return ups, downs
+        return ups, downs, jnp.where(at_end, up[0], down[tiles])
 
     def prepare(j, _):
-        first = j * few
+        first = lo + j * few
         for c in range(chunks):
-            at = base + SUB * c
+            at = SUB + SUB * c
             rows = pl.ds(at, SUB)
 
             def load(ext, plane, dx=0):
@@ -297,6 +309,8 @@
                 ks = [load(ext_k, i + 1, dx) for dx in (1, -1)]
                 us = [load(ext_u, i + 1, dx) for dx in (1, -1)]
                 yk, yu = beside(k), beside(u)
+                beyond[0, l, rows] = yk[2]
+                beyond[1, l, rows] = yu[2]
                 above = [k[t] + k_next[t] for t in own]
                 for t in own:
                     y_up, y_down = yk[0][t] + k[t], yk[1][t] + k[t]
@@ -305,24 +319,22 @@
                     flow = (y_up * yu[0][t] + y_down * yu[1][t]) + (x_up * us[0][t] + x_down * us[1][t])
                     flow = flow + (above[t] * u_next[t] + below[t] * u_last[t])
                     flow = flow - total * u[t]
-                    if c == 0:
-                        flow = jnp.where(low_rows, flow, 0.0)
                     if c == chunks - 1:
-                        flow = jnp.where(high_rows, flow, 0.0)
+                        flow = jnp.where(keep, flow, 0.0)
                     cy[l, t, rows] = y_up
                     cy_low[l, t, rows] = y_down
-                    cx[l, t, rows] = x_up
+                    store(cx, l, t, c, chunks, x_up)
                     cz[l, t, rows] = below[t]
-                    diag[l, t, rows] = total + shift
-                    r[l + 1, t, rows] = flow
+                    diag[l, t, rows] = total
+                    store(r, l + 1, t, c, chunks, flow)
                 k_last, u_last, k, u, below = k, u, k_next, u_next, above
         return 0
 
-    lax.fori_loop(0, levels // few, prepare, 0)
+    lax.fori_loop(0, (hi - lo) // few, prepare, 0)
 
 
 def chain_kernel(
-    start, storage_ref, ext_u_in, ext_k, ext_s, y0, y1, flux, r_in, cz_in, cx_in, cy_in, cy_low_in, diag_in,
+    storage_ref, ext_u_in, ext_k, ext_s, y0, y1, flux, beyond, r_in, cz_in, cx_in, cy_in, cy_low_in, diag_in,
     ext_u, p1, p2, moments, flux_out, r, cz, cx, cy, cy_low, diag,
     inside, sem,
 ):
@@ -330,41 +342,43 @@
     flux_copy.start()
     levels = ext_u.shape[0] - 2
     tiles, all_rows = ext_u.shape[1] - 1, ext_u.shape[2]
-    nx = all_rows - 2 * SUB
-    window = nx + 2 * HALO
+    nx = all_rows - 3 * SUB
+    window = nx + SUB
+    chunks = window // SUB
     gx, gy, ngx, ngy = lax.axis_index("gx"), lax.axis_index("gy"), lax.axis_size("gx"), lax.axis_size("gy")
     odd = gy % 2 == 1
     has_low, has_high = gy > 0, gy < ngy - 1
-    lane = iota((window, LANES), 1)
-    keep_high = lane < jnp.where(has_high, HALO, 0)
-    keep_low = lane >= jnp.where(has_low, LANES - HALO, LANES)
-    base = start[0]
-
-    def third(f, l):
+    even = (iota((window, LANES), 1) // HALO) % 2 == 0
+
+    def halves(f):
         a, b = y0[f], y1[f]
-        high, low = jnp.where(odd, b, a), jnp.where(odd, a, b)
-        high = pltpu.roll(high, (LANES - HALO * l) % LANES, 1) if (HALO * l) % LANES else high
-        low = pltpu.roll(low, (2 * LANES - HALO - HALO * l) % LANES, 1)
-        return jnp.where(keep_high, high, jnp.where(keep_low, low, 0.0))
+        high = jnp.where(has_high, jnp.where(odd, b, a), 0.0)
+        low = jnp.where(has_low, jnp.where(odd, a, b), 0.0)
+        return jnp.where(even, high, low), jnp.where(even, low, high)
+
+    def third(packed, l):
+        turn = (LANES - HALO * l) % LANES
+        return pltpu.roll(packed[l % 2], turn, 1) if turn else packed[l % 2]
 
     zero_tile = jnp.zeros((SUB, LANES), F32)
-    for l in range(levels):
-        for f, ext in enumerate((ext_u, ext_k)):
-            ext[l + 1, tiles, :SUB] = zero_tile
-            ext[l + 1, tiles, SUB + nx :] = zero_tile
-            ext[l + 1, tiles, pl.ds(base, window)] = third(f, l)
+    for f, ext in enumerate((ext_u, ext_k)):
+        packed = halves(f)
+        for l in range(levels):
+            columns = third(packed, l)
+            for c in range(chunks):
+                store(ext, l + 1, tiles, c, chunks, columns[SUB * c : SUB * c + SUB])
     blank = jnp.zeros((all_rows, LANES), F32)
     for t in range(tiles + 1):
         for ext in (r, p1, p2):
             ext[0, t] = blank
             ext[levels + 1, t] = blank
 
-    row = iota((all_rows, LANES), 0) - SUB
-    col = iota((all_rows, LANES), 1)
-    row_ok = ((row >= 0) & (row < nx)) | ((row >= nx) & (gx < ngx - 1)) | ((row < 0) & (gx > 0))
+    row, col = iota((SUB, LANES), 0), iota((SUB, LANES), 1)
+    row_ok = ((row < HALO) & (gx < ngx - 1)) | ((row >= HALO) & (gx > 0))
     col_ok = ((col < HALO) & has_high) | ((col >= LANES - HALO) & has_low)
     inside[0] = jnp.where(row_ok, 1.0, 0.0)
-    inside[1] = jnp.where(row_ok & col_ok, 1.0, 0.0)
+    inside[1] = jnp.where(col_ok, 1.0, 0.0)
+    inside[2] = jnp.where(row_ok & col_ok, 1.0, 0.0)
 
     lane8 = iota((SUB, LANES), 1)
     at_end, at_start = lane8 == LANES - 1, lane8 == 0
@@ -377,23 +391,22 @@
         downs = [jnp.where(at_start, down[(t - 1) % n], down[t]) for t in range(n)]
         return ups, downs
 
-    def masked(w, t, at, chunk):
+    def masked(w, t, chunk):
         if t == tiles:
-            return w * inside[1, pl.ds(at, SUB)]
-        if chunk in (0, chunks - 1):
-            return w * inside[0, pl.ds(at, SUB)]
+            return w * inside[2 if chunk == chunks - 1 else 1]
+        if chunk == chunks - 1:
+            return w * inside[0]
         return w
 
     shift = storage_ref[0] - CENTRE
-    chunks = window // SUB
     every = range(tiles + 1)
-    few = next(n for n in (3, 2, 1) if levels % n == 0)
-    many = next(n for n in (6, 5, 4, 3, 2, 1) if levels % n == 0)
+    few = steps(levels, 30)
+    many = steps(levels, 15)
 
     def prepare(j, _):
         first = j * few
         for c in range(chunks):
-            at = base + SUB * c
+            at = SUB + SUB * c
             rows = pl.ds(at, SUB)
 
             def load(ext, plane, dx=0):
@@ -408,44 +421,44 @@
                 edge = [[ext[l + 1, t, rows] for ext in (ext_k, ext_u)] for t in (0, tiles - 1)]
                 k_up, u_up = pltpu.roll(k, LANES - 1, 1), pltpu.roll(u, LANES - 1, 1)
                 k_down, u_down = pltpu.roll(k, 1, 1), pltpu.roll(u, 1, 1)
-                ahead = [pltpu.roll(v, LANES - 1, 1) for v in edge[0]]
-                behind = [pltpu.roll(v, 1, 1) for v in edge[1]]
-                y_up = k + jnp.where(at_end, ahead[0], k_up)
-                y_down = k + jnp.where(at_start, behind[0], k_down)
+                k_own, u_own = beyond[0, l, rows], beyond[1, l, rows]
+                y_up = k + jnp.where(at_end, k_own, k_up)
+                y_down = k + jnp.where(at_start, k_own, k_down)
                 x_up, x_down = k + load(ext_k, i + 1, 1), k + load(ext_k, i + 1, -1)
                 above = k + k_next
                 total = ((y_up + y_down) + (x_up + x_down)) + (above + below)
-                flow = y_up * jnp.where(at_end, ahead[1], u_up) + y_down * jnp.where(at_start, behind[1], u_down)
+                flow = y_up * jnp.where(at_end, u_own, u_up) + y_down * jnp.where(at_start, u_own, u_down)
                 flow = flow + (x_up * load(ext_u, i + 1, 1) + x_down * load(ext_u, i + 1, -1))
                 flow = flow + (above * u_next + below * u_last)
                 cy[l, tiles, rows] = y_up
                 cy_low[l, tiles, rows] = y_down
-                cx[l, tiles, rows] = x_up
+                store(cx, l, tiles, c, chunks, x_up)
                 cz[l, tiles, rows] = below
                 diag[l, tiles, rows] = total + shift
-                r[l + 1, tiles, rows] = masked(flow - total * u, tiles, at, c)
+                store(r, l + 1, tiles, c, chunks, masked(flow - total * u, tiles, c))
                 for t, (ko, uo), here, kn, un, face in (
                     (0, edge[0], at_start, k_down, u_down, cy_low),
                     (tiles - 1, edge[1], at_end, k_up, u_up, cy),
                 ):
                     kn, un = jnp.where(here, kn, 0.0), jnp.where(here, un, 0.0)
                     face[l, t, rows] = face[l, t, rows] + kn
-                    diag[l, t, rows] = diag[l, t, rows] + kn
-                    r[l + 1, t, rows] = r[l + 1, t, rows] + ((ko + kn) * un - kn * uo)
+                    diag[l, t, rows] = diag[l, t, rows] + (kn + shift)
+                    store(r, l + 1, t, c, chunks, r[l + 1, t, rows] + ((ko + kn) * un - kn * uo))
                 k_last, u_last, k, u, below = k, u, k_next, u_next, above
         return 0
 
     lax.fori_loop(0, levels // few, prepare, 0)
     for c in range(chunks):
-        at = base + SUB * c
         for t in every:
-            cz[levels, t, pl.ds(at, SUB)] = zero_tile
+            cz[levels, t, SUB + SUB * c : 2 * SUB + SUB * c] = zero_tile
+    packed = halves(2)
     for l in range(NS):
-        for t in range(tiles):
-            rows = pl.ds(base, window)
-            r[l + 1, t, rows] = r[l + 1, t, rows] + ext_s[l, t, rows]
-        rows = pl.ds(base, window)
-        r[l + 1, tiles, rows] = r[l + 1, tiles, rows] + third(2, l)
+        columns = third(packed, l)
+        for c in range(chunks):
+            rows = slice(SUB * c, SUB * c + SUB)
+            for t in every:
+                extra = columns[rows] if t == tiles else ext_s[l, t, rows]
+                store(r, l + 1, t, c, chunks, r[l + 1, t, SUB + SUB * c : 2 * SUB + SUB * c] + extra)
 
     def operator(src, l, at, outs, unroll):
         rows = pl.ds(at, SUB)
@@ -467,10 +480,9 @@
         def step(j, _):
             l = j * many
             for c in range(chunks):
-                at = base + SUB * c
-                for i, _, ws in operator(src, l, at, every, many):
+                for i, _, ws in operator(src, l, SUB + SUB * c, every, many):
                     for t, w in enumerate(ws):
-                        dst[l + i + 1, t, pl.ds(at, SUB)] = masked(w, t, at, c)
+                        store(dst, l + i + 1, t, c, chunks, masked(w, t, c))
             return 0
 
         lax.fori_loop(0, levels // many, step, 0)
@@ -562,8 +574,7 @@
 ):
     levels, nx, ny = state.shape[1:]
     tiles = ny // LANES
-    window = nx + 2 * HALO
-    start = jnp.full((1,), SUB - HALO, jnp.int32)
+    window = nx + SUB
     edge = pltpu.VMEM((levels, SUB, ny), F32)
     (layers,) = call(layers_kernel, [(NS, nx, ny)], [state], scratch=[pltpu.SemaphoreType.DMA(())], hbm=(0,))
     partner = lax.ppermute(layers, "comp", [(i, i ^ 1) for i in range(lax.axis_size("comp"))])
@@ -596,33 +607,33 @@
         smem=(0,),
     )
     s0, s1 = swap(s0, "gx", 0), swap(s1, "gx", 1)
-    ext = (levels + 2, tiles + 1, nx + 2 * SUB, LANES)
-    ext_u, ext_k, y0, y1 = call(
-        fields_kernel, [ext, ext] + [(3, window, LANES)] * 2, [start, src, state, conduct, x0, x1], smem=(0,)
-    )
+    ext = (levels + 2, tiles + 1, nx + 3 * SUB, LANES)
+    ext_u, ext_k, y0, y1 = call(fields_kernel, [ext, ext] + [(3, window, LANES)] * 2, [src, state, conduct, x0, x1])
+    coef = (levels,) + ext[1:]
+    shapes = [ext, (levels + 1,) + ext[1:]] + [coef] * 4 + [(2, levels) + ext[2:]]
+    middle = levels * EARLY[0] // EARLY[1]
+    coefs = call(functools.partial(coefficients_kernel, 0, middle), shapes, [y0, ext_u, ext_k])
     ext_s, y0, y1 = call(
         columns_kernel,
-        [(NS, tiles, nx + 2 * SUB, LANES)] + [(3, window, LANES)] * 2,
-        [start, src, s0, s1, y0, y1],
-        smem=(0,),
-        alias={4: 1, 5: 2},
-    )
-    coef = (levels,) + ext[1:]
-    coefs = call(
-        coefficients_kernel,
-        [ext, (levels + 1,) + ext[1:]] + [coef] * 4,
-        [start, storage, ext_s, ext_u, ext_k],
-        smem=(0, 1),
+        [(NS, tiles, window, LANES)] + [(3, window, LANES)] * 2,
+        [src, s0, s1, y0, y1, coefs[0]],
+        alias={3: 1, 4: 2},
+    )
+    *coefs, beyond = call(
+        functools.partial(coefficients_kernel, middle, levels),
+        shapes,
+        [ext_s, ext_u, ext_k, *coefs],
+        alias={3 + i: i for i in range(len(shapes))},
     )
     y0, y1 = swap(y0, "gy", 0), swap(y1, "gy", 1)
     ext_u, p1, p2, moments, flux, r, *_ = call(
         chain_kernel,
         [ext] * 3 + [(SUB, LANES), (1, nx, ny)] + [c.shape for c in coefs],
-        [start, storage, ext_u, ext_k, ext_s, y0, y1, flux, *coefs],
-        scratch=[pltpu.VMEM((2, nx + 2 * SUB, LANES), F32), pltpu.SemaphoreType.DMA(())],
+        [storage, ext_u, ext_k, ext_s, y0, y1, flux, beyond, *coefs],
+        scratch=[pltpu.VMEM((3, SUB, LANES), F32), pltpu.SemaphoreType.DMA(())],
         hbm_outs=(4,),
-        smem=(0, 1),
-        alias={2: 0, **{8 + i: 5 + i for i in range(len(coefs))}},
+        smem=(0,),
+        alias={1: 0, **{8 + i: 5 + i for i in range(len(coefs))}},
     )
     (moments,) = call(add_kernel, [(SUB, LANES)], everyone(moments, "gx"))
     parts = everyone(moments, "gy")

time: 43.2 us -> 41.2 us (0.954)
  Pallas kernels: 16.8 us -> 14.4 us
    pallas_call x10 -> x11, Pallas kernels: 16.8 us -> 14.4 us  [call(): pl.pallas_call(kernel, out_shape=[jax.ShapeDtypeStruct(s, F32) if i in hb...]
    ppermute x6, waiting for transfers between devices: 2.58 us -> 3.32 us  [swap(): return lax.ppermute(value, ('gx', 'gy'), pairs)]
  transfers between devices with their start and end apart: 13 -> 13, of which waited for: 8 -> 7; matrix products, arithmetic and copies ran while one was open for 0% -> 0% of each run, Pallas kernels for 13% -> 12%
where the time goes in v4:
time: 41.2 us; the launch traced here: 41 us
  Pallas kernels  14.4 us (35%)
  starting transfers between devices  12.8 us (31%)
  waiting for transfers between devices  12.3 us (30%)
  between operations  1.44 us (3%)
    pallas_call x11, Pallas kernels, call(): pl.pallas_call(kernel, out_shape=[jax.ShapeDtypeStruct(s, F32) if i in hb...  14.4 us
    ppermute x6, starting transfers between devices, everyone(): lax.ppermute(value, axis, [(i, i ^ d) for i in range(n)])  6.37 us
    ppermute x6, waiting for transfers between devices, everyone(): lax.ppermute(value, axis, [(i, i ^ d) for i in range(n)])  5.21 us
    ppermute x6, starting transfers between devices, swap(): return lax.ppermute(value, ('gx', 'gy'), pairs)  4.93 us
    ppermute x1, waiting for transfers between devices, step(): lax.ppermute(layers, 'comp', [(i, i ^ 1) for i in range(lax.axis_size('co...  3.8 us
    ppermute x6, waiting for transfers between devices, swap(): return lax.ppermute(value, ('gx', 'gy'), pairs)  3.32 us
    ppermute x1, starting transfers between devices, step(): lax.ppermute(layers, 'comp', [(i, i ^ 1) for i in range(lax.axis_size('co...  1.52 us
  transfers between devices with their start and end apart: 13, of which 7 were waited for; matrix products, arithmetic and copies ran while one was open for 0% of the time, Pallas kernels for 12%

profile of v4, /device:TPU:0, one launch (start us, length us, event | category | flops | bytes accessed | tf_op | source)
XLA Modules:
  0.0 41.0 jit_solution(6867654497602874587)
XLA Ops:
  0.6 0.0 copy-start
  0.6 0.0 copy-start.1
  0.7 1.1 %shard_map.104.layers.after = f32[6,32,256]{2,1,0:T(8,128)S(1)} custom-call(f32[1,30,32,256]{3,2,1,0:T(8,128)} %u_ref.1), custom_call_target="tpu_custom_call" | custom-call | tf_op jit(solution)/shard_map/pallas_call | solution.py:80
  1.8 1.4 %shard_map.107 = (f32[30,8,256]{2,1,0:T(8,128)S(1)}, f32[30,8,256]{2,1,0:T(8,128)S(1)}) custom-call(f32[6,32,256]{2,1,0:T(8,128)S(1)} %shard_map.104.layers.after, f32[1,30,32,256]{3,2,1,0:T(8,128)} %u_ref.1, f32[1,30,32,256]{3,2,1,0:T(8,128)} %k_ref.1), custom_call_target="tpu_custom_call" | custom-call | tf_op jit(solution)/shard_map/pallas_call | solution.py:80
  3.2 0.6 %collective-permute-start.1 = (f32[30,8,256]{2,1,0:T(8,128)S(1)}, f32[30,8,256]{2,1,0:T(8,128)S(1)}, u32[]{:S(2)}, u32[]{:S(2)}) collective-permute-start(f32[30,8,256]{2,1,0:T(8,128)S(1)} %get-tuple-element.36), channel_id=1, source_target_pairs={{0,4},{1,5},{2,6},{3,7},{4,0},{5,1},{6,2},{7,3},{8,12},{9,13},{10,... | collective-permute-start | bytes 737288 | tf_op jit(solution)/shard_map/ppermute | solution.py:50
  3.7 2.6 %collective-permute-start.2 = (f32[30,8,256]{2,1,0:T(8,128)S(1)}, f32[30,8,256]{2,1,0:T(8,128)S(1)}, u32[]{:S(2)}, u32[]{:S(2)}) collective-permute-start(f32[30,8,256]{2,1,0:T(8,128)S(1)} %get-tuple-element.37), channel_id=1, source_target_pairs={{0,1},{1,0},{2,3},{3,2},{4,8},{5,9},{6,10},{7,11},{8,4},{9,5},{10,... | collective-permute-start | bytes 737288 | tf_op jit(solution)/shard_map/ppermute | solution.py:50
  6.4 1.5 %collective-permute-start = (f32[6,32,256]{2,1,0:T(8,128)S(1)}, f32[6,32,256]{2,1,0:T(8,128)S(1)}, u32[]{:S(2)}, u32[]{:S(2)}) collective-permute-start(f32[6,32,256]{2,1,0:T(8,128)S(1)} %shard_map.104.layers.after), channel_id=1, source_target_pairs={{0,16},{16,0},{1,17},{17,1},{2,18},{18,2},{3,19},{19,3},{4,20},{20... | collective-permute-start | bytes 589832 | tf_op jit(solution)/shard_map/ppermute | solution.py:580
  7.9 1.5 %shard_map.105.prof = f32[15,32,256]{2,1,0:T(8,128)S(1)} custom-call(f32[2,16]{1,0:T(2,128)} %bitcast.3, f32[6,2,16]{2,1,0:T(2,128)} %bitcast.2, s32[1,32,256]{2,1,0:T(8,128)} %kind_hbm.1, f32[6,32,256]{2,1,0:T(8,128)S(1)} %shard_map.104.layers.after), custom_call_target="tpu_custom_call" | custom-call | tf_op jit(solution)/shard_map/pallas_call | solution.py:80
  9.4 3.8 %collective-permute-done.part_ref = f32[6,32,256]{2,1,0:T(8,128)S(1)} collective-permute-done((f32[6,32,256]{2,1,0:T(8,128)S(1)}, f32[6,32,256]{2,1,0:T(8,128)S(1)}, u32[]{:S(2)}, u32[]{:S(2)}) %collective-permute-start) | collective-permute-done | bytes 196640 | tf_op jit(solution)/shard_map/ppermute | solution.py:580
  13.2 0.9 %shard_map.106 = (f32[1,32,256]{2,1,0:T(8,128)S(1)}, f32[6,32,256]{2,1,0:T(8,128)S(1)}, f32[3,8,256]{2,1,0:T(8,128)S(1)}, f32[3,8,256]{2,1,0:T(8,128)S(1)}) custom-call(s32[1,32]{1,0:T(1,128)S(1)} %copy-done.4, f32[6,32,256]{2,1,0:T(8,128)S(1)} %collective-permute-done.part_ref, f32[1,256,128]{2,1,0:T(8,128)S(1)} %copy-done.2, ...), custom_call_target="tpu_custom_call" | custom-call | tf_op jit(solution)/shard_map/pallas_call | solution.py:80
  14.2 0.1 collective-permute-start.3
  14.2 0.8 %collective-permute-start.4 = (f32[3,8,256]{2,1,0:T(8,128)S(1)}, f32[3,8,256]{2,1,0:T(8,128)S(1)}, u32[]{:S(2)}, u32[]{:S(2)}) collective-permute-start(f32[3,8,256]{2,1,0:T(8,128)S(1)} %get-tuple-element.41), channel_id=1, source_target_pairs={{0,1},{1,0},{2,3},{3,2},{4,8},{5,9},{6,10},{7,11},{8,4},{9,5},{10,... | collective-permute-start | bytes 73736 | tf_op jit(solution)/shard_map/ppermute | solution.py:50
  15.1 0.0 collective-permute-done.1.x0
  15.1 0.8 %shard_map.108 = (f32[32,3,56,128]{3,2,1,0:T(8,128)S(1)}, f32[32,3,56,128]{3,2,1,0:T(8,128)S(1)}, f32[3,40,128]{2,1,0:T(8,128)S(1)}, f32[3,40,128]{2,1,0:T(8,128)S(1)}) custom-call(f32[6,32,256]{2,1,0:T(8,128)S(1)} %get-tuple-element.35.after.s_ref, f32[1,30,32,256]{3,2,1,0:T(8,128)S(1)} %copy-done, f32[1,30,32,256]{3,2,1,0:T(8,128)S(1)} %copy-done.1, ...), custom_call_target="tpu_custom_call" | custom-call | tf_op jit(solution)/shard_map/pallas_call | solution.py:80
  15.9 0.7 %shard_map.109 = (f32[32,3,56,128]{3,2,1,0:T(8,128)S(1)}, f32[31,3,56,128]{3,2,1,0:T(8,128)S(1)}, f32[30,3,56,128]{3,2,1,0:T(8,128)S(1)}, f32[30,3,56,128]{3,2,1...) custom-call(f32[3,40,128]{2,1,0:T(8,128)S(1)} %get-tuple-element.42., ...), custom_call_target="tpu_custom_call" | custom-call | tf_op jit(solution)/shard_map/pallas_call | solution.py:80
  16.6 1.5 %collective-permute-done.4.s1 = f32[3,8,256]{2,1,0:T(8,128)S(1)} collective-permute-done((f32[3,8,256]{2,1,0:T(8,128)S(1)}, f32[3,8,256]{2,1,0:T(8,128)S(1)}, u32[]{:S(2)}, u32[]{:S(2)}) %collective-permute-start.4) | collective-permute-done | bytes 24608 | tf_op jit(solution)/shard_map/ppermute | solution.py:50
  18.1 0.1 shard_map.110
  18.2 0.8 %collective-permute-start.5 = (f32[3,40,128]{2,1,0:T(8,128)S(1)}, f32[3,40,128]{2,1,0:T(8,128)S(1)}, u32[]{:S(2)}, u32[]{:S(2)}) collective-permute-start(f32[3,40,128]{2,1,0:T(8,128)S(1)} %get-tuple-element.46), channel_id=1, source_target_pairs={{0,1},{1,0},{2,3},{3,2},{4,5},{5,4},{6,7},{7,6},{8,9},{9,8},{10,11... | collective-permute-start | bytes 184328 | tf_op jit(solution)/shard_map/ppermute | solution.py:50
  19.7 1.0 %shard_map.111 = (f32[32,3,56,128]{3,2,1,0:T(8,128)S(1)}, f32[31,3,56,128]{3,2,1,0:T(8,128)S(1)}, f32[30,3,56,128]{3,2,1,0:T(8,128)S(1)}, f32[30,3,56,128]{3,2,1...) custom-call(f32[6,2,40,128]{3,2,1,0:T(8,128)S(1)} %get-tuple-element, ...), custom_call_target="tpu_custom_call", output_to_operand_aliasing={{0}: (3, {}), {1}: (4, {}), {2}: (5, {}), {3}: (6, {}), {4}... | custom-call | tf_op jit(solution)/shard_map/pallas_call | solution.py:80
  20.7 1.8 %collective-permute-done.5.y0 = f32[3,40,128]{2,1,0:T(8,128)S(1)} collective-permute-done((f32[3,40,128]{2,1,0:T(8,128)S(1)}, f32[3,40,128]{2,1,0:T(8,128)S(1)}, u32[]{:S(2)}, u32[]{:S(2)}) %collective-permute-start.5) | collective-permute-done | bytes 61472 | tf_op jit(solution)/shard_map/ppermute | solution.py:50
  22.5 5.7 %shard_map.112 = (f32[32,3,56,128]{3,2,1,0:T(8,128)S(1)}, f32[32,3,56,128]{3,2,1,0:T(8,128)S(1)}, f32[32,3,56,128]{3,2,1,0:T(8,128)S(1)}, f32[8,128]{1,0:T(8,128...) custom-call(f32[1]{0:T(128)S(6)} %copy.43.storage_ref, ...), custom_call_target="tpu_custom_call", output_to_operand_aliasing={{0}: (1, {}), {5}: (8, {}), {6}: (9, {}), {7}: (10, {}), {8... | custom-call | tf_op jit(solution)/shard_map/pallas_call | solution.py:80
  28.2 0.1 collective-permute-start.9
  28.3 0.6 %collective-permute-start.8 = (f32[8,128]{1,0:T(8,128)S(1)}, f32[8,128]{1,0:T(8,128)S(1)}, u32[]{:S(2)}, u32[]{:S(2)}) collective-permute-start(f32[8,128]{1,0:T(8,128)S(1)} %get-tuple-element.62.refs_0_), channel_id=1, source_target_pairs={{0,8},{4,12},{8,0},{12,4},{1,9},{5,13},{9,1},{13,5},{2,10},{6,14},... | collective-permute-start | bytes 12296 | tf_op jit(solution)/shard_map/ppermute | solution.py:55
  28.9 1.3 %collective-permute-start.7 = (f32[8,128]{1,0:T(8,128)S(1)}, f32[8,128]{1,0:T(8,128)S(1)}, u32[]{:S(2)}, u32[]{:S(2)}) collective-permute-start(f32[8,128]{1,0:T(8,128)S(1)} %get-tuple-element.62.refs_0_), channel_id=1, source_target_pairs={{0,4},{4,0},{8,12},{12,8},{1,5},{5,1},{9,13},{13,9},{2,6},{6,2},{1... | collective-permute-start | bytes 12296 | tf_op jit(solution)/shard_map/ppermute | solution.py:55
  30.2 1.2 %collective-permute-done.9.refs_3_ = f32[8,128]{1,0:T(8,128)S(1)} collective-permute-done((f32[8,128]{1,0:T(8,128)S(1)}, f32[8,128]{1,0:T(8,128)S(1)}, u32[]{:S(2)}, u32[]{:S(2)}) %collective-permute-start.9) | collective-permute-done | bytes 4128 | tf_op jit(solution)/shard_map/ppermute | solution.py:55
  31.3 0.7 %collective-permute-done.8.refs_2_ = f32[8,128]{1,0:T(8,128)S(1)} collective-permute-done((f32[8,128]{1,0:T(8,128)S(1)}, f32[8,128]{1,0:T(8,128)S(1)}, u32[]{:S(2)}, u32[]{:S(2)}) %collective-permute-start.8) | collective-permute-done | bytes 4128 | tf_op jit(solution)/shard_map/ppermute | solution.py:55
  32.0 3.3 %collective-permute-start.12 = (f32[8,128]{1,0:T(8,128)S(1)}, f32[8,128]{1,0:T(8,128)S(1)}, u32[]{:S(2)}, u32[]{:S(2)}) collective-permute-start(f32[8,128]{1,0:T(8,128)S(1)} %shard_map.113.refs_0_), channel_id=1, source_target_pairs={{0,3},{1,2},{2,1},{3,0},{4,7},{5,6},{6,5},{7,4},{8,11},{9,10},{10,... | collective-permute-start | bytes 12296 | tf_op jit(solution)/shard_map/ppermute | solution.py:55
  35.3 0.6 %collective-permute-start.11 = (f32[8,128]{1,0:T(8,128)S(1)}, f32[8,128]{1,0:T(8,128)S(1)}, u32[]{:S(2)}, u32[]{:S(2)}) collective-permute-start(f32[8,128]{1,0:T(8,128)S(1)} %shard_map.113.refs_0_), channel_id=1, source_target_pairs={{0,2},{1,3},{2,0},{3,1},{4,6},{5,7},{6,4},{7,5},{8,10},{9,11},{10,... | collective-permute-start | bytes 12296 | tf_op jit(solution)/shard_map/ppermute | solution.py:55
  36.0 0.5 %collective-permute-start.10 = (f32[8,128]{1,0:T(8,128)S(1)}, f32[8,128]{1,0:T(8,128)S(1)}, u32[]{:S(2)}, u32[]{:S(2)}) collective-permute-start(f32[8,128]{1,0:T(8,128)S(1)} %shard_map.113.refs_0_), channel_id=1, source_target_pairs={{0,1},{1,0},{2,3},{3,2},{4,5},{5,4},{6,7},{7,6},{8,9},{9,8},{10,11... | collective-permute-start | bytes 12296 | tf_op jit(solution)/shard_map/ppermute | solution.py:55
  36.5 1.0 %collective-permute-done.12.refs_3_ = f32[8,128]{1,0:T(8,128)S(1)} collective-permute-done((f32[8,128]{1,0:T(8,128)S(1)}, f32[8,128]{1,0:T(8,128)S(1)}, u32[]{:S(2)}, u32[]{:S(2)}) %collective-permute-start.12) | collective-permute-done | bytes 4128 | tf_op jit(solution)/shard_map/ppermute | solution.py:55
  37.5 2.4 %collective-permute-done.11.refs_2_ = f32[8,128]{1,0:T(8,128)S(1)} collective-permute-done((f32[8,128]{1,0:T(8,128)S(1)}, f32[8,128]{1,0:T(8,128)S(1)}, u32[]{:S(2)}, u32[]{:S(2)}) %collective-permute-start.11) | collective-permute-done | bytes 4128 | tf_op jit(solution)/shard_map/ppermute | solution.py:55
  39.8 1.1 %shard_map.114 = f32[1,30,32,256]{3,2,1,0:T(8,128)} custom-call(f32[8,128]{1,0:T(8,128)S(1)} %shard_map.113.refs_0_, f32[8,128]{1,0:T(8,128)S(1)} %collective-permute-done.10.refs_1_, f32[8,128]{1,0:T(8,128)S(1)} %collective-permute-done.11.refs_2_, f32[8,128]{1,0:T(8,128)S(1)} %collective-permute-done.12.refs_3_, ...), custom_call_target="tpu_custom_call" | custom-call | tf_op jit(solution)/shard_map/pallas_call | solution.py:80
  (15 shorter events, 0.0 us)
Async XLA Ops:
  0.6 14.4 %copy-start = (f32[1,30,32,256]{3,2,1,0:T(8,128)S(1)}, f32[1,30,32,256]{3,2,1,0:T(8,128)}, u32[]{:S(2)}) copy-start(f32[1,30,32,256]{3,2,1,0:T(8,128)} %u_ref.1) | copy-start | bytes 2949124
  0.6 14.4 %copy-start.1 = (f32[1,30,32,256]{3,2,1,0:T(8,128)S(1)}, f32[1,30,32,256]{3,2,1,0:T(8,128)}, u32[]{:S(2)}) copy-start(f32[1,30,32,256]{3,2,1,0:T(8,128)} %k_ref.1) | copy-start | bytes 2949124
  0.7 12.6 %copy-start.2 = (f32[1,256,128]{2,1,0:T(8,128)S(1)}, f32[1,256,128]{2,1,0:T(8,128)}, u32[]{:S(2)}) copy-start(f32[1,256,128]{2,1,0:T(8,128)} %w_ref.1) | copy-start | bytes 393220
  0.7 12.6 %copy-start.4 = (s32[1,32]{1,0:T(1,128)S(1)}, s32[1,32]{1,0:T(1,128)}, u32[]{:S(2)}) copy-start(s32[1,32]{1,0:T(1,128)} %rows_ref.1) | copy-start | bytes 388
  0.7 12.6 %copy-start.3 = (f32[1,32,256]{2,1,0:T(8,128)S(1)}, f32[1,32,256]{2,1,0:T(8,128)}, u32[]{:S(2)}) copy-start(f32[1,32,256]{2,1,0:T(8,128)} %surf_ref.1) | copy-start | bytes 98308
  3.2 11.9 %collective-permute-start.1 = (f32[30,8,256]{2,1,0:T(8,128)S(1)}, f32[30,8,256]{2,1,0:T(8,128)S(1)}, u32[]{:S(2)}, u32[]{:S(2)}) collective-permute-start(f32[30,8,256]{2,1,0:T(8,128)S(1)} %get-tuple-element.36), channel_id=1, source_target_pairs={{0,4},{1,5},{2,6},{3,7},{4,0},{5,1},{6,2},{7,3},{8,12},{9,13},{10,... | collective-permute-start | bytes 737288 | tf_op jit(solution)/shard_map/ppermute | solution.py:50
  3.7 11.3 %collective-permute-start.2 = (f32[30,8,256]{2,1,0:T(8,128)S(1)}, f32[30,8,256]{2,1,0:T(8,128)S(1)}, u32[]{:S(2)}, u32[]{:S(2)}) collective-permute-start(f32[30,8,256]{2,1,0:T(8,128)S(1)} %get-tuple-element.37), channel_id=1, source_target_pairs={{0,1},{1,0},{2,3},{3,2},{4,8},{5,9},{6,10},{7,11},{8,4},{9,5},{10,... | collective-permute-start | bytes 737288 | tf_op jit(solution)/shard_map/ppermute | solution.py:50
  6.4 6.8 %collective-permute-start = (f32[6,32,256]{2,1,0:T(8,128)S(1)}, f32[6,32,256]{2,1,0:T(8,128)S(1)}, u32[]{:S(2)}, u32[]{:S(2)}) collective-permute-start(f32[6,32,256]{2,1,0:T(8,128)S(1)} %shard_map.104.layers.after), channel_id=1, source_target_pairs={{0,16},{16,0},{1,17},{17,1},{2,18},{18,2},{3,19},{19,3},{4,20},{20... | collective-permute-start | bytes 589832 | tf_op jit(solution)/shard_map/ppermute | solution.py:580
  14.2 2.4 %collective-permute-start.3 = (f32[3,8,256]{2,1,0:T(8,128)S(1)}, f32[3,8,256]{2,1,0:T(8,128)S(1)}, u32[]{:S(2)}, u32[]{:S(2)}) collective-permute-start(f32[3,8,256]{2,1,0:T(8,128)S(1)} %get-tuple-element.40), channel_id=1, source_target_pairs={{0,4},{1,5},{2,6},{3,7},{4,0},{5,1},{6,2},{7,3},{8,12},{9,13},{10,... | collective-permute-start | bytes 73736 | tf_op jit(solution)/shard_map/ppermute | solution.py:50
  14.2 3.9 %collective-permute-start.4 = (f32[3,8,256]{2,1,0:T(8,128)S(1)}, f32[3,8,256]{2,1,0:T(8,128)S(1)}, u32[]{:S(2)}, u32[]{:S(2)}) collective-permute-start(f32[3,8,256]{2,1,0:T(8,128)S(1)} %get-tuple-element.41), channel_id=1, source_target_pairs={{0,1},{1,0},{2,3},{3,2},{4,8},{5,9},{6,10},{7,11},{8,4},{9,5},{10,... | collective-permute-start | bytes 73736 | tf_op jit(solution)/shard_map/ppermute | solution.py:50
  18.2 4.3 %collective-permute-start.5 = (f32[3,40,128]{2,1,0:T(8,128)S(1)}, f32[3,40,128]{2,1,0:T(8,128)S(1)}, u32[]{:S(2)}, u32[]{:S(2)}) collective-permute-start(f32[3,40,128]{2,1,0:T(8,128)S(1)} %get-tuple-element.46), channel_id=1, source_target_pairs={{0,1},{1,0},{2,3},{3,2},{4,5},{5,4},{6,7},{7,6},{8,9},{9,8},{10,11... | collective-permute-start | bytes 184328 | tf_op jit(solution)/shard_map/ppermute | solution.py:50
  19.1 3.5 %collective-permute-start.6 = (f32[3,40,128]{2,1,0:T(8,128)S(1)}, f32[3,40,128]{2,1,0:T(8,128)S(1)}, u32[]{:S(2)}, u32[]{:S(2)}) collective-permute-start(f32[3,40,128]{2,1,0:T(8,128)S(1)} %get-tuple-element.47), channel_id=1, source_target_pairs={{0,4},{1,2},{2,1},{3,7},{4,0},{5,6},{6,5},{7,3},{8,12},{9,10},{10,... | collective-permute-start | bytes 184328 | tf_op jit(solution)/shard_map/ppermute | solution.py:50
  28.2 3.1 %collective-permute-start.9 = (f32[8,128]{1,0:T(8,128)S(1)}, f32[8,128]{1,0:T(8,128)S(1)}, u32[]{:S(2)}, u32[]{:S(2)}) collective-permute-start(f32[8,128]{1,0:T(8,128)S(1)} %get-tuple-element.62.refs_0_), channel_id=1, source_target_pairs={{0,12},{4,8},{8,4},{12,0},{1,13},{5,9},{9,5},{13,1},{2,14},{6,10},... | collective-permute-start | bytes 12296 | tf_op jit(solution)/shard_map/ppermute | solution.py:55
  28.3 3.7 %collective-permute-start.8 = (f32[8,128]{1,0:T(8,128)S(1)}, f32[8,128]{1,0:T(8,128)S(1)}, u32[]{:S(2)}, u32[]{:S(2)}) collective-permute-start(f32[8,128]{1,0:T(8,128)S(1)} %get-tuple-element.62.refs_0_), channel_id=1, source_target_pairs={{0,8},{4,12},{8,0},{12,4},{1,9},{5,13},{9,1},{13,5},{2,10},{6,14},... | collective-permute-start | bytes 12296 | tf_op jit(solution)/shard_map/ppermute | solution.py:55
  28.9 3.1 %collective-permute-start.7 = (f32[8,128]{1,0:T(8,128)S(1)}, f32[8,128]{1,0:T(8,128)S(1)}, u32[]{:S(2)}, u32[]{:S(2)}) collective-permute-start(f32[8,128]{1,0:T(8,128)S(1)} %get-tuple-element.62.refs_0_), channel_id=1, source_target_pairs={{0,4},{4,0},{8,12},{12,8},{1,5},{5,1},{9,13},{13,9},{2,6},{6,2},{1... | collective-permute-start | bytes 12296 | tf_op jit(solution)/shard_map/ppermute | solution.py:55
  32.0 5.5 %collective-permute-start.12 = (f32[8,128]{1,0:T(8,128)S(1)}, f32[8,128]{1,0:T(8,128)S(1)}, u32[]{:S(2)}, u32[]{:S(2)}) collective-permute-start(f32[8,128]{1,0:T(8,128)S(1)} %shard_map.113.refs_0_), channel_id=1, source_target_pairs={{0,3},{1,2},{2,1},{3,0},{4,7},{5,6},{6,5},{7,4},{8,11},{9,10},{10,... | collective-permute-start | bytes 12296 | tf_op jit(solution)/shard_map/ppermute | solution.py:55
  35.3 4.5 %collective-permute-start.11 = (f32[8,128]{1,0:T(8,128)S(1)}, f32[8,128]{1,0:T(8,128)S(1)}, u32[]{:S(2)}, u32[]{:S(2)}) collective-permute-start(f32[8,128]{1,0:T(8,128)S(1)} %shard_map.113.refs_0_), channel_id=1, source_target_pairs={{0,2},{1,3},{2,0},{3,1},{4,6},{5,7},{6,4},{7,5},{8,10},{9,11},{10,... | collective-permute-start | bytes 12296 | tf_op jit(solution)/shard_map/ppermute | solution.py:55
  36.0 3.9 %collective-permute-start.10 = (f32[8,128]{1,0:T(8,128)S(1)}, f32[8,128]{1,0:T(8,128)S(1)}, u32[]{:S(2)}, u32[]{:S(2)}) collective-permute-start(f32[8,128]{1,0:T(8,128)S(1)} %shard_map.113.refs_0_), channel_id=1, source_target_pairs={{0,1},{1,0},{2,3},{3,2},{4,5},{5,4},{6,7},{7,6},{8,9},{9,8},{10,11... | collective-permute-start | bytes 12296 | tf_op jit(solution)/shard_map/ppermute | solution.py:55
